TPU v7x, 128 devices: a whole 4x4x4 slice. The times are simulated.
128 devices in a mesh: space: 8 (over y, x_lo), mode: 16 (over x_hi, z, core).
Axes of the slice: x: 4 (x_hi: 2, x_lo: 2; x = x_hi * 2 + x_lo), y: 4, z: 4, core: 2. Of those that a mesh axis runs over, the one named last changes fastest.
Arguments:
- source_field: float32 [16, 4, 128, 4096], P('space', None, None, 'mode'), may hold values from -6 to 6
- mean_operator: float32 [16, 4, 128, 896], P('space'), may hold values from -0.109375 to 0.109375
- field_operators: float32 [4, 16, 4, 128, 896], P(None, 'space'), may hold values from -0.078125 to 0.078125
- adjacency: int32 [16, 4, 4], P('space'), may hold values from 0 to 3
- mode_masks: int32 [4], replicated, may hold values from 256 to 2048, as said below
Outputs:
- solution_field: float32 [16, 4, 128, 4096], P('space', None, None, 'mode')
- residual: float32 [16, 4, 128, 4096], P('space', None, None, 'mode')
Inputs may be any that keep to these rules, and one draw needn't show every extreme that they name: `mode_masks`: each value is 256 times a power of two, at most 2048, and every such value belongs to at least one field.
All inputs are finite; a program needn't handle non-finite values.
Results may differ from a plain program's by a relative error of at most 0.0001.
Values sent between devices are 32-bit elements; how exact they have to be, the bound alone decides.
No kernel may reach another device: no remote copies, remote signals or barrier semaphores. Data moves between devices by JAX's collectives and lax.ppermute only.
A program may use at most 128 MiB of HBM per device.

v0:
```python
import jax
import jax.numpy as jnp
from jax import lax
from jax.sharding import PartitionSpec as P

DEGREE = 4


coupling_coef = 0.5773502691896258
theta_value = 1.0
delta_value = 0.7


def padded_2(cells, sides, width):
    for axis, dim in sides:
        count = lax.axis_size(axis)
        ends = count - 1
        head = lax.slice_in_dim(cells, 0, width, axis=dim)
        tail = lax.slice_in_dim(cells, cells.shape[dim] - width, cells.shape[dim], axis=dim)
        cells = jnp.concatenate(
            [
                lax.ppermute(tail, axis, [(i, (i + 1) % count) for i in range(ends)]),
                cells,
                lax.ppermute(head, axis, [((i + 1) % count, i) for i in range(ends)]),
            ],
            axis=dim,
        )
    return cells


def swapped(value, axis, distance):
    mask = 2**distance
    pairs = [(source, source ^ mask) for source in range(lax.axis_size(axis))]
    return lax.ppermute(value, axis, pairs)


def gather_columns(padded, adjacency):
    centre = padded[1:-1]
    lower_layer = padded[:-2]
    upper_layer = padded[2:]
    in_layer = jax.vmap(lambda slab_layer, neighbours: slab_layer[neighbours])(centre, adjacency)
    stacked = jnp.concatenate(
        [centre[:, :, None], lower_layer[:, :, None], upper_layer[:, :, None], in_layer], axis=2
    )
    shape_now = centre.shape
    return stacked.reshape(shape_now[0], shape_now[1], 7 * shape_now[2], shape_now[3])


def block_product(operator, columns):
    return jnp.einsum(
        "lfij,lfjm->lfim",
        operator,
        columns,
        precision=lax.Precision.HIGHEST,
        preferred_element_type=jnp.float32,
    )


def per_device(source_field, mean_operator, field_operators, adjacency, mode_masks):
    modes_dev = source_field.shape[3]
    bit_total = lax.axis_size("mode").bit_length() - 1
    selectors = [
        jnp.where(mode_masks == modes_dev * (1 << bit_number), coupling_coef, 0.0).astype(
            jnp.float32
        )
        for bit_number in range(bit_total)
    ]

    def operate_on(field):
        padded = padded_2(field, (("space", 0),), 1)
        columns = gather_columns(padded, adjacency)
        result = field + block_product(mean_operator, columns)
        field_terms = jnp.einsum(
            "jlfik,lfkm->jlfim",
            field_operators,
            columns,
            precision=lax.Precision.HIGHEST,
            preferred_element_type=jnp.float32,
        )
        bit_terms = [
            jnp.einsum("j,jlfim->lfim", selector, field_terms, precision=lax.Precision.HIGHEST)
            for selector in selectors
        ]
        for bit_number in range(bit_total):
            result = result + swapped(bit_terms[bit_number], "mode", bit_number)
        return result

    sigma_value = theta_value / delta_value
    solution_field = jnp.zeros_like(source_field)
    residual = source_field
    direction = source_field / theta_value
    ratio_now = jnp.asarray(1.0 / sigma_value, dtype=jnp.float32)

    def iterate_once(count, carry):
        solution_field, residual, direction, ratio_now = carry
        solution_field = solution_field + direction
        residual = residual - operate_on(direction)
        ratio_new = 1.0 / (2.0 * sigma_value - ratio_now)
        direction = ratio_new * ratio_now * direction + 2.0 * ratio_new / delta_value * residual
        return (solution_field, residual, direction, ratio_new)

    solution_field, residual, direction, ratio_now = lax.fori_loop(
        0, DEGREE, iterate_once, (solution_field, residual, direction, ratio_now)
    )
    return (solution_field, residual)


def solution(mesh):
    in_specs = (
        P("space", None, None, "mode"),
        P("space", None, None, None),
        P(None, "space", None, None, None),
        P("space", None, None),
        P(),
    )
    out_specs = (P("space", None, None, "mode"), P("space", None, None, "mode"))
    return jax.shard_map(
        per_device, mesh=mesh, in_specs=in_specs, out_specs=out_specs, check_vma=False
    )
```

profile of v0, /device:TPU:1, one launch (start us, length us, event | category | flops | bytes accessed | tf_op | source)
XLA Modules:
  0.0 516.9 jit_solution(9477462086264856543)
XLA Ops:
  1.3 1.5 copy.24
  2.9 12.0 %copy.26 = f32[4,2,4,128,896]{4,3,0,2,1:T(8,128)} copy(f32[4,2,4,128,896]{4,3,2,1,0:T(8,128)} %param.9) | data formatting | bytes 29360128
  15.0 498.1 %while.19 = (s32[]{:T(128)}, f32[2,4,128,256]{2,3,1,0:T(8,128)}, f32[2,4,128,256]{2,3,1,0:T(8,128)S(1)}, f32[2,4,128,256]{2,3,1,0:T(8,128)S(1)}, f32[]{:T(128)},...) while((s32[]{:T(128)}, f32[2,4,128,256]{2,3,1,0:T(8,128)}, ...), condition=%wide.region_1.2_spmd.clone, body=%wide.region_0.1_spmd.clone.sunk | while | flops 14109114368 | bytes 146277744 | solution.py:102
  15.3 1.1 fusion.33
  16.4 4.8 collective-permute-start
  21.1 1.3 collective-permute-start.1
  22.5 2.8 gather_fusion
  25.4 5.6 %copy.55 = f32[32,128,256]{2,1,0:T(8,128)} copy(f32[32,128,256]{1,2,0:T(8,128)} %gather_fusion) | data formatting | bytes 8388608 | tf_op jit(solution)/shard_map/while/body/eval_jaxpr/vmap()/gather | solution.py:41
  31.2 13.2 %collective-permute-done.1 = f32[1,4,128,256]{3,2,1,0:T(8,128)} collective-permute-done((f32[1,4,128,256]{3,2,1,0:T(8,128)}, f32[1,4,128,256]{3,2,1,0:T(8,128)}, u32[]{:S(2)}, u32[]{:S(2)}) %collective-permute-start.1) | collective-permute-done | bytes 524320 | tf_op jit(solution)/shard_map/while/body/eval_jaxpr/ppermute | solution.py:24
  44.4 1.4 fusion.34
  45.8 2.7 pad_maximum_fusion.4
  48.5 32.7 %fusion.35 = (f32[2,4,128,256]{2,3,1,0:T(8,128)}, f32[2,4,128,256]{2,3,1,0:T(8,128)}, f32[2,4,128,256]{2,3,1,0:T(8,128)}, f32[2,4,128,256]{2,3,1,0:T(8,128)}) fusion(f32[4]{0:T(128)S(1)} %get-tuple-element.395, f32[4]{0:T(128)S(1)} %get-tuple-element.396, f32[4]{0:T(128)S(1)} %get-tuple-element.397, f32[4]{0:T(128)S(1)} %get-tuple-element.398, ...), kind=kOutput, calls=%fused_computation.6.clone.1 | convolution fusion | flops 11281629184 | bytes 26214464 | tf_op jit(solution)/shard_map/while/body/eval_jaxpr/jlfik,lfkm->jlfim/dot_general | solution.py:73
  81.3 2.7 collective-permute-start.2
  84.0 3.6 collective-permute-start.3
  88.4 2.4 collective-permute-start.5
  90.8 15.4 %collective-permute-done.2 = f32[2,4,128,256]{2,3,1,0:T(8,128)} collective-permute-done((f32[2,4,128,256]{2,3,1,0:T(8,128)}, f32[2,4,128,256]{2,3,1,0:T(8,128)}, u32[]{:S(2)}, u32[]{:S(2)}) %collective-permute-start.2) | collective-permute-done | bytes 1048608 | tf_op jit(solution)/shard_map/while/body/eval_jaxpr/ppermute | solution.py:34
  106.2 3.4 collective-permute-done.3
  109.6 22.9 %collective-permute-done.4 = f32[2,4,128,256]{2,3,1,0:T(8,128)} collective-permute-done((f32[2,4,128,256]{2,3,1,0:T(8,128)}, f32[2,4,128,256]{2,3,1,0:T(8,128)}, u32[]{:S(2)}, u32[]{:S(2)}) %collective-permute-start.4) | collective-permute-done | bytes 1048608 | tf_op jit(solution)/shard_map/while/body/eval_jaxpr/ppermute | solution.py:34
  132.5 15.9 %multiply_add_fusion.2 = (f32[2,4,128,256]{2,3,1,0:T(8,128)S(1)}, f32[2,4,128,256]{2,3,1,0:T(8,128)S(1)}, f32[2,4,128,256]{2,3,1,0:T(8,128)S(1)}) fusion(f32[2,4,128,256]{2,3,1,0:T(8,128)S(1)} %get-tuple-element.374, f32[]{:T(128)S(6)} %div.16, f32[]{:T(128)S(6)} %mul.49, f32[2,4,128,256]{2,3,1,0:T(8,128)S(1)} %copy-done.1, pred[]{:T(512)S(6)} %compare.3, ...), kind=kOutput, calls=%fused_computation.22.clone.1 | convolution fusion | flops 2821455872 | bytes 21495816 | tf_op jit(solution)/shard_map/while/body/eval_jaxpr/lfij,lfjm->lfim/dot_general | solution.py:50
  149.8 1.1 fusion.33
  150.9 3.0 collective-permute-start
  153.9 1.3 collective-permute-start.1
  155.3 2.8 gather_fusion
  158.1 5.6 %copy.55 = f32[32,128,256]{2,1,0:T(8,128)} copy(f32[32,128,256]{1,2,0:T(8,128)} %gather_fusion) | data formatting | bytes 8388608 | tf_op jit(solution)/shard_map/while/body/eval_jaxpr/vmap()/gather | solution.py:41
  163.7 12.2 %collective-permute-done.1 = f32[1,4,128,256]{3,2,1,0:T(8,128)} collective-permute-done((f32[1,4,128,256]{3,2,1,0:T(8,128)}, f32[1,4,128,256]{3,2,1,0:T(8,128)}, u32[]{:S(2)}, u32[]{:S(2)}) %collective-permute-start.1) | collective-permute-done | bytes 524320 | tf_op jit(solution)/shard_map/while/body/eval_jaxpr/ppermute | solution.py:24
  176.0 1.4 fusion.34
  177.4 2.7 pad_maximum_fusion.4
  180.1 32.7 %fusion.35 = (f32[2,4,128,256]{2,3,1,0:T(8,128)}, f32[2,4,128,256]{2,3,1,0:T(8,128)}, f32[2,4,128,256]{2,3,1,0:T(8,128)}, f32[2,4,128,256]{2,3,1,0:T(8,128)}) fusion(f32[4]{0:T(128)S(1)} %get-tuple-element.395, f32[4]{0:T(128)S(1)} %get-tuple-element.396, f32[4]{0:T(128)S(1)} %get-tuple-element.397, f32[4]{0:T(128)S(1)} %get-tuple-element.398, ...), kind=kOutput, calls=%fused_computation.6.clone.1 | convolution fusion | flops 11281629184 | bytes 26214464 | tf_op jit(solution)/shard_map/while/body/eval_jaxpr/jlfik,lfkm->jlfim/dot_general | solution.py:73
  213.9 4.2 collective-permute-start.5
  218.2 17.4 %collective-permute-done.2 = f32[2,4,128,256]{2,3,1,0:T(8,128)} collective-permute-done((f32[2,4,128,256]{2,3,1,0:T(8,128)}, f32[2,4,128,256]{2,3,1,0:T(8,128)}, u32[]{:S(2)}, u32[]{:S(2)}) %collective-permute-start.2) | collective-permute-done | bytes 1048608 | tf_op jit(solution)/shard_map/while/body/eval_jaxpr/ppermute | solution.py:34
  235.6 20.5 %collective-permute-done.4 = f32[2,4,128,256]{2,3,1,0:T(8,128)} collective-permute-done((f32[2,4,128,256]{2,3,1,0:T(8,128)}, f32[2,4,128,256]{2,3,1,0:T(8,128)}, u32[]{:S(2)}, u32[]{:S(2)}) %collective-permute-start.4) | collective-permute-done | bytes 1048608 | tf_op jit(solution)/shard_map/while/body/eval_jaxpr/ppermute | solution.py:34
  256.1 15.9 %multiply_add_fusion.2 = (f32[2,4,128,256]{2,3,1,0:T(8,128)S(1)}, f32[2,4,128,256]{2,3,1,0:T(8,128)S(1)}, f32[2,4,128,256]{2,3,1,0:T(8,128)S(1)}) fusion(f32[2,4,128,256]{2,3,1,0:T(8,128)S(1)} %get-tuple-element.374, f32[]{:T(128)S(6)} %div.16, f32[]{:T(128)S(6)} %mul.49, f32[2,4,128,256]{2,3,1,0:T(8,128)S(1)} %copy-done.1, pred[]{:T(512)S(6)} %compare.3, ...), kind=kOutput, calls=%fused_computation.22.clone.1 | convolution fusion | flops 2821455872 | bytes 21495816 | tf_op jit(solution)/shard_map/while/body/eval_jaxpr/lfij,lfjm->lfim/dot_general | solution.py:50
  274.4 3.9 collective-permute-start
  278.4 1.3 collective-permute-start.1
  279.7 2.8 gather_fusion
  282.6 5.6 %copy.55 = f32[32,128,256]{2,1,0:T(8,128)} copy(f32[32,128,256]{1,2,0:T(8,128)} %gather_fusion) | data formatting | bytes 8388608 | tf_op jit(solution)/shard_map/while/body/eval_jaxpr/vmap()/gather | solution.py:41
  288.2 9.2 %collective-permute-done.1 = f32[1,4,128,256]{3,2,1,0:T(8,128)} collective-permute-done((f32[1,4,128,256]{3,2,1,0:T(8,128)}, f32[1,4,128,256]{3,2,1,0:T(8,128)}, u32[]{:S(2)}, u32[]{:S(2)}) %collective-permute-start.1) | collective-permute-done | bytes 524320 | tf_op jit(solution)/shard_map/while/body/eval_jaxpr/ppermute | solution.py:24
  297.4 1.4 fusion.34
  298.8 2.7 pad_maximum_fusion.4
  301.5 32.7 %fusion.35 = (f32[2,4,128,256]{2,3,1,0:T(8,128)}, f32[2,4,128,256]{2,3,1,0:T(8,128)}, f32[2,4,128,256]{2,3,1,0:T(8,128)}, f32[2,4,128,256]{2,3,1,0:T(8,128)}) fusion(f32[4]{0:T(128)S(1)} %get-tuple-element.395, f32[4]{0:T(128)S(1)} %get-tuple-element.396, f32[4]{0:T(128)S(1)} %get-tuple-element.397, f32[4]{0:T(128)S(1)} %get-tuple-element.398, ...), kind=kOutput, calls=%fused_computation.6.clone.1 | convolution fusion | flops 11281629184 | bytes 26214464 | tf_op jit(solution)/shard_map/while/body/eval_jaxpr/jlfik,lfkm->jlfim/dot_general | solution.py:73
  334.3 2.7 collective-permute-start.2
  337.0 3.0 collective-permute-start.3
  340.0 6.4 %collective-permute-start.5 = (f32[2,4,128,256]{2,3,1,0:T(8,128)}, f32[2,4,128,256]{2,3,1,0:T(8,128)}, u32[]{:S(2)}, u32[]{:S(2)}) collective-permute-start(f32[2,4,128,256]{2,3,1,0:T(8,128)} %get-tuple-element.351), channel_id=1, source_target_pairs={{0,1},{1,0},{2,3},{3,2},{4,5},{5,4},{6,7},{7,6},{8,9},{9,8},{10,11... | collective-permute-start | bytes 3145736 | tf_op jit(solution)/shard_map/while/body/eval_jaxpr/ppermute | solution.py:34
  346.4 8.8 %collective-permute-done.2 = f32[2,4,128,256]{2,3,1,0:T(8,128)} collective-permute-done((f32[2,4,128,256]{2,3,1,0:T(8,128)}, f32[2,4,128,256]{2,3,1,0:T(8,128)}, u32[]{:S(2)}, u32[]{:S(2)}) %collective-permute-start.2) | collective-permute-done | bytes 1048608 | tf_op jit(solution)/shard_map/while/body/eval_jaxpr/ppermute | solution.py:34
  355.2 2.5 collective-permute-done.3
  357.7 21.7 %collective-permute-done.4 = f32[2,4,128,256]{2,3,1,0:T(8,128)} collective-permute-done((f32[2,4,128,256]{2,3,1,0:T(8,128)}, f32[2,4,128,256]{2,3,1,0:T(8,128)}, u32[]{:S(2)}, u32[]{:S(2)}) %collective-permute-start.4) | collective-permute-done | bytes 1048608 | tf_op jit(solution)/shard_map/while/body/eval_jaxpr/ppermute | solution.py:34
  379.4 15.9 %multiply_add_fusion.2 = (f32[2,4,128,256]{2,3,1,0:T(8,128)S(1)}, f32[2,4,128,256]{2,3,1,0:T(8,128)S(1)}, f32[2,4,128,256]{2,3,1,0:T(8,128)S(1)}) fusion(f32[2,4,128,256]{2,3,1,0:T(8,128)S(1)} %get-tuple-element.374, f32[]{:T(128)S(6)} %div.16, f32[]{:T(128)S(6)} %mul.49, f32[2,4,128,256]{2,3,1,0:T(8,128)S(1)} %copy-done.1, pred[]{:T(512)S(6)} %compare.3, ...), kind=kOutput, calls=%fused_computation.22.clone.1 | convolution fusion | flops 2821455872 | bytes 21495816 | tf_op jit(solution)/shard_map/while/body/eval_jaxpr/lfij,lfjm->lfim/dot_general | solution.py:50
  397.8 3.0 collective-permute-start
  400.8 1.3 collective-permute-start.1
  402.2 2.8 gather_fusion
  405.0 5.6 %copy.55 = f32[32,128,256]{2,1,0:T(8,128)} copy(f32[32,128,256]{1,2,0:T(8,128)} %gather_fusion) | data formatting | bytes 8388608 | tf_op jit(solution)/shard_map/while/body/eval_jaxpr/vmap()/gather | solution.py:41
  410.6 7.0 %collective-permute-done.1 = f32[1,4,128,256]{3,2,1,0:T(8,128)} collective-permute-done((f32[1,4,128,256]{3,2,1,0:T(8,128)}, f32[1,4,128,256]{3,2,1,0:T(8,128)}, u32[]{:S(2)}, u32[]{:S(2)}) %collective-permute-start.1) | collective-permute-done | bytes 524320 | tf_op jit(solution)/shard_map/while/body/eval_jaxpr/ppermute | solution.py:24
  417.6 1.4 fusion.34
  419.0 2.7 pad_maximum_fusion.4
  421.7 32.7 %fusion.35 = (f32[2,4,128,256]{2,3,1,0:T(8,128)}, f32[2,4,128,256]{2,3,1,0:T(8,128)}, f32[2,4,128,256]{2,3,1,0:T(8,128)}, f32[2,4,128,256]{2,3,1,0:T(8,128)}) fusion(f32[4]{0:T(128)S(1)} %get-tuple-element.395, f32[4]{0:T(128)S(1)} %get-tuple-element.396, f32[4]{0:T(128)S(1)} %get-tuple-element.397, f32[4]{0:T(128)S(1)} %get-tuple-element.398, ...), kind=kOutput, calls=%fused_computation.6.clone.1 | convolution fusion | flops 11281629184 | bytes 26214464 | tf_op jit(solution)/shard_map/while/body/eval_jaxpr/jlfik,lfkm->jlfim/dot_general | solution.py:73
  454.5 1.7 collective-permute-start.2
  456.2 2.0 collective-permute-start.3
  458.2 8.5 %collective-permute-start.5 = (f32[2,4,128,256]{2,3,1,0:T(8,128)}, f32[2,4,128,256]{2,3,1,0:T(8,128)}, u32[]{:S(2)}, u32[]{:S(2)}) collective-permute-start(f32[2,4,128,256]{2,3,1,0:T(8,128)} %get-tuple-element.351), channel_id=1, source_target_pairs={{0,1},{1,0},{2,3},{3,2},{4,5},{5,4},{6,7},{7,6},{8,9},{9,8},{10,11... | collective-permute-start | bytes 3145736 | tf_op jit(solution)/shard_map/while/body/eval_jaxpr/ppermute | solution.py:34
  466.8 6.2 %collective-permute-done.2 = f32[2,4,128,256]{2,3,1,0:T(8,128)} collective-permute-done((f32[2,4,128,256]{2,3,1,0:T(8,128)}, f32[2,4,128,256]{2,3,1,0:T(8,128)}, u32[]{:S(2)}, u32[]{:S(2)}) %collective-permute-start.2) | collective-permute-done | bytes 1048608 | tf_op jit(solution)/shard_map/while/body/eval_jaxpr/ppermute | solution.py:34
  473.0 1.4 collective-permute-done.3
  474.4 21.7 %collective-permute-done.4 = f32[2,4,128,256]{2,3,1,0:T(8,128)} collective-permute-done((f32[2,4,128,256]{2,3,1,0:T(8,128)}, f32[2,4,128,256]{2,3,1,0:T(8,128)}, u32[]{:S(2)}, u32[]{:S(2)}) %collective-permute-start.4) | collective-permute-done | bytes 1048608 | tf_op jit(solution)/shard_map/while/body/eval_jaxpr/ppermute | solution.py:34
  496.1 15.9 %multiply_add_fusion.2 = (f32[2,4,128,256]{2,3,1,0:T(8,128)S(1)}, f32[2,4,128,256]{2,3,1,0:T(8,128)S(1)}, f32[2,4,128,256]{2,3,1,0:T(8,128)S(1)}) fusion(f32[2,4,128,256]{2,3,1,0:T(8,128)S(1)} %get-tuple-element.374, f32[]{:T(128)S(6)} %div.16, f32[]{:T(128)S(6)} %mul.49, f32[2,4,128,256]{2,3,1,0:T(8,128)S(1)} %copy-done.1, pred[]{:T(512)S(6)} %compare.3, ...), kind=kOutput, calls=%fused_computation.22.clone.1 | convolution fusion | flops 2821455872 | bytes 21495816 | tf_op jit(solution)/shard_map/while/body/eval_jaxpr/lfij,lfjm->lfim/dot_general | solution.py:50
  513.1 1.3 copy.28
  514.4 2.5 copy.27
  (58 shorter events, 10.6 us)
Async XLA Ops:
  2.9 12.0 %copy-start.3 = (s32[2,4,4]{2,1,0:T(4,128)S(1)}, s32[2,4,4]{2,1,0:T(4,128)}, u32[]{:S(2)}) copy-start(s32[2,4,4]{2,1,0:T(4,128)} %param.10) | copy-start | bytes 388
  16.4 14.8 %collective-permute-start = (f32[1,4,128,256]{3,2,1,0:T(8,128)}, f32[1,4,128,256]{3,2,1,0:T(8,128)}, u32[]{:S(2)}, u32[]{:S(2)}) collective-permute-start(f32[1,4,128,256]{3,2,1,0:T(8,128)} %get-tuple-element.344), channel_id=1, source_target_pairs={{0,16},{16,32},{32,48},{48,64},{64,80},{80,96},{96,112},{1,17},{17... | collective-permute-start | bytes 1572872 | tf_op jit(solution)/shard_map/while/body/eval_jaxpr/ppermute | solution.py:22
  21.1 23.3 %collective-permute-start.1 = (f32[1,4,128,256]{3,2,1,0:T(8,128)}, f32[1,4,128,256]{3,2,1,0:T(8,128)}, u32[]{:S(2)}, u32[]{:S(2)}) collective-permute-start(f32[1,4,128,256]{3,2,1,0:T(8,128)} %get-tuple-element.345), channel_id=1, source_target_pairs={{16,0},{32,16},{48,32},{64,48},{80,64},{96,80},{112,96},{17,1},{33... | collective-permute-start | bytes 1572872 | tf_op jit(solution)/shard_map/while/body/eval_jaxpr/ppermute | solution.py:24
  48.5 32.8 %copy-start = (f32[2,4,7,128,256]{4,3,2,1,0:T(8,128)}, f32[2,4,7,128,256]{4,3,2,1,0:T(8,128)S(1)}, u32[]{:S(2)}) copy-start(f32[2,4,7,128,256]{4,3,2,1,0:T(8,128)S(1)} %pad_maximum_fusion.4) | copy-start | bytes 22020100 | tf_op jit(solution)/shard_map/while
  48.5 84.0 %copy-start.1 = (f32[2,4,128,256]{2,3,1,0:T(8,128)S(1)}, f32[2,4,128,256]{2,3,1,0:T(8,128)}, u32[]{:S(2)}) copy-start(f32[2,4,128,256]{2,3,1,0:T(8,128)} %get-tuple-element.372) | copy-start | bytes 3145732 | tf_op jit(solution)/shard_map/while
  81.3 24.9 %collective-permute-start.2 = (f32[2,4,128,256]{2,3,1,0:T(8,128)}, f32[2,4,128,256]{2,3,1,0:T(8,128)}, u32[]{:S(2)}, u32[]{:S(2)}) collective-permute-start(f32[2,4,128,256]{2,3,1,0:T(8,128)} %get-tuple-element.348), channel_id=1, source_target_pairs={{0,8},{1,9},{2,10},{3,11},{4,12},{5,13},{6,14},{7,15},{8,0},{9,1},... | collective-permute-start | bytes 3145736 | tf_op jit(solution)/shard_map/while/body/eval_jaxpr/ppermute | solution.py:34
  84.0 25.6 %collective-permute-start.3 = (f32[2,4,128,256]{2,3,1,0:T(8,128)}, f32[2,4,128,256]{2,3,1,0:T(8,128)}, u32[]{:S(2)}, u32[]{:S(2)}) collective-permute-start(f32[2,4,128,256]{2,3,1,0:T(8,128)} %get-tuple-element.349), channel_id=1, source_target_pairs={{0,4},{1,5},{2,6},{3,7},{4,0},{5,1},{6,2},{7,3},{8,12},{9,13},{10,... | collective-permute-start | bytes 3145736 | tf_op jit(solution)/shard_map/while/body/eval_jaxpr/ppermute | solution.py:34
  87.6 44.9 %collective-permute-start.4 = (f32[2,4,128,256]{2,3,1,0:T(8,128)}, f32[2,4,128,256]{2,3,1,0:T(8,128)}, u32[]{:S(2)}, u32[]{:S(2)}) collective-permute-start(f32[2,4,128,256]{2,3,1,0:T(8,128)} %get-tuple-element.350), channel_id=1, source_target_pairs={{0,2},{1,3},{2,0},{3,1},{4,6},{5,7},{6,4},{7,5},{8,10},{9,11},{10,... | collective-permute-start | bytes 3145736 | tf_op jit(solution)/shard_map/while/body/eval_jaxpr/ppermute | solution.py:34
  88.4 44.1 %collective-permute-start.5 = (f32[2,4,128,256]{2,3,1,0:T(8,128)}, f32[2,4,128,256]{2,3,1,0:T(8,128)}, u32[]{:S(2)}, u32[]{:S(2)}) collective-permute-start(f32[2,4,128,256]{2,3,1,0:T(8,128)} %get-tuple-element.351), channel_id=1, source_target_pairs={{0,1},{1,0},{2,3},{3,2},{4,5},{5,4},{6,7},{7,6},{8,9},{9,8},{10,11... | collective-permute-start | bytes 3145736 | tf_op jit(solution)/shard_map/while/body/eval_jaxpr/ppermute | solution.py:34
  148.5 1.0 copy-start.2
  150.9 12.9 %collective-permute-start = (f32[1,4,128,256]{3,2,1,0:T(8,128)}, f32[1,4,128,256]{3,2,1,0:T(8,128)}, u32[]{:S(2)}, u32[]{:S(2)}) collective-permute-start(f32[1,4,128,256]{3,2,1,0:T(8,128)} %get-tuple-element.344), channel_id=1, source_target_pairs={{0,16},{16,32},{32,48},{48,64},{64,80},{80,96},{96,112},{1,17},{17... | collective-permute-start | bytes 1572872 | tf_op jit(solution)/shard_map/while/body/eval_jaxpr/ppermute | solution.py:22
  153.9 22.1 %collective-permute-start.1 = (f32[1,4,128,256]{3,2,1,0:T(8,128)}, f32[1,4,128,256]{3,2,1,0:T(8,128)}, u32[]{:S(2)}, u32[]{:S(2)}) collective-permute-start(f32[1,4,128,256]{3,2,1,0:T(8,128)} %get-tuple-element.345), channel_id=1, source_target_pairs={{16,0},{32,16},{48,32},{64,48},{80,64},{96,80},{112,96},{17,1},{33... | collective-permute-start | bytes 1572872 | tf_op jit(solution)/shard_map/while/body/eval_jaxpr/ppermute | solution.py:24
  180.1 32.8 %copy-start = (f32[2,4,7,128,256]{4,3,2,1,0:T(8,128)}, f32[2,4,7,128,256]{4,3,2,1,0:T(8,128)S(1)}, u32[]{:S(2)}) copy-start(f32[2,4,7,128,256]{4,3,2,1,0:T(8,128)S(1)} %pad_maximum_fusion.4) | copy-start | bytes 22020100 | tf_op jit(solution)/shard_map/while
  180.1 76.0 %copy-start.1 = (f32[2,4,128,256]{2,3,1,0:T(8,128)S(1)}, f32[2,4,128,256]{2,3,1,0:T(8,128)}, u32[]{:S(2)}) copy-start(f32[2,4,128,256]{2,3,1,0:T(8,128)} %get-tuple-element.372) | copy-start | bytes 3145732 | tf_op jit(solution)/shard_map/while
  212.8 22.8 %collective-permute-start.2 = (f32[2,4,128,256]{2,3,1,0:T(8,128)}, f32[2,4,128,256]{2,3,1,0:T(8,128)}, u32[]{:S(2)}, u32[]{:S(2)}) collective-permute-start(f32[2,4,128,256]{2,3,1,0:T(8,128)} %get-tuple-element.348), channel_id=1, source_target_pairs={{0,8},{1,9},{2,10},{3,11},{4,12},{5,13},{6,14},{7,15},{8,0},{9,1},... | collective-permute-start | bytes 3145736 | tf_op jit(solution)/shard_map/while/body/eval_jaxpr/ppermute | solution.py:34
  213.0 22.6 %collective-permute-start.3 = (f32[2,4,128,256]{2,3,1,0:T(8,128)}, f32[2,4,128,256]{2,3,1,0:T(8,128)}, u32[]{:S(2)}, u32[]{:S(2)}) collective-permute-start(f32[2,4,128,256]{2,3,1,0:T(8,128)} %get-tuple-element.349), channel_id=1, source_target_pairs={{0,4},{1,5},{2,6},{3,7},{4,0},{5,1},{6,2},{7,3},{8,12},{9,13},{10,... | collective-permute-start | bytes 3145736 | tf_op jit(solution)/shard_map/while/body/eval_jaxpr/ppermute | solution.py:34
  213.9 42.2 %collective-permute-start.4 = (f32[2,4,128,256]{2,3,1,0:T(8,128)}, f32[2,4,128,256]{2,3,1,0:T(8,128)}, u32[]{:S(2)}, u32[]{:S(2)}) collective-permute-start(f32[2,4,128,256]{2,3,1,0:T(8,128)} %get-tuple-element.350), channel_id=1, source_target_pairs={{0,2},{1,3},{2,0},{3,1},{4,6},{5,7},{6,4},{7,5},{8,10},{9,11},{10,... | collective-permute-start | bytes 3145736 | tf_op jit(solution)/shard_map/while/body/eval_jaxpr/ppermute | solution.py:34
  213.9 42.2 %collective-permute-start.5 = (f32[2,4,128,256]{2,3,1,0:T(8,128)}, f32[2,4,128,256]{2,3,1,0:T(8,128)}, u32[]{:S(2)}, u32[]{:S(2)}) collective-permute-start(f32[2,4,128,256]{2,3,1,0:T(8,128)} %get-tuple-element.351), channel_id=1, source_target_pairs={{0,1},{1,0},{2,3},{3,2},{4,5},{5,4},{6,7},{7,6},{8,9},{9,8},{10,11... | collective-permute-start | bytes 3145736 | tf_op jit(solution)/shard_map/while/body/eval_jaxpr/ppermute | solution.py:34
  272.0 1.0 copy-start.2
  274.4 13.8 %collective-permute-start = (f32[1,4,128,256]{3,2,1,0:T(8,128)}, f32[1,4,128,256]{3,2,1,0:T(8,128)}, u32[]{:S(2)}, u32[]{:S(2)}) collective-permute-start(f32[1,4,128,256]{3,2,1,0:T(8,128)} %get-tuple-element.344), channel_id=1, source_target_pairs={{0,16},{16,32},{32,48},{48,64},{64,80},{80,96},{96,112},{1,17},{17... | collective-permute-start | bytes 1572872 | tf_op jit(solution)/shard_map/while/body/eval_jaxpr/ppermute | solution.py:22
  278.4 19.1 %collective-permute-start.1 = (f32[1,4,128,256]{3,2,1,0:T(8,128)}, f32[1,4,128,256]{3,2,1,0:T(8,128)}, u32[]{:S(2)}, u32[]{:S(2)}) collective-permute-start(f32[1,4,128,256]{3,2,1,0:T(8,128)} %get-tuple-element.345), channel_id=1, source_target_pairs={{16,0},{32,16},{48,32},{64,48},{80,64},{96,80},{112,96},{17,1},{33... | collective-permute-start | bytes 1572872 | tf_op jit(solution)/shard_map/while/body/eval_jaxpr/ppermute | solution.py:24
  301.5 32.8 %copy-start = (f32[2,4,7,128,256]{4,3,2,1,0:T(8,128)}, f32[2,4,7,128,256]{4,3,2,1,0:T(8,128)S(1)}, u32[]{:S(2)}) copy-start(f32[2,4,7,128,256]{4,3,2,1,0:T(8,128)S(1)} %pad_maximum_fusion.4) | copy-start | bytes 22020100 | tf_op jit(solution)/shard_map/while
  301.5 77.9 %copy-start.1 = (f32[2,4,128,256]{2,3,1,0:T(8,128)S(1)}, f32[2,4,128,256]{2,3,1,0:T(8,128)}, u32[]{:S(2)}) copy-start(f32[2,4,128,256]{2,3,1,0:T(8,128)} %get-tuple-element.372) | copy-start | bytes 3145732 | tf_op jit(solution)/shard_map/while
  334.3 21.0 %collective-permute-start.2 = (f32[2,4,128,256]{2,3,1,0:T(8,128)}, f32[2,4,128,256]{2,3,1,0:T(8,128)}, u32[]{:S(2)}, u32[]{:S(2)}) collective-permute-start(f32[2,4,128,256]{2,3,1,0:T(8,128)} %get-tuple-element.348), channel_id=1, source_target_pairs={{0,8},{1,9},{2,10},{3,11},{4,12},{5,13},{6,14},{7,15},{8,0},{9,1},... | collective-permute-start | bytes 3145736 | tf_op jit(solution)/shard_map/while/body/eval_jaxpr/ppermute | solution.py:34
  337.0 20.7 %collective-permute-start.3 = (f32[2,4,128,256]{2,3,1,0:T(8,128)}, f32[2,4,128,256]{2,3,1,0:T(8,128)}, u32[]{:S(2)}, u32[]{:S(2)}) collective-permute-start(f32[2,4,128,256]{2,3,1,0:T(8,128)} %get-tuple-element.349), channel_id=1, source_target_pairs={{0,4},{1,5},{2,6},{3,7},{4,0},{5,1},{6,2},{7,3},{8,12},{9,13},{10,... | collective-permute-start | bytes 3145736 | tf_op jit(solution)/shard_map/while/body/eval_jaxpr/ppermute | solution.py:34
  340.0 39.4 %collective-permute-start.4 = (f32[2,4,128,256]{2,3,1,0:T(8,128)}, f32[2,4,128,256]{2,3,1,0:T(8,128)}, u32[]{:S(2)}, u32[]{:S(2)}) collective-permute-start(f32[2,4,128,256]{2,3,1,0:T(8,128)} %get-tuple-element.350), channel_id=1, source_target_pairs={{0,2},{1,3},{2,0},{3,1},{4,6},{5,7},{6,4},{7,5},{8,10},{9,11},{10,... | collective-permute-start | bytes 3145736 | tf_op jit(solution)/shard_map/while/body/eval_jaxpr/ppermute | solution.py:34
  340.0 39.4 %collective-permute-start.5 = (f32[2,4,128,256]{2,3,1,0:T(8,128)}, f32[2,4,128,256]{2,3,1,0:T(8,128)}, u32[]{:S(2)}, u32[]{:S(2)}) collective-permute-start(f32[2,4,128,256]{2,3,1,0:T(8,128)} %get-tuple-element.351), channel_id=1, source_target_pairs={{0,1},{1,0},{2,3},{3,2},{4,5},{5,4},{6,7},{7,6},{8,9},{9,8},{10,11... | collective-permute-start | bytes 3145736 | tf_op jit(solution)/shard_map/while/body/eval_jaxpr/ppermute | solution.py:34
  395.4 1.0 copy-start.2
  397.8 12.9 %collective-permute-start = (f32[1,4,128,256]{3,2,1,0:T(8,128)}, f32[1,4,128,256]{3,2,1,0:T(8,128)}, u32[]{:S(2)}, u32[]{:S(2)}) collective-permute-start(f32[1,4,128,256]{3,2,1,0:T(8,128)} %get-tuple-element.344), channel_id=1, source_target_pairs={{0,16},{16,32},{32,48},{48,64},{64,80},{80,96},{96,112},{1,17},{17... | collective-permute-start | bytes 1572872 | tf_op jit(solution)/shard_map/while/body/eval_jaxpr/ppermute | solution.py:22
  400.8 16.8 %collective-permute-start.1 = (f32[1,4,128,256]{3,2,1,0:T(8,128)}, f32[1,4,128,256]{3,2,1,0:T(8,128)}, u32[]{:S(2)}, u32[]{:S(2)}) collective-permute-start(f32[1,4,128,256]{3,2,1,0:T(8,128)} %get-tuple-element.345), channel_id=1, source_target_pairs={{16,0},{32,16},{48,32},{64,48},{80,64},{96,80},{112,96},{17,1},{33... | collective-permute-start | bytes 1572872 | tf_op jit(solution)/shard_map/while/body/eval_jaxpr/ppermute | solution.py:24
  421.7 32.8 %copy-start = (f32[2,4,7,128,256]{4,3,2,1,0:T(8,128)}, f32[2,4,7,128,256]{4,3,2,1,0:T(8,128)S(1)}, u32[]{:S(2)}) copy-start(f32[2,4,7,128,256]{4,3,2,1,0:T(8,128)S(1)} %pad_maximum_fusion.4) | copy-start | bytes 22020100 | tf_op jit(solution)/shard_map/while
  421.7 74.4 %copy-start.1 = (f32[2,4,128,256]{2,3,1,0:T(8,128)S(1)}, f32[2,4,128,256]{2,3,1,0:T(8,128)}, u32[]{:S(2)}) copy-start(f32[2,4,128,256]{2,3,1,0:T(8,128)} %get-tuple-element.372) | copy-start | bytes 3145732 | tf_op jit(solution)/shard_map/while
  454.5 18.5 %collective-permute-start.2 = (f32[2,4,128,256]{2,3,1,0:T(8,128)}, f32[2,4,128,256]{2,3,1,0:T(8,128)}, u32[]{:S(2)}, u32[]{:S(2)}) collective-permute-start(f32[2,4,128,256]{2,3,1,0:T(8,128)} %get-tuple-element.348), channel_id=1, source_target_pairs={{0,8},{1,9},{2,10},{3,11},{4,12},{5,13},{6,14},{7,15},{8,0},{9,1},... | collective-permute-start | bytes 3145736 | tf_op jit(solution)/shard_map/while/body/eval_jaxpr/ppermute | solution.py:34
  456.2 18.3 %collective-permute-start.3 = (f32[2,4,128,256]{2,3,1,0:T(8,128)}, f32[2,4,128,256]{2,3,1,0:T(8,128)}, u32[]{:S(2)}, u32[]{:S(2)}) collective-permute-start(f32[2,4,128,256]{2,3,1,0:T(8,128)} %get-tuple-element.349), channel_id=1, source_target_pairs={{0,4},{1,5},{2,6},{3,7},{4,0},{5,1},{6,2},{7,3},{8,12},{9,13},{10,... | collective-permute-start | bytes 3145736 | tf_op jit(solution)/shard_map/while/body/eval_jaxpr/ppermute | solution.py:34
  458.2 37.9 %collective-permute-start.4 = (f32[2,4,128,256]{2,3,1,0:T(8,128)}, f32[2,4,128,256]{2,3,1,0:T(8,128)}, u32[]{:S(2)}, u32[]{:S(2)}) collective-permute-start(f32[2,4,128,256]{2,3,1,0:T(8,128)} %get-tuple-element.350), channel_id=1, source_target_pairs={{0,2},{1,3},{2,0},{3,1},{4,6},{5,7},{6,4},{7,5},{8,10},{9,11},{10,... | collective-permute-start | bytes 3145736 | tf_op jit(solution)/shard_map/while/body/eval_jaxpr/ppermute | solution.py:34
  458.2 37.9 %collective-permute-start.5 = (f32[2,4,128,256]{2,3,1,0:T(8,128)}, f32[2,4,128,256]{2,3,1,0:T(8,128)}, u32[]{:S(2)}, u32[]{:S(2)}) collective-permute-start(f32[2,4,128,256]{2,3,1,0:T(8,128)} %get-tuple-element.351), channel_id=1, source_target_pairs={{0,1},{1,0},{2,3},{3,2},{4,5},{5,4},{6,7},{7,6},{8,9},{9,8},{10,11... | collective-permute-start | bytes 3145736 | tf_op jit(solution)/shard_map/while/body/eval_jaxpr/ppermute | solution.py:34
  512.1 1.0 copy-start.2
where the time goes:
time: 525 us; the launch traced here: 517 us
  matrix products  195 us (37%)
  waiting for transfers between devices  184 us (35%)
  local copies, waits for them, and re-layouts  61.2 us (12%)
  starting transfers between devices  59 us (11%)
  other arithmetic  16.9 us (3%)
    ppermute x16, waiting for transfers between devices, swapped(): return lax.ppermute(value, axis, pairs)  142 us
    dot_general x4, matrix products, operate_on(): jnp.einsum('jlfik,lfkm->jlfim', field_operators, columns, precision=lax.P...  131 us
    dot_general x4, matrix products, block_product(): jnp.einsum('lfij,lfjm->lfim', operator, columns, precision=lax.Precision....  63.8 us
    ppermute x4, waiting for transfers between devices, padded_2(): lax.ppermute(head, axis, [((i + 1) % count, i) for i in range(ends)])  41.6 us
    ppermute x16, starting transfers between devices, swapped(): return lax.ppermute(value, axis, pairs)  39.2 us
    gather x12, local copies, waits for them, and re-layouts, gather_columns(): slab_layer[neighbours]  34.2 us
    unnamed x7, local copies, waits for them, and re-layouts  17.5 us
    ppermute x4, starting transfers between devices, padded_2(): lax.ppermute(tail, axis, [(i, (i + 1) % count) for i in range(ends)])  14.7 us
  transfers between devices with their start and end apart: 24, of which 16 were waited for; matrix products, arithmetic and copies ran while one was open for 7% of the time, Pallas kernels for 0%

commit v1 on v0

v1 whole, which is shorter than its diff:
```python
import functools

import jax
import jax.numpy as jnp
from jax import lax
from jax.experimental import pallas as pl
from jax.experimental.pallas import tpu as pltpu
from jax.sharding import PartitionSpec as P

DEGREE = 4
COUPLING = 0.5773502691896258
THETA = 1.0
DELTA = 0.7
AXES = ("space", "mode")
F32 = jnp.float32
BF16 = jnp.bfloat16
NT = (((1,), (1,)), ((), ()))


def split2(value):
    high = value.astype(BF16)
    return high, (value - high.astype(F32)).astype(BF16)


def dot_nt(left, right):
    return lax.dot_general(left, right, NT, preferred_element_type=F32)


def swap_rows(value, bit, group):
    step = group << bit
    count = value.shape[0] // step
    return jnp.concatenate(
        [value[(i ^ 1) * step : (i ^ 1) * step + step] for i in range(count)], axis=0
    )


def permuted(value, op, group):
    return value if op == 0 else swap_rows(value, op - 1, group)


def split_kernel(where_ref, field_ref, out_ref):
    pieces, layers, faces, group, blk = out_ref.shape
    half = pieces // 2
    first = where_ref[0] * half
    second = half - first
    lead = where_ref[1]
    for l in range(layers):
        at = lead if l == 0 else 1 - lead
        for f in range(faces):
            rows = field_ref[at, f].T.reshape(pieces, group, blk)
            out_ref[pl.ds(first, half), l, f] = rows[:half]
            out_ref[pl.ds(second, half), l, f] = rows[half:]


def join_kernel(where_ref, in_ref, out_ref):
    pieces, layers, faces, group, blk = in_ref.shape
    half = pieces // 2
    first = where_ref[0] * half
    second = half - first
    lead = where_ref[1]
    for l in range(layers):
        at = lead if l == 0 else 1 - lead
        for f in range(faces):
            low = in_ref[pl.ds(first, half), l, f].reshape(half * group, blk)
            top = in_ref[pl.ds(second, half), l, f].reshape(half * group, blk)
            out_ref[at, f] = jnp.concatenate([low.T, top.T], axis=1)


def field_of(masks, op, modes_dev):
    want = modes_dev * lax.shift_left(jnp.int32(1), jnp.maximum(op - 1, 0))
    found = jnp.int32(0)
    for j in range(masks.shape[0]):
        found = found + jnp.where(masks[j] == want, j, 0)
    return found


def prepare_kernel(
    masks_ref, adj_ref, where_ref, mean_ref, field_ref,
    dh_ref, dl_ref, hh_ref, hl_ref, ch_ref, cl_ref, dense,
):
    spot = pl.program_id(0)
    op = pl.program_id(1)
    faces, blk = mean_ref.shape[1], mean_ref.shape[2]
    lead = where_ref[1]
    layer = jnp.where(spot == 0, lead, 1 - lead)
    halo_at = pl.multiple_of((1 + layer) * blk, blk)
    cross_at = pl.multiple_of((2 - layer) * blk, blk)

    def build(src, scale):
        dense[...] = jnp.zeros_like(dense)
        for f in range(faces):
            rows = slice(f * blk, f * blk + blk)
            dense[f, rows] = src(f, 0)
            for s in range(4):
                other = adj_ref[layer, f, s]
                dense[other, rows] = dense[other, rows] + src(f, (3 + s) * blk)
        for g in range(faces):
            high, low = split2(dense[g] * scale)
            dh_ref[0, 0, :, g * blk : g * blk + blk] = high
            dl_ref[0, 0, :, g * blk : g * blk + blk] = low
        for f in range(faces):
            hh_ref[0, 0, f], hl_ref[0, 0, f] = split2(src(f, halo_at) * scale)
            ch_ref[0, 0, f], cl_ref[0, 0, f] = split2(src(f, cross_at) * scale)

    @pl.when(op == 0)
    def _():
        build(lambda f, k: mean_ref[0, f, :, pl.ds(k, blk)], 1.0)

    @pl.when(op > 0)
    def _():
        build(lambda f, k: field_ref[0, 0, f, :, pl.ds(k, blk)], COUPLING)


def off_layer(total, field, op_h, op_l, layer, f, group):
    high, low = split2(field)
    lefts, rights = [], []
    for op in range(op_h.shape[1]):
        ph, plow = permuted(high, op, group), permuted(low, op, group)
        wh, wl = op_h[layer, op, f], op_l[layer, op, f]
        lefts += [ph, plow, ph]
        rights += [wh, wh, wl]
    return total + dot_nt(jnp.concatenate(lefts, axis=1), jnp.concatenate(rights, axis=1))


def local_kernel(group, d0_ref, d1_ref, dh_ref, dl_ref, ch_ref, cl_ref, a0_ref, a1_ref):
    faces, rows, blk = d0_ref.shape
    ops = dh_ref.shape[1]
    for l, (d_ref, other_ref, acc_ref) in enumerate(
        ((d0_ref, d1_ref, a0_ref), (d1_ref, d0_ref, a1_ref))
    ):
        parts = [split2(d_ref[f]) for f in range(faces)]
        high = jnp.concatenate([p[0] for p in parts], axis=1)
        low = jnp.concatenate([p[1] for p in parts], axis=1)
        total = None
        for op in range(ops):
            ph, plow = permuted(high, op, group), permuted(low, op, group)
            term = dot_nt(ph, dh_ref[l, op]) + dot_nt(plow, dh_ref[l, op]) + dot_nt(ph, dl_ref[l, op])
            total = term if total is None else total + term
        for f in range(faces):
            here = d_ref[f] + total[:, f * blk : f * blk + blk]
            acc_ref[f] = off_layer(here, other_ref[f], ch_ref, cl_ref, l, f, group)


def finish_kernel(group, coef, layer, last, with_first, *refs):
    c_d, c_r = coef
    halo_ref, acc_ref, d_ref, r_ref = refs[:4]
    rest = list(refs[4:])
    x_ref = None if last else rest.pop(0)
    first_ref = rest.pop(0) if with_first else None
    hh_ref, hl_ref = rest[:2]
    outs = rest[2:]
    faces, rows, blk = d_ref.shape
    for f in range(faces):
        applied = off_layer(acc_ref[f], halo_ref[f], hh_ref, hl_ref, layer, f, group)
        result = r_ref[f] - applied
        if not last:
            outs[0][f] = result
            new = c_d * d_ref[f] + c_r * result
            outs[1][f] = new
            result = x_ref[f] + new
        if with_first:
            outs[-1][:, 0, f] = first_ref[f].reshape(rows // group, group, blk)
            outs[-1][:, 1, f] = result.reshape(rows // group, group, blk)
        else:
            outs[-1][f] = result


MIB = 1 << 20


def call(body, outs, args, smem=0, flops=0, limit=16):
    spaces = [pltpu.SMEM] * smem + [pltpu.VMEM] * (len(args) - smem)
    size = sum(a.size * a.dtype.itemsize for a in args) + sum(
        o.size * o.dtype.itemsize for o in outs
    )
    return pl.pallas_call(
        body,
        out_shape=outs,
        in_specs=[pl.BlockSpec(memory_space=s) for s in spaces],
        out_specs=[pl.BlockSpec(memory_space=pltpu.VMEM) for _ in outs],
        compiler_params=pltpu.CompilerParams(vmem_limit_bytes=limit * MIB),
        cost_estimate=pl.CostEstimate(flops=flops, bytes_accessed=size, transcendentals=0),
    )(*args)


def shape(dims, dtype=F32):
    return jax.ShapeDtypeStruct(tuple(dims), dtype)


def prepare(where, mean_operator, field_operators, adjacency, mode_masks, modes_dev, bits):
    layers, faces, blk, wide = mean_operator.shape
    ops = bits + 1
    full = faces * blk

    def layer_of(spot, where):
        return jnp.where(spot == 0, where[1], 1 - where[1])

    dense_spec = pl.BlockSpec((1, 1, full, full), lambda l, op, *_: (l, op, 0, 0))
    side_spec = pl.BlockSpec((1, 1, faces, blk, blk), lambda l, op, *_: (l, op, 0, 0, 0))
    grid_spec = pltpu.PrefetchScalarGridSpec(
        num_scalar_prefetch=3,
        grid=(layers, ops),
        in_specs=[
            pl.BlockSpec(
                (1, faces, blk, wide), lambda l, op, masks, adj, where: (layer_of(l, where), 0, 0, 0)
            ),
            pl.BlockSpec(
                (1, 1, faces, blk, wide),
                lambda l, op, masks, adj, where: (
                    field_of(masks, op, modes_dev), layer_of(l, where), 0, 0, 0,
                ),
            ),
        ],
        out_specs=[dense_spec] * 2 + [side_spec] * 4,
        scratch_shapes=[pltpu.VMEM((faces, full, blk), F32)],
    )
    dense = shape((layers, ops, full, full), BF16)
    side = shape((layers, ops, faces, blk, blk), BF16)
    return pl.pallas_call(
        prepare_kernel,
        grid_spec=grid_spec,
        out_shape=[dense] * 2 + [side] * 4,
        compiler_params=pltpu.CompilerParams(vmem_limit_bytes=42 * MIB),
        cost_estimate=pl.CostEstimate(flops=10**8, bytes_accessed=36 * MIB, transcendentals=0),
    )(mode_masks, adjacency, where, mean_operator, field_operators)


def pair_list(count, modes, inner):
    half = modes // 2
    pairs = []
    for s in range(count):
        t = s + 1 if (s % 2 == 0) == inner else s - 1
        if 0 <= t < count:
            turn = half if (s // 2 - t // 2) % 2 else 0
            pairs += [(s * modes + m, t * modes + (m ^ turn)) for m in range(modes)]
    return pairs


def per_device(source_field, mean_operator, field_operators, adjacency, mode_masks):
    layers, faces, blk, modes_dev = source_field.shape
    count, modes = lax.axis_size("space"), lax.axis_size("mode")
    bits = modes.bit_length() - 1
    group = modes_dev // modes
    rows = modes * group
    slab = lax.axis_index("space").astype(jnp.int32)
    flip = lax.shift_right_logical(slab, 1) & 1
    where = jnp.stack([flip, 1 - (slab & 1)])
    pieces = shape((modes, layers, faces, group, blk))
    layer = shape((faces, rows, blk))

    (sent,) = call(split_kernel, [pieces], [where, source_field], smem=1, limit=8)
    got = lax.all_to_all(sent, "mode", 0, 0, tiled=True)
    weights = prepare(
        where, mean_operator, field_operators, adjacency, mode_masks, modes_dev, bits
    )
    got, *weights = lax.optimization_barrier((got, *weights))
    dh, dl, hh, hl, ch, cl = weights
    b = [got[:, l].transpose(1, 0, 2, 3).reshape(faces, rows, blk) for l in range(layers)]

    links = [pair_list(count, modes, True), pair_list(count, modes, False)]
    sigma = THETA / DELTA
    rho = 1.0 / sigma
    d, r = [v / THETA for v in b], b
    x = d
    flops = 2 * rows * blk * blk * 3 * (bits + 1) * faces
    for step in range(DEGREE):
        last = step == DEGREE - 1
        halo = [lax.ppermute(d[l], AXES, links[l]) for l in range(layers)]
        acc = call(
            functools.partial(local_kernel, group),
            [layer, layer],
            [*d, dh, dl, ch, cl],
            flops=10 * flops,
        )
        rho_new = 1.0 / (2.0 * sigma - rho)
        coef = (rho_new * rho, 2.0 * rho_new / DELTA)
        rho = rho_new
        fresh = []
        for l in range(layers):
            gather = l == layers - 1 and step >= DEGREE - 2
            args = [halo[l], acc[l], d[l], r[l]] + ([] if last else [x[l]])
            args += [fresh[0][-1]] if gather else []
            fresh.append(
                call(
                    functools.partial(finish_kernel, group, coef, l, last, gather),
                    [layer] * (0 if last else 2) + [pieces if gather else layer],
                    args + [hh, hl],
                    flops=2 * flops,
                )
            )
        if last:
            r_back = lax.all_to_all(fresh[-1][-1], "mode", 0, 0, tiled=True)
        else:
            r, d, x = zip(*fresh)
            if step == DEGREE - 2:
                x_back = lax.all_to_all(x[-1], "mode", 0, 0, tiled=True)
    field = shape(source_field.shape)
    (x_end,) = call(join_kernel, [field], [where, x_back], smem=1, limit=8)
    (r_end,) = call(join_kernel, [field], [where, r_back], smem=1, limit=8)
    return x_end, r_end


def solution(mesh):
    in_specs = (
        P("space", None, None, "mode"),
        P("space", None, None, None),
        P(None, "space", None, None, None),
        P("space", None, None),
        P(),
    )
    out_specs = (P("space", None, None, "mode"), P("space", None, None, "mode"))
    return jax.shard_map(
        per_device, mesh=mesh, in_specs=in_specs, out_specs=out_specs, check_vma=False
    )
```

time: 525 us -> 154 us (0.29); the launches traced: 517 us -> 153 us
  matrix products: 195 us -> 0 us
  waiting for transfers between devices: 184 us -> 27.7 us
  Pallas kernels: 0 us -> 56.2 us
  local copies, waits for them, and re-layouts: 61.2 us -> 26 us
  other arithmetic: 16.9 us -> 0.08 us
  starting transfers between devices: 59 us -> 42.5 us
    dot_general x8 -> x0, matrix products: 195 us -> none  [the longest x4 131 us: operate_on(): jnp.einsum('jlfik,lfkm->jlfim', field_operators, columns, precision=lax.P...]
    ppermute x24 -> x8, waiting for transfers between devices: 184 us -> 13 us  [per_device(): halo = [lax.ppermute(d[l], AXES, links[l]) for l in range(layers)]]
    pallas_call x0 -> x16, Pallas kernels: none -> 56.2 us  [the longest x15 41.1 us: call(): pl.pallas_call(body, out_shape=outs, in_specs=[pl.BlockSpec(memory_space=...]
    ppermute x24 -> x8, starting transfers between devices: 59 us -> 17 us  [per_device(): halo = [lax.ppermute(d[l], AXES, links[l]) for l in range(layers)]]
    gather x12 -> x0, local copies, waits for them, and re-layouts: 34.2 us -> none  [gather_columns(): slab_layer[neighbours]]
    all_to_all x0 -> x3, starting transfers between devices: none -> 25.5 us  [the longest x1 9.29 us: per_device(): got = lax.all_to_all(sent, 'mode', 0, 0, tiled=True)]
    all_to_all x0 -> x3, waiting for transfers between devices: none -> 14.7 us  [the longest x1 14.7 us: per_device(): r_back = lax.all_to_all(fresh[-1][-1], 'mode', 0, 0, tiled=True)]
    concatenate x4 -> x0, other arithmetic: 10.7 us -> none  [gather_columns(): jnp.concatenate([centre[:, :, None], lower_layer[:, :, None], upper_layer...]
  transfers between devices with their start and end apart: 24 -> 11, of which waited for: 16 -> 5; matrix products, arithmetic and copies ran while one was open for 7% -> 0% of each run, Pallas kernels for 0% -> 33%
where the time goes in v1:
time: 154 us; the launch traced here: 153 us
  Pallas kernels  56.2 us (36%)
  starting transfers between devices  42.5 us (28%)
  waiting for transfers between devices  27.7 us (18%)
  local copies, waits for them, and re-layouts  26 us (17%)
    pallas_call x15, Pallas kernels, call(): pl.pallas_call(body, out_shape=outs, in_specs=[pl.BlockSpec(memory_space=...  41.1 us
    unnamed x48, local copies, waits for them, and re-layouts  24.5 us
    ppermute x8, starting transfers between devices, per_device(): halo = [lax.ppermute(d[l], AXES, links[l]) for l in range(layers)]  17 us
    pallas_call x1, Pallas kernels, prepare(): pl.pallas_call(prepare_kernel, grid_spec=grid_spec, out_shape=[dense] * 2...  15.1 us
    all_to_all x1, waiting for transfers between devices, per_device(): r_back = lax.all_to_all(fresh[-1][-1], 'mode', 0, 0, tiled=True)  14.7 us
    ppermute x8, waiting for transfers between devices, per_device(): halo = [lax.ppermute(d[l], AXES, links[l]) for l in range(layers)]  13 us
    all_to_all x1, starting transfers between devices, per_device(): got = lax.all_to_all(sent, 'mode', 0, 0, tiled=True)  9.29 us
    all_to_all x1, starting transfers between devices, per_device(): x_back = lax.all_to_all(x[-1], 'mode', 0, 0, tiled=True)  8.14 us
  transfers between devices with their start and end apart: 11, of which 5 were waited for; matrix products, arithmetic and copies ran while one was open for 0% of the time, Pallas kernels for 33%

profile of v1, /device:TPU:1, one launch (start us, length us, event | category | flops | bytes accessed | tf_op | source)
XLA Modules:
  0.0 153.4 jit_solution(10336213770064027257)
XLA Ops:
  0.6 0.0 copy-start.10
  0.6 0.0 copy-start.11
  0.7 0.1 pad_add_fusion.where_ref
  0.7 1.2 copy-done.2
  2.0 1.9 %shard_map.68 = f32[16,2,4,16,128]{4,3,2,1,0:T(8,128)} custom-call(s32[2]{0:T(128)S(1)} %pad_add_fusion.where_ref, f32[2,4,128,256]{3,2,1,0:T(8,128)S(1)} %copy-done.2), custom_call_target="tpu_custom_call" | custom-call | bytes 2097160 | tf_op jit(solution)/shard_map/pallas_call | solution.py:176
  3.8 9.3 %all-to-all-start = ((f32[16,2,4,16,128]{4,3,2,1,0:T(8,128)}), f32[16,2,4,16,128]{4,3,2,1,0:T(8,128)}, u32[]{:S(2)}, u32[]{:S(2)}) async-start(f32[16,2,4,16,128]{4,3,2,1,0:T(8,128)} %shard_map.68), calls=%async_computation | async-start | bytes 2097152 | tf_op jit(solution)/shard_map/all_to_all | solution.py:252
  13.1 0.0 copy-done.10
  13.1 0.0 copy-done.11
  13.1 0.0 copy-start.1
  13.1 2.0 %copy-done.1 = f32[2,4,128,896]{3,2,1,0:T(8,128)S(1)} copy-done((f32[2,4,128,896]{3,2,1,0:T(8,128)S(1)}, f32[2,4,128,896]{3,2,1,0:T(8,128)}, u32[]{:S(2)}) %copy-start.1) | copy-done | bytes 3670040
  15.2 15.1 %shard_map.69 = (bf16[2,5,512,512]{3,2,1,0:T(8,128)(2,1)}, bf16[2,5,512,512]{3,2,1,0:T(8,128)(2,1)}, bf16[2,5,4,128,128]{4,3,2,1,0:T(8,128)(2,1)S(1)}, bf16[2,5,...) custom-call(s32[4]{0:T(128)S(1)} %copy-done.11, ...), custom_call_target="tpu_custom_call" | custom-call | flops 100000000 | bytes 37748736 | tf_op jit(solution)/shard_map/pallas_call | solution.py:219
  30.2 1.1 copy-done.18
  31.3 1.1 copy-done.21
  32.4 0.0 all-to-all-done
  32.4 1.5 slice_bitcast_fusion
  33.9 0.4 collective-permute-start.2
  34.4 0.7 collective-permute-start
  35.1 2.5 %copy-done.12 = bf16[2,5,512,512]{3,2,1,0:T(8,128)(2,1)S(1)} copy-done((bf16[2,5,512,512]{3,2,1,0:T(8,128)(2,1)S(1)}, bf16[2,5,512,512]{3,2,1,0:T(8,128)(2,1)}, u32[]{:S(2)}) %copy-start.12) | copy-done | bytes 5242904
  37.6 2.5 %copy-done.15 = bf16[2,5,512,512]{3,2,1,0:T(8,128)(2,1)S(1)} copy-done((bf16[2,5,512,512]{3,2,1,0:T(8,128)(2,1)S(1)}, bf16[2,5,512,512]{3,2,1,0:T(8,128)(2,1)}, u32[]{:S(2)}) %copy-start.15) | copy-done | bytes 5242904
  40.1 6.3 %shard_map.70 = (f32[4,256,128]{2,1,0:T(8,128)S(1)}, f32[4,256,128]{2,1,0:T(8,128)S(1)}) custom-call(f32[4,256,128]{2,1,0:T(8,128)S(1)} %bitcast.18, f32[4,256,128]{2,1,0:T(8,128)S(1)} %bitcast.13, bf16[2,5,512,512]{3,2,1,0:T(8,128)(2,1)S(1)} %copy-done.12, bf16[2,5,512,512]{3,2,1,0:T(8,128)(2,1)S(1)} %copy-done.15, ...), custom_call_target="tpu_custom_call" | custom-call | flops 5033164800 | bytes 15204352 | tf_op jit(solution)/shard_map/pallas_call | solution.py:176
  46.4 1.0 collective-permute-done.2.refs_0_
  47.4 1.2 shard_map.72
  48.6 0.0 copy-start.13
  48.6 4.5 %collective-permute-start.4 = (f32[4,256,128]{2,1,0:T(8,128)S(1)}, f32[4,256,128]{2,1,0:T(8,128)S(1)}, u32[]{:S(2)}, u32[]{:S(2)}) collective-permute-start(f32[4,256,128]{2,1,0:T(8,128)S(1)} %get-tuple-element.57.d0_ref.refs_2_), channel_id=1, source_target_pairs={{0,16},{1,17},{2,18},{3,19},{4,20},{5,21},{6,22},{7,23},{8,24},{9,... | collective-permute-start | bytes 1572872 | tf_op jit(solution)/shard_map/ppermute | solution.py:268
  53.1 0.0 collective-permute-done.refs_0_
  53.1 1.2 shard_map.71
  54.3 0.9 collective-permute-start.1
  55.2 6.3 %shard_map.73 = (f32[4,256,128]{2,1,0:T(8,128)S(1)}, f32[4,256,128]{2,1,0:T(8,128)S(1)}) custom-call(f32[4,256,128]{2,1,0:T(8,128)S(1)} %get-tuple-element.57.d0_ref.refs_2_, f32[4,256,128]{2,1,0:T(8,128)S(1)} %get-tuple-element.55.d1_ref.refs_2_, bf16[2,5,512,512]{3,2,1,0:T(8,128)(2,1)S(1)} %copy-done.13, bf16[2,5,512,512]{3,2,1,0:T(8,128)(2,1)S(1)} %copy-done.16, ...), custom_call_target="tpu_custom_call" | custom-call | flops 5033164800 | bytes 15204352 | tf_op jit(solution)/shard_map/pallas_call | solution.py:176
  61.6 2.9 %collective-permute-done.4.refs_0_ = f32[4,256,128]{2,1,0:T(8,128)S(1)} collective-permute-done((f32[4,256,128]{2,1,0:T(8,128)S(1)}, f32[4,256,128]{2,1,0:T(8,128)S(1)}, u32[]{:S(2)}, u32[]{:S(2)}) %collective-permute-start.4) | collective-permute-done | bytes 524320 | tf_op jit(solution)/shard_map/ppermute | solution.py:268
  64.5 1.2 shard_map.75
  65.7 1.2 collective-permute-start.5
  66.9 0.0 collective-permute-done.1.refs_0_
  66.9 1.2 shard_map.74
  68.1 0.9 collective-permute-start.3
  69.0 6.3 %shard_map.76 = (f32[4,256,128]{2,1,0:T(8,128)S(1)}, f32[4,256,128]{2,1,0:T(8,128)S(1)}) custom-call(f32[4,256,128]{2,1,0:T(8,128)S(1)} %get-tuple-element.65.d0_ref.refs_2_, f32[4,256,128]{2,1,0:T(8,128)S(1)} %get-tuple-element.61.d1_ref.refs_2_, bf16[2,5,512,512]{3,2,1,0:T(8,128)(2,1)S(1)} %copy-done.13, bf16[2,5,512,512]{3,2,1,0:T(8,128)(2,1)S(1)} %copy-done.16, ...), custom_call_target="tpu_custom_call" | custom-call | flops 5033164800 | bytes 15204352 | tf_op jit(solution)/shard_map/pallas_call | solution.py:176
  75.4 2.3 %collective-permute-done.5.refs_0_ = f32[4,256,128]{2,1,0:T(8,128)S(1)} collective-permute-done((f32[4,256,128]{2,1,0:T(8,128)S(1)}, f32[4,256,128]{2,1,0:T(8,128)S(1)}, u32[]{:S(2)}, u32[]{:S(2)}) %collective-permute-start.5) | collective-permute-done | bytes 524320 | tf_op jit(solution)/shard_map/ppermute | solution.py:268
  77.7 1.2 shard_map.77
  78.9 0.8 copy-done.4
  79.7 0.0 collective-permute-done.3.refs_0_
  79.7 1.2 shard_map.78
  80.9 0.0 copy-start.3
  80.9 1.0 copy-done.3
  81.8 0.8 copy-done.6
  82.7 0.8 copy-done.8
  83.5 8.1 %all-to-all-start.1 = ((f32[16,2,4,16,128]{4,3,2,1,0:T(8,128)}), f32[16,2,4,16,128]{4,3,2,1,0:T(8,128)}, u32[]{:S(2)}, u32[]{:S(2)}) async-start(f32[16,2,4,16,128]{4,3,2,1,0:T(8,128)} %copy-done.3), calls=%async_computation.1 | async-start | bytes 2097152 | tf_op jit(solution)/shard_map/all_to_all | solution.py:296
  91.6 7.5 %collective-permute-start.7 = (f32[4,256,128]{2,1,0:T(8,128)}, f32[4,256,128]{2,1,0:T(8,128)S(1)}, u32[]{:S(2)}, u32[]{:S(2)}) collective-permute-start(f32[4,256,128]{2,1,0:T(8,128)} %copy-done.4), channel_id=1, source_target_pairs={{0,16},{1,17},{2,18},{3,19},{4,20},{5,21},{6,22},{7,23},{8,24},{9,... | collective-permute-start | bytes 1572872 | tf_op jit(solution)/shard_map/ppermute | solution.py:268
  99.1 0.9 collective-permute-start.6
  100.0 1.0 copy-done.5
  101.1 1.0 copy-done.9
  102.1 2.5 %copy-done.14 = bf16[2,5,512,512]{3,2,1,0:T(8,128)(2,1)S(1)} copy-done((bf16[2,5,512,512]{3,2,1,0:T(8,128)(2,1)S(1)}, bf16[2,5,512,512]{3,2,1,0:T(8,128)(2,1)}, u32[]{:S(2)}) %copy-start.14) | copy-done | bytes 5242904
  104.6 2.5 %copy-done.17 = bf16[2,5,512,512]{3,2,1,0:T(8,128)(2,1)S(1)} copy-done((bf16[2,5,512,512]{3,2,1,0:T(8,128)(2,1)S(1)}, bf16[2,5,512,512]{3,2,1,0:T(8,128)(2,1)}, u32[]{:S(2)}) %copy-start.17) | copy-done | bytes 5242904
  107.1 1.3 copy-done.20
  108.4 1.3 copy-done.23
  109.7 6.3 %shard_map.80 = (f32[4,256,128]{2,1,0:T(8,128)S(1)}, f32[4,256,128]{2,1,0:T(8,128)S(1)}) custom-call(f32[4,256,128]{2,1,0:T(8,128)S(1)} %copy-done.5, f32[4,256,128]{2,1,0:T(8,128)S(1)} %copy-done.9, bf16[2,5,512,512]{3,2,1,0:T(8,128)(2,1)S(1)} %copy-done.14, bf16[2,5,512,512]{3,2,1,0:T(8,128)(2,1)S(1)} %copy-done.17, ...), custom_call_target="tpu_custom_call" | custom-call | flops 5033164800 | bytes 15204352 | tf_op jit(solution)/shard_map/pallas_call | solution.py:176
  116.1 6.8 %collective-permute-done.7.refs_0_ = f32[4,256,128]{2,1,0:T(8,128)S(1)} collective-permute-done((f32[4,256,128]{2,1,0:T(8,128)}, f32[4,256,128]{2,1,0:T(8,128)S(1)}, u32[]{:S(2)}, u32[]{:S(2)}) %collective-permute-start.7) | collective-permute-done | bytes 524320 | tf_op jit(solution)/shard_map/ppermute | solution.py:268
  122.8 1.2 shard_map.81.refs_4_
  124.0 0.0 collective-permute-done.6.refs_0_
  124.1 1.2 shard_map.82
  125.3 1.0 copy-done
  126.3 0.0 all-to-all-done.1.in_ref
  126.3 8.0 %all-to-all-start.2 = ((f32[16,2,4,16,128]{4,3,2,1,0:T(8,128)}), f32[16,2,4,16,128]{4,3,2,1,0:T(8,128)S(1)}, u32[]{:S(2)}, u32[]{:S(2)}) async-start(f32[16,2,4,16,128]{4,3,2,1,0:T(8,128)} %copy-done), calls=%async_computation.2 | async-start | bytes 2097152 | tf_op jit(solution)/shard_map/all_to_all | solution.py:292
  134.3 2.5 %shard_map.79 = f32[2,4,128,256]{3,2,1,0:T(8,128)} custom-call(s32[2]{0:T(128)S(1)} %pad_add_fusion.where_ref, f32[16,2,4,16,128]{4,3,2,1,0:T(8,128)} %all-to-all-done.1.in_ref), custom_call_target="tpu_custom_call" | custom-call | bytes 2097160 | tf_op jit(solution)/shard_map/pallas_call | solution.py:176
  136.8 14.7 %all-to-all-done.2.in_ref = f32[16,2,4,16,128]{4,3,2,1,0:T(8,128)S(1)} async-done(((f32[16,2,4,16,128]{4,3,2,1,0:T(8,128)}), f32[16,2,4,16,128]{4,3,2,1,0:T(8,128)S(1)}, u32[]{:S(2)}, u32[]{:S(2)}) %all-to-all-start.2) | async-done | bytes 1048608 | tf_op jit(solution)/shard_map/all_to_all | solution.py:292
  151.5 1.9 %shard_map.83 = f32[2,4,128,256]{3,2,1,0:T(8,128)} custom-call(s32[2]{0:T(128)S(1)} %pad_add_fusion.where_ref, f32[16,2,4,16,128]{4,3,2,1,0:T(8,128)S(1)} %all-to-all-done.2.in_ref), custom_call_target="tpu_custom_call" | custom-call | bytes 2097160 | tf_op jit(solution)/shard_map/pallas_call | solution.py:176
  (26 shorter events, 0.1 us)
Async XLA Ops:
  0.6 12.5 %copy-start.10 = (s32[2,4,4]{2,1,0:T(4,128)S(1)}, s32[2,4,4]{2,1,0:T(4,128)}, u32[]{:S(2)}) copy-start(s32[2,4,4]{2,1,0:T(4,128)} %adj_ref.1) | copy-start | bytes 388
  0.6 12.5 %copy-start.11 = (s32[4]{0:T(128)S(1)}, s32[4]{0:T(128)}, u32[]{:S(2)}) copy-start(s32[4]{0:T(128)} %masks_ref.1) | copy-start | bytes 52
  0.7 1.2 copy-start.2
  3.8 28.6 %all-to-all-start = ((f32[16,2,4,16,128]{4,3,2,1,0:T(8,128)}), f32[16,2,4,16,128]{4,3,2,1,0:T(8,128)}, u32[]{:S(2)}, u32[]{:S(2)}) async-start(f32[16,2,4,16,128]{4,3,2,1,0:T(8,128)} %shard_map.68), calls=%async_computation | async-start | bytes 2097152 | tf_op jit(solution)/shard_map/all_to_all | solution.py:252
  13.1 2.0 %copy-start.1 = (f32[2,4,128,896]{3,2,1,0:T(8,128)S(1)}, f32[2,4,128,896]{3,2,1,0:T(8,128)}, u32[]{:S(2)}) copy-start(f32[2,4,128,896]{3,2,1,0:T(8,128)} %mean_ref.1) | copy-start | bytes 11010052
  30.2 1.1 copy-start.18
  31.3 1.1 copy-start.21
  32.4 2.7 %copy-start.19 = (bf16[2,5,4,128,128]{4,3,2,1,0:T(8,128)(2,1)S(1)}, bf16[2,5,4,128,128]{4,3,2,1,0:T(8,128)(2,1)}, u32[]{:S(2)}) copy-start(bf16[2,5,4,128,128]{4,3,2,1,0:T(8,128)(2,1)} %copy-done.18) | copy-start | bytes 3932164
  32.4 2.7 %copy-start.22 = (bf16[2,5,4,128,128]{4,3,2,1,0:T(8,128)(2,1)S(1)}, bf16[2,5,4,128,128]{4,3,2,1,0:T(8,128)(2,1)}, u32[]{:S(2)}) copy-start(bf16[2,5,4,128,128]{4,3,2,1,0:T(8,128)(2,1)} %copy-done.21) | copy-start | bytes 3932164
  33.9 13.5 %collective-permute-start.2 = (f32[4,256,128]{2,1,0:T(8,128)S(1)}, f32[4,256,128]{2,1,0:T(8,128)S(1)}, u32[]{:S(2)}, u32[]{:S(2)}) collective-permute-start(f32[4,256,128]{2,1,0:T(8,128)S(1)} %bitcast.17), channel_id=1, source_target_pairs={{0,16},{1,17},{2,18},{3,19},{4,20},{5,21},{6,22},{7,23},{8,24},{9,... | collective-permute-start | bytes 1572872 | tf_op jit(solution)/shard_map/ppermute | solution.py:268
  34.4 18.7 %collective-permute-start = (f32[4,256,128]{2,1,0:T(8,128)S(1)}, f32[4,256,128]{2,1,0:T(8,128)S(1)}, u32[]{:S(2)}, u32[]{:S(2)}) collective-permute-start(f32[4,256,128]{2,1,0:T(8,128)S(1)} %bitcast.12), channel_id=1, source_target_pairs={{16,40},{17,41},{18,42},{19,43},{20,44},{21,45},{22,46},{23,47},{2... | collective-permute-start | bytes 1572872 | tf_op jit(solution)/shard_map/ppermute | solution.py:268
  35.1 2.5 %copy-start.12 = (bf16[2,5,512,512]{3,2,1,0:T(8,128)(2,1)S(1)}, bf16[2,5,512,512]{3,2,1,0:T(8,128)(2,1)}, u32[]{:S(2)}) copy-start(bf16[2,5,512,512]{3,2,1,0:T(8,128)(2,1)} %get-tuple-element.48.dh_ref) | copy-start | bytes 15728644
  37.6 2.5 %copy-start.15 = (bf16[2,5,512,512]{3,2,1,0:T(8,128)(2,1)S(1)}, bf16[2,5,512,512]{3,2,1,0:T(8,128)(2,1)}, u32[]{:S(2)}) copy-start(bf16[2,5,512,512]{3,2,1,0:T(8,128)(2,1)} %get-tuple-element.49.dl_ref) | copy-start | bytes 15728644
  47.4 7.8 %copy-start.16 = (bf16[2,5,512,512]{3,2,1,0:T(8,128)(2,1)S(1)}, bf16[2,5,512,512]{3,2,1,0:T(8,128)(2,1)}, u32[]{:S(2)}) copy-start(bf16[2,5,512,512]{3,2,1,0:T(8,128)(2,1)} %get-tuple-element.49.dl_ref) | copy-start | bytes 15728644
  48.6 6.6 %copy-start.13 = (bf16[2,5,512,512]{3,2,1,0:T(8,128)(2,1)S(1)}, bf16[2,5,512,512]{3,2,1,0:T(8,128)(2,1)}, u32[]{:S(2)}) copy-start(bf16[2,5,512,512]{3,2,1,0:T(8,128)(2,1)} %get-tuple-element.48.dh_ref) | copy-start | bytes 15728644
  48.6 15.9 %collective-permute-start.4 = (f32[4,256,128]{2,1,0:T(8,128)S(1)}, f32[4,256,128]{2,1,0:T(8,128)S(1)}, u32[]{:S(2)}, u32[]{:S(2)}) collective-permute-start(f32[4,256,128]{2,1,0:T(8,128)S(1)} %get-tuple-element.57.d0_ref.refs_2_), channel_id=1, source_target_pairs={{0,16},{1,17},{2,18},{3,19},{4,20},{5,21},{6,22},{7,23},{8,24},{9,... | collective-permute-start | bytes 1572872 | tf_op jit(solution)/shard_map/ppermute | solution.py:268
  54.3 12.6 %collective-permute-start.1 = (f32[4,256,128]{2,1,0:T(8,128)S(1)}, f32[4,256,128]{2,1,0:T(8,128)S(1)}, u32[]{:S(2)}, u32[]{:S(2)}) collective-permute-start(f32[4,256,128]{2,1,0:T(8,128)S(1)} %get-tuple-element.55.d1_ref.refs_2_), channel_id=1, source_target_pairs={{16,40},{17,41},{18,42},{19,43},{20,44},{21,45},{22,46},{23,47},{2... | collective-permute-start | bytes 1572872 | tf_op jit(solution)/shard_map/ppermute | solution.py:268
  65.7 12.0 %collective-permute-start.5 = (f32[4,256,128]{2,1,0:T(8,128)S(1)}, f32[4,256,128]{2,1,0:T(8,128)S(1)}, u32[]{:S(2)}, u32[]{:S(2)}) collective-permute-start(f32[4,256,128]{2,1,0:T(8,128)S(1)} %get-tuple-element.65.d0_ref.refs_2_), channel_id=1, source_target_pairs={{0,16},{1,17},{2,18},{3,19},{4,20},{5,21},{6,22},{7,23},{8,24},{9,... | collective-permute-start | bytes 1572872 | tf_op jit(solution)/shard_map/ppermute | solution.py:268
  68.1 11.6 %collective-permute-start.3 = (f32[4,256,128]{2,1,0:T(8,128)S(1)}, f32[4,256,128]{2,1,0:T(8,128)S(1)}, u32[]{:S(2)}, u32[]{:S(2)}) collective-permute-start(f32[4,256,128]{2,1,0:T(8,128)S(1)} %get-tuple-element.61.d1_ref.refs_2_), channel_id=1, source_target_pairs={{16,40},{17,41},{18,42},{19,43},{20,44},{21,45},{22,46},{23,47},{2... | collective-permute-start | bytes 1572872 | tf_op jit(solution)/shard_map/ppermute | solution.py:268
  78.9 0.8 copy-start.4
  80.9 1.0 copy-start.3
  81.8 0.8 copy-start.6
  82.7 0.8 copy-start.8
  83.5 42.8 %all-to-all-start.1 = ((f32[16,2,4,16,128]{4,3,2,1,0:T(8,128)}), f32[16,2,4,16,128]{4,3,2,1,0:T(8,128)}, u32[]{:S(2)}, u32[]{:S(2)}) async-start(f32[16,2,4,16,128]{4,3,2,1,0:T(8,128)} %copy-done.3), calls=%async_computation.1 | async-start | bytes 2097152 | tf_op jit(solution)/shard_map/all_to_all | solution.py:296
  91.6 31.2 %collective-permute-start.7 = (f32[4,256,128]{2,1,0:T(8,128)}, f32[4,256,128]{2,1,0:T(8,128)S(1)}, u32[]{:S(2)}, u32[]{:S(2)}) collective-permute-start(f32[4,256,128]{2,1,0:T(8,128)} %copy-done.4), channel_id=1, source_target_pairs={{0,16},{1,17},{2,18},{3,19},{4,20},{5,21},{6,22},{7,23},{8,24},{9,... | collective-permute-start | bytes 1572872 | tf_op jit(solution)/shard_map/ppermute | solution.py:268
  99.1 25.0 %collective-permute-start.6 = (f32[4,256,128]{2,1,0:T(8,128)}, f32[4,256,128]{2,1,0:T(8,128)S(1)}, u32[]{:S(2)}, u32[]{:S(2)}) collective-permute-start(f32[4,256,128]{2,1,0:T(8,128)} %copy-done.8), channel_id=1, source_target_pairs={{16,40},{17,41},{18,42},{19,43},{20,44},{21,45},{22,46},{23,47},{2... | collective-permute-start | bytes 1572872 | tf_op jit(solution)/shard_map/ppermute | solution.py:268
  100.0 1.0 copy-start.5
  101.1 1.0 copy-start.9
  102.1 2.5 %copy-start.14 = (bf16[2,5,512,512]{3,2,1,0:T(8,128)(2,1)S(1)}, bf16[2,5,512,512]{3,2,1,0:T(8,128)(2,1)}, u32[]{:S(2)}) copy-start(bf16[2,5,512,512]{3,2,1,0:T(8,128)(2,1)} %get-tuple-element.48.dh_ref) | copy-start | bytes 15728644
  104.6 2.5 %copy-start.17 = (bf16[2,5,512,512]{3,2,1,0:T(8,128)(2,1)S(1)}, bf16[2,5,512,512]{3,2,1,0:T(8,128)(2,1)}, u32[]{:S(2)}) copy-start(bf16[2,5,512,512]{3,2,1,0:T(8,128)(2,1)} %get-tuple-element.49.dl_ref) | copy-start | bytes 15728644
  107.1 1.3 copy-start.20
  108.4 1.3 copy-start.23
  116.1 8.0 %copy-start.7 = (f32[4,256,128]{2,1,0:T(8,128)S(1)}, f32[4,256,128]{2,1,0:T(8,128)}, u32[]{:S(2)}) copy-start(f32[4,256,128]{2,1,0:T(8,128)} %copy-done.6) | copy-start | bytes 1572868
  125.3 1.0 copy-start
  126.3 25.2 %all-to-all-start.2 = ((f32[16,2,4,16,128]{4,3,2,1,0:T(8,128)}), f32[16,2,4,16,128]{4,3,2,1,0:T(8,128)S(1)}, u32[]{:S(2)}, u32[]{:S(2)}) async-start(f32[16,2,4,16,128]{4,3,2,1,0:T(8,128)} %copy-done), calls=%async_computation.2 | async-start | bytes 2097152 | tf_op jit(solution)/shard_map/all_to_all | solution.py:292

commit v2 on v1

--- a/solution.py
+++ b/solution.py
@@ -39,31 +39,34 @@
 
 
 def split_kernel(where_ref, field_ref, out_ref):
-    pieces, layers, faces, group, blk = out_ref.shape
+    pieces, _, faces, group, blk = out_ref.shape
+    half = pieces // 2
+    first = where_ref[0] * half
+    second = half - first
+    for f in range(faces):
+        rows = field_ref[0, f].T.reshape(pieces, group, blk)
+        out_ref[pl.ds(first, half), 0, f] = rows[:half]
+        out_ref[pl.ds(second, half), 0, f] = rows[half:]
+
+
+def join_kernel(where_ref, in_ref, x_ref, r_ref, buffer, sems):
+    pieces, fields, layers, faces, group, blk = in_ref.shape
     half = pieces // 2
     first = where_ref[0] * half
     second = half - first
     lead = where_ref[1]
-    for l in range(layers):
-        at = lead if l == 0 else 1 - lead
-        for f in range(faces):
-            rows = field_ref[at, f].T.reshape(pieces, group, blk)
-            out_ref[pl.ds(first, half), l, f] = rows[:half]
-            out_ref[pl.ds(second, half), l, f] = rows[half:]
-
-
-def join_kernel(where_ref, in_ref, out_ref):
-    pieces, layers, faces, group, blk = in_ref.shape
-    half = pieces // 2
-    first = where_ref[0] * half
-    second = half - first
-    lead = where_ref[1]
-    for l in range(layers):
-        at = lead if l == 0 else 1 - lead
-        for f in range(faces):
-            low = in_ref[pl.ds(first, half), l, f].reshape(half * group, blk)
-            top = in_ref[pl.ds(second, half), l, f].reshape(half * group, blk)
-            out_ref[at, f] = jnp.concatenate([low.T, top.T], axis=1)
+    copies = []
+    for k, out_ref in enumerate((x_ref, r_ref)):
+        for l in range(layers):
+            at = lead if l == 0 else 1 - lead
+            for f in range(faces):
+                low = in_ref[pl.ds(first, half), k, l, f].reshape(half * group, blk)
+                top = in_ref[pl.ds(second, half), k, l, f].reshape(half * group, blk)
+                buffer[k, l, f] = jnp.concatenate([low.T, top.T], axis=1)
+            copies.append(pltpu.make_async_copy(buffer.at[k, l], out_ref.at[at], sems.at[k, l]))
+            copies[-1].start()
+    for copy in copies:
+        copy.wait()
 
 
 def field_of(masks, op, modes_dev):
@@ -122,13 +125,16 @@
     return total + dot_nt(jnp.concatenate(lefts, axis=1), jnp.concatenate(rights, axis=1))
 
 
-def local_kernel(group, d0_ref, d1_ref, dh_ref, dl_ref, ch_ref, cl_ref, a0_ref, a1_ref):
-    faces, rows, blk = d0_ref.shape
+def local_kernel(group, with_x, *refs):
+    count = 6 if with_x else 4
+    d_refs, r_refs, x_refs = refs[0:2], refs[2:4], refs[4:count]
+    dh_ref, dl_ref, ch_ref, cl_ref = refs[count : count + 4]
+    pre_refs = refs[count + 4 : count + 6]
+    x_outs = refs[count + 6 :]
+    faces, rows, blk = d_refs[0].shape
     ops = dh_ref.shape[1]
-    for l, (d_ref, other_ref, acc_ref) in enumerate(
-        ((d0_ref, d1_ref, a0_ref), (d1_ref, d0_ref, a1_ref))
-    ):
-        parts = [split2(d_ref[f]) for f in range(faces)]
+    for l in range(2):
+        parts = [split2(d_refs[l][f]) for f in range(faces)]
         high = jnp.concatenate([p[0] for p in parts], axis=1)
         low = jnp.concatenate([p[1] for p in parts], axis=1)
         total = None
@@ -137,38 +143,51 @@
             term = dot_nt(ph, dh_ref[l, op]) + dot_nt(plow, dh_ref[l, op]) + dot_nt(ph, dl_ref[l, op])
             total = term if total is None else total + term
         for f in range(faces):
-            here = d_ref[f] + total[:, f * blk : f * blk + blk]
-            acc_ref[f] = off_layer(here, other_ref[f], ch_ref, cl_ref, l, f, group)
-
-
-def finish_kernel(group, coef, layer, last, with_first, *refs):
+            here = d_refs[l][f] + total[:, f * blk : f * blk + blk]
+            applied = off_layer(here, d_refs[1 - l][f], ch_ref, cl_ref, l, f, group)
+            pre_refs[l][f] = r_refs[l][f] - applied
+            if with_x:
+                x_outs[l][f] = x_refs[l][f] + d_refs[l][f]
+
+
+def finish_kernel(group, coef, layer, halo_ref, pre_ref, hh_ref, hl_ref, d_ref, r_out, d_out):
     c_d, c_r = coef
-    halo_ref, acc_ref, d_ref, r_ref = refs[:4]
-    rest = list(refs[4:])
-    x_ref = None if last else rest.pop(0)
-    first_ref = rest.pop(0) if with_first else None
-    hh_ref, hl_ref = rest[:2]
-    outs = rest[2:]
-    faces, rows, blk = d_ref.shape
-    for f in range(faces):
-        applied = off_layer(acc_ref[f], halo_ref[f], hh_ref, hl_ref, layer, f, group)
-        result = r_ref[f] - applied
-        if not last:
-            outs[0][f] = result
-            new = c_d * d_ref[f] + c_r * result
-            outs[1][f] = new
-            result = x_ref[f] + new
-        if with_first:
-            outs[-1][:, 0, f] = first_ref[f].reshape(rows // group, group, blk)
-            outs[-1][:, 1, f] = result.reshape(rows // group, group, blk)
-        else:
-            outs[-1][f] = result
+    for f in range(halo_ref.shape[0]):
+        residual = pre_ref[f] - off_layer(0.0, halo_ref[f], hh_ref, hl_ref, layer, f, group)
+        r_out[f] = residual
+        d_out[f] = c_d * d_ref[f] + c_r * residual
+
+
+def last_kernel(
+    group, halo0_ref, halo1_ref, pre0_ref, pre1_ref, x0_ref, x1_ref, hh_ref, hl_ref,
+    send_ref, buffer, sems,
+):
+    copies = []
+
+    def send(k, l):
+        copies.append(
+            pltpu.make_async_copy(buffer.at[:, k, l], send_ref.at[:, k, l], sems.at[k, l])
+        )
+        copies[-1].start()
+
+    faces, _, blk = halo0_ref.shape
+    for l, x_ref in enumerate((x0_ref, x1_ref)):
+        for f in range(faces):
+            buffer[:, 0, l, f] = x_ref[f].reshape(-1, group, blk)
+        send(0, l)
+    for l, (halo_ref, pre_ref) in enumerate(((halo0_ref, pre0_ref), (halo1_ref, pre1_ref))):
+        for f in range(faces):
+            share = off_layer(0.0, halo_ref[f], hh_ref, hl_ref, l, f, group)
+            buffer[:, 1, l, f] = (pre_ref[f] - share).reshape(-1, group, blk)
+        send(1, l)
+    for copy in copies:
+        copy.wait()
 
 
 MIB = 1 << 20
 
 
-def call(body, outs, args, smem=0, flops=0, limit=16):
+def call(body, outs, args, smem=0, flops=0, limit=6, out_space=pltpu.VMEM, scratch=()):
     spaces = [pltpu.SMEM] * smem + [pltpu.VMEM] * (len(args) - smem)
     size = sum(a.size * a.dtype.itemsize for a in args) + sum(
         o.size * o.dtype.itemsize for o in outs
@@ -177,7 +196,8 @@
         body,
         out_shape=outs,
         in_specs=[pl.BlockSpec(memory_space=s) for s in spaces],
-        out_specs=[pl.BlockSpec(memory_space=pltpu.VMEM) for _ in outs],
+        out_specs=[pl.BlockSpec(memory_space=out_space) for _ in outs],
+        scratch_shapes=list(scratch),
         compiler_params=pltpu.CompilerParams(vmem_limit_bytes=limit * MIB),
         cost_estimate=pl.CostEstimate(flops=flops, bytes_accessed=size, transcendentals=0),
     )(*args)
@@ -220,7 +240,7 @@
         prepare_kernel,
         grid_spec=grid_spec,
         out_shape=[dense] * 2 + [side] * 4,
-        compiler_params=pltpu.CompilerParams(vmem_limit_bytes=42 * MIB),
+        compiler_params=pltpu.CompilerParams(vmem_limit_bytes=56 * MIB),
         cost_estimate=pl.CostEstimate(flops=10**8, bytes_accessed=36 * MIB, transcendentals=0),
     )(mode_masks, adjacency, where, mean_operator, field_operators)
 
@@ -248,7 +268,23 @@
     pieces = shape((modes, layers, faces, group, blk))
     layer = shape((faces, rows, blk))
 
-    (sent,) = call(split_kernel, [pieces], [where, source_field], smem=1, limit=8)
+    sent = pl.pallas_call(
+        split_kernel,
+        grid_spec=pltpu.PrefetchScalarGridSpec(
+            num_scalar_prefetch=1,
+            grid=(layers,),
+            in_specs=[
+                pl.BlockSpec(
+                    (1, faces, blk, modes_dev),
+                    lambda l, where: (jnp.where(l == 0, where[1], 1 - where[1]), 0, 0, 0),
+                )
+            ],
+            out_specs=pl.BlockSpec((modes, 1, faces, group, blk), lambda l, where: (0, l, 0, 0, 0)),
+        ),
+        out_shape=pieces,
+        compiler_params=pltpu.CompilerParams(vmem_limit_bytes=60 * MIB),
+        cost_estimate=pl.CostEstimate(flops=0, bytes_accessed=2 * MIB, transcendentals=0),
+    )(where, source_field)
     got = lax.all_to_all(sent, "mode", 0, 0, tiled=True)
     weights = prepare(
         where, mean_operator, field_operators, adjacency, mode_masks, modes_dev, bits
@@ -261,43 +297,61 @@
     sigma = THETA / DELTA
     rho = 1.0 / sigma
     d, r = [v / THETA for v in b], b
-    x = d
     flops = 2 * rows * blk * blk * 3 * (bits + 1) * faces
     for step in range(DEGREE):
         last = step == DEGREE - 1
         halo = [lax.ppermute(d[l], AXES, links[l]) for l in range(layers)]
-        acc = call(
-            functools.partial(local_kernel, group),
-            [layer, layer],
-            [*d, dh, dl, ch, cl],
+        pre0, pre1, *x_next = call(
+            functools.partial(local_kernel, group, step > 0),
+            [layer] * (4 if step else 2),
+            [*d, *r, *(x if step else []), dh, dl, ch, cl],
             flops=10 * flops,
         )
+        pre = [pre0, pre1]
+        x = x_next if step else d
         rho_new = 1.0 / (2.0 * sigma - rho)
         coef = (rho_new * rho, 2.0 * rho_new / DELTA)
         rho = rho_new
-        fresh = []
-        for l in range(layers):
-            gather = l == layers - 1 and step >= DEGREE - 2
-            args = [halo[l], acc[l], d[l], r[l]] + ([] if last else [x[l]])
-            args += [fresh[0][-1]] if gather else []
-            fresh.append(
-                call(
-                    functools.partial(finish_kernel, group, coef, l, last, gather),
-                    [layer] * (0 if last else 2) + [pieces if gather else layer],
-                    args + [hh, hl],
-                    flops=2 * flops,
+        if not last:
+            fresh = []
+            for l in range(layers):
+                if fresh:
+                    pre[l], _ = lax.optimization_barrier((pre[l], fresh[0][1]))
+                fresh.append(
+                    call(
+                        functools.partial(finish_kernel, group, coef, l),
+                        [layer, layer],
+                        [halo[l], pre[l], hh, hl, d[l]],
+                        flops=2 * flops,
+                    )
                 )
-            )
-        if last:
-            r_back = lax.all_to_all(fresh[-1][-1], "mode", 0, 0, tiled=True)
-        else:
-            r, d, x = zip(*fresh)
-            if step == DEGREE - 2:
-                x_back = lax.all_to_all(x[-1], "mode", 0, 0, tiled=True)
+            r, d = zip(*fresh)
+    both = (modes, 2) + pieces.shape[1:]
+    (send,) = call(
+        functools.partial(last_kernel, group),
+        [shape(both)],
+        [*halo, *pre, *x, hh, hl],
+        flops=4 * flops,
+        limit=12,
+        out_space=pltpu.HBM,
+        scratch=[pltpu.VMEM(both, F32), pltpu.SemaphoreType.DMA((2, layers))],
+    )
+    back = lax.all_to_all(send, "mode", 0, 0, tiled=True)
     field = shape(source_field.shape)
-    (x_end,) = call(join_kernel, [field], [where, x_back], smem=1, limit=8)
-    (r_end,) = call(join_kernel, [field], [where, r_back], smem=1, limit=8)
-    return x_end, r_end
+    return tuple(
+        call(
+            join_kernel,
+            [field, field],
+            [where, back],
+            smem=1,
+            limit=12,
+            out_space=pltpu.HBM,
+            scratch=[
+                pltpu.VMEM((2,) + source_field.shape, F32),
+                pltpu.SemaphoreType.DMA((2, layers)),
+            ],
+        )
+    )
 
 
 def solution(mesh):

time: 154 us -> 144 us (0.935)
  blocking collectives: 0 us -> 41.2 us
  local copies, waits for them, and re-layouts: 26 us -> 5.37 us
  waiting for transfers between devices: 27.7 us -> 8.7 us
  starting transfers between devices: 42.5 us -> 27.9 us
  Pallas kernels: 56.2 us -> 58.5 us
    all_to_all x0 -> x1, blocking collectives: none -> 41.2 us  [per_device(): back = lax.all_to_all(send, 'mode', 0, 0, tiled=True)]
    unnamed x48 -> x16, local copies, waits for them, and re-layouts: 24.5 us -> 5.22 us
    all_to_all x2 -> x0, starting transfers between devices: 16.2 us -> none  [the longest x1 8.14 us: per_device(): x_back = lax.all_to_all(x[-1], 'mode', 0, 0, tiled=True)]
    all_to_all x2 -> x0, waiting for transfers between devices: 14.7 us -> none  [the longest x1 14.7 us: per_device(): r_back = lax.all_to_all(fresh[-1][-1], 'mode', 0, 0, tiled=True)]
    ppermute x8, waiting for transfers between devices: 13 us -> 8.7 us  [per_device(): halo = [lax.ppermute(d[l], AXES, links[l]) for l in range(layers)]]
    pallas_call x15 -> x12, Pallas kernels: 41.1 us -> 37.2 us  [call(): pl.pallas_call(body, out_shape=outs, in_specs=[pl.BlockSpec(memory_space=...]
    pallas_call x1, Pallas kernels: 15.1 us -> 18.4 us  [prepare(): pl.pallas_call(prepare_kernel, grid_spec=grid_spec, out_shape=[dense] * 2...]
    pallas_call x0 -> x1, Pallas kernels: none -> 2.94 us  [per_device(): pl.pallas_call(split_kernel, grid_spec=pltpu.PrefetchScalarGridSpec(num_s...]
  transfers between devices with their start and end apart: 11 -> 9, of which waited for: 5 -> 4; matrix products, arithmetic and copies ran while one was open for 0% -> 0% of each run, Pallas kernels for 33% -> 35%
where the time goes in v2:
time: 144 us; the launch traced here: 143 us
  Pallas kernels  58.5 us (41%)
  blocking collectives  41.2 us (29%)
  starting transfers between devices  27.9 us (19%)
  waiting for transfers between devices  8.7 us (6%)
  local copies, waits for them, and re-layouts  5.37 us (4%)
    all_to_all x1, blocking collectives, per_device(): back = lax.all_to_all(send, 'mode', 0, 0, tiled=True)  41.2 us
    pallas_call x12, Pallas kernels, call(): pl.pallas_call(body, out_shape=outs, in_specs=[pl.BlockSpec(memory_space=...  37.2 us
    ppermute x8, starting transfers between devices, per_device(): halo = [lax.ppermute(d[l], AXES, links[l]) for l in range(layers)]  18.6 us
    pallas_call x1, Pallas kernels, prepare(): pl.pallas_call(prepare_kernel, grid_spec=grid_spec, out_shape=[dense] * 2...  18.4 us
    all_to_all x1, starting transfers between devices, per_device(): got = lax.all_to_all(sent, 'mode', 0, 0, tiled=True)  9.29 us
    ppermute x8, waiting for transfers between devices, per_device(): halo = [lax.ppermute(d[l], AXES, links[l]) for l in range(layers)]  8.7 us
    unnamed x16, local copies, waits for them, and re-layouts  5.22 us
    pallas_call x1, Pallas kernels, per_device(): pl.pallas_call(split_kernel, grid_spec=pltpu.PrefetchScalarGridSpec(num_s...  2.94 us
  transfers between devices with their start and end apart: 9, of which 4 were waited for; matrix products, arithmetic and copies ran while one was open for 0% of the time, Pallas kernels for 35%

profile of v2, /device:TPU:1, one launch (start us, length us, event | category | flops | bytes accessed | tf_op | source)
XLA Modules:
  0.0 143.4 jit_solution(3439120527386233113)
XLA Ops:
  0.6 0.6 pad_add_fusion.where_ref
  1.2 2.9 %shard_map.68 = f32[16,2,4,16,128]{4,3,2,1,0:T(8,128)} custom-call(s32[2]{0:T(128)} %pad_add_fusion.where_ref, f32[2,4,128,256]{3,2,1,0:T(8,128)} %field_ref.2), custom_call_target="tpu_custom_call" | custom-call | bytes 2097152 | tf_op jit(solution)/shard_map/pallas_call | solution.py:271
  4.2 9.3 %all-to-all-start = ((f32[16,2,4,16,128]{4,3,2,1,0:T(8,128)}), f32[16,2,4,16,128]{4,3,2,1,0:T(8,128)S(1)}, u32[]{:S(2)}, u32[]{:S(2)}) async-start(f32[16,2,4,16,128]{4,3,2,1,0:T(8,128)} %shard_map.68), calls=%async_computation | async-start | bytes 2097152 | tf_op jit(solution)/shard_map/all_to_all | solution.py:288
  13.5 18.4 %shard_map.69 = (bf16[2,5,512,512]{3,2,1,0:T(8,128)(2,1)}, bf16[2,5,512,512]{3,2,1,0:T(8,128)(2,1)}, bf16[2,5,4,128,128]{4,3,2,1,0:T(8,128)(2,1)}, bf16[2,5,4,12...) custom-call(s32[4]{0:T(128)} %masks_ref.1, ...), custom_call_target="tpu_custom_call" | custom-call | flops 100000000 | bytes 37748736 | tf_op jit(solution)/shard_map/pallas_call | solution.py:239
  31.9 0.0 all-to-all-done
  31.9 0.0 copy-start.6
  31.9 0.0 copy-start.7
  31.9 0.1 slice_bitcast_fusion
  32.1 0.4 collective-permute-start
  32.5 0.0 copy-start
  32.6 0.0 copy-start.1
  32.6 0.8 collective-permute-start.2
  33.4 0.0 copy-done.6
  33.4 0.2 copy-done.7
  33.6 0.0 copy-start.3
  33.6 2.5 %copy-done.3 = bf16[2,5,512,512]{3,2,1,0:T(8,128)(2,1)S(1)} copy-done((bf16[2,5,512,512]{3,2,1,0:T(8,128)(2,1)S(1)}, bf16[2,5,512,512]{3,2,1,0:T(8,128)(2,1)}, u32[]{:S(2)}) %copy-start.3) | copy-done | bytes 5242904
  36.1 0.0 copy-start.5
  36.1 2.5 %copy-done.5 = bf16[2,5,512,512]{3,2,1,0:T(8,128)(2,1)S(1)} copy-done((bf16[2,5,512,512]{3,2,1,0:T(8,128)(2,1)S(1)}, bf16[2,5,512,512]{3,2,1,0:T(8,128)(2,1)}, u32[]{:S(2)}) %copy-start.5) | copy-done | bytes 5242904
  38.6 6.3 %shard_map.70 = (f32[4,256,128]{2,1,0:T(8,128)S(1)}, f32[4,256,128]{2,1,0:T(8,128)S(1)}) custom-call(f32[4,256,128]{2,1,0:T(8,128)S(1)} %bitcast.13, f32[4,256,128]{2,1,0:T(8,128)S(1)} %bitcast.18, f32[4,256,128]{2,1,0:T(8,128)S(1)} %bitcast.14, f32[4,256,128]{2,1,0:T(8,128)S(1)} %bitcast.19, bf16[2,5,512,512]{3,2,1,0:T(8,128)(2,1)S(1)} %copy-done.3, ...), custom_call_target="tpu_custom_call" | custom-call | flops 5033164800 | bytes 16252928 | tf_op jit(solution)/shard_map/pallas_call | solution.py:195
  44.9 0.7 collective-permute-done.halo_ref
  45.6 0.0 copy-done
  45.6 0.0 copy-done.1
  45.6 0.0 copy-start.4
  45.6 1.2 shard_map.71
  46.8 4.6 %collective-permute-start.1 = (f32[4,256,128]{2,1,0:T(8,128)S(1)}, f32[4,256,128]{2,1,0:T(8,128)S(1)}, u32[]{:S(2)}, u32[]{:S(2)}) collective-permute-start(f32[4,256,128]{2,1,0:T(8,128)S(1)} %get-tuple-element.58.refs_0_.d_ref), channel_id=1, source_target_pairs={{0,16},{1,17},{2,18},{3,19},{4,20},{5,21},{6,22},{7,23},{8,24},{9,... | collective-permute-start | bytes 1572872 | tf_op jit(solution)/shard_map/ppermute | solution.py:303
  51.4 0.0 collective-permute-done.2.halo_ref
  51.4 1.2 shard_map.72
  52.6 0.9 collective-permute-start.4
  53.5 0.0 copy-done.4
  53.5 6.3 %shard_map.73 = (f32[4,256,128]{2,1,0:T(8,128)S(1)}, f32[4,256,128]{2,1,0:T(8,128)S(1)}, f32[4,256,128]{2,1,0:T(8,128)S(1)}, f32[4,256,128]{2,1,0:T(8,128)S(1)}) custom-call(f32[4,256,128]{2,1,0:T(8,128)S(1)} %get-tuple-element.58.refs_0_.d_ref, f32[4,256,128]{2,1,0:T(8,128)S(1)} %get-tuple-element.61.refs_1_.d_ref, ...), custom_call_target="tpu_custom_call" | custom-call | flops 5033164800 | bytes 18350080 | tf_op jit(solution)/shard_map/pallas_call | solution.py:195
  59.8 3.0 %collective-permute-done.1.halo_ref = f32[4,256,128]{2,1,0:T(8,128)S(1)} collective-permute-done((f32[4,256,128]{2,1,0:T(8,128)S(1)}, f32[4,256,128]{2,1,0:T(8,128)S(1)}, u32[]{:S(2)}, u32[]{:S(2)}) %collective-permute-start.1) | collective-permute-done | bytes 524320 | tf_op jit(solution)/shard_map/ppermute | solution.py:303
  62.8 1.2 shard_map.74
  64.0 1.2 collective-permute-start.3
  65.2 0.0 collective-permute-done.4.halo_ref
  65.2 1.2 shard_map.75
  66.4 0.9 collective-permute-start.6
  67.3 6.3 %shard_map.76 = (f32[4,256,128]{2,1,0:T(8,128)S(1)}, f32[4,256,128]{2,1,0:T(8,128)S(1)}, f32[4,256,128]{2,1,0:T(8,128)S(1)}, f32[4,256,128]{2,1,0:T(8,128)S(1)}) custom-call(f32[4,256,128]{2,1,0:T(8,128)S(1)} %get-tuple-element.65.refs_0_.d_ref, f32[4,256,128]{2,1,0:T(8,128)S(1)} %get-tuple-element.68.refs_1_.d_ref, ...), custom_call_target="tpu_custom_call" | custom-call | flops 5033164800 | bytes 18350080 | tf_op jit(solution)/shard_map/pallas_call | solution.py:195
  73.6 2.3 %collective-permute-done.3.halo_ref = f32[4,256,128]{2,1,0:T(8,128)S(1)} collective-permute-done((f32[4,256,128]{2,1,0:T(8,128)S(1)}, f32[4,256,128]{2,1,0:T(8,128)S(1)}, u32[]{:S(2)}, u32[]{:S(2)}) %collective-permute-start.3) | collective-permute-done | bytes 524320 | tf_op jit(solution)/shard_map/ppermute | solution.py:303
  76.0 1.2 shard_map.77
  77.1 0.0 collective-permute-done.6.halo_ref
  77.2 1.2 shard_map.78
  78.4 0.7 collective-permute-start.7
  79.1 9.1 %collective-permute-start.5 = (f32[4,256,128]{2,1,0:T(8,128)S(1)}, f32[4,256,128]{2,1,0:T(8,128)S(1)}, u32[]{:S(2)}, u32[]{:S(2)}) collective-permute-start(f32[4,256,128]{2,1,0:T(8,128)S(1)} %get-tuple-element.74.refs_0_), channel_id=1, source_target_pairs={{0,16},{1,17},{2,18},{3,19},{4,20},{5,21},{6,22},{7,23},{8,24},{9,... | collective-permute-start | bytes 1572872 | tf_op jit(solution)/shard_map/ppermute | solution.py:303
  88.1 6.3 %shard_map.79 = (f32[4,256,128]{2,1,0:T(8,128)S(1)}, f32[4,256,128]{2,1,0:T(8,128)S(1)}, f32[4,256,128]{2,1,0:T(8,128)S(1)}, f32[4,256,128]{2,1,0:T(8,128)S(1)}) custom-call(f32[4,256,128]{2,1,0:T(8,128)S(1)} %get-tuple-element.74.refs_0_, f32[4,256,128]{2,1,0:T(8,128)S(1)} %get-tuple-element.77.refs_1_, f32[4,256,128]{2,1,0:T(8,128)S(1)} %get-tuple-element.78.refs_2_, ...), custom_call_target="tpu_custom_call" | custom-call | flops 5033164800 | bytes 18350080 | tf_op jit(solution)/shard_map/pallas_call | solution.py:195
  94.5 0.0 collective-permute-done.7.halo1_ref
  94.5 2.7 %collective-permute-done.5.halo0_ref = f32[4,256,128]{2,1,0:T(8,128)S(1)} collective-permute-done((f32[4,256,128]{2,1,0:T(8,128)S(1)}, f32[4,256,128]{2,1,0:T(8,128)S(1)}, u32[]{:S(2)}, u32[]{:S(2)}) %collective-permute-start.5) | collective-permute-done | bytes 524320 | tf_op jit(solution)/shard_map/ppermute | solution.py:303
  97.2 2.6 %shard_map.80 = f32[16,2,2,4,16,128]{5,4,3,2,1,0:T(8,128)S(1)} custom-call(f32[4,256,128]{2,1,0:T(8,128)S(1)} %collective-permute-done.5.halo0_ref, f32[4,256,128]{2,1,0:T(8,128)S(1)} %collective-permute-done.7.halo1_ref, f32[4,256,128]{2,1,0:T(8,128)S(1)} %get-tuple-element.82.pre0_ref, f32[4,256,128]{2,1,0:T(8,128)S(1)} %get-tuple-element.83.pre1_ref, ...), custom_call_target="tpu_custom_call" | custom-call | flops 2013265920 | bytes 7864320 | tf_op jit(solution)/shard_map/pallas_call | solution.py:195
  99.8 0.0 copy-start.2
  99.8 41.2 %all_to_all.10.in_ref = f32[16,2,2,4,16,128]{5,4,3,2,1,0:T(8,128)S(1)} all-to-all(f32[16,2,2,4,16,128]{5,4,3,2,1,0:T(8,128)S(1)} %shard_map.80), channel_id=1, replica_groups=mesh['space'=8,'mode'=16] {'mode'}, dimensions={0} | all-to-all | bytes 4194304 | tf_op jit(solution)/shard_map/all_to_all | solution.py:339
  141.1 0.0 copy-done.2
  141.1 2.1 %shard_map.81 = (f32[2,4,128,256]{3,2,1,0:T(8,128)}, f32[2,4,128,256]{3,2,1,0:T(8,128)}) custom-call(s32[2]{0:T(128)S(1)} %copy-done.2, f32[16,2,2,4,16,128]{5,4,3,2,1,0:T(8,128)S(1)} %all_to_all.10.in_ref), custom_call_target="tpu_custom_call" | custom-call | bytes 4194312 | tf_op jit(solution)/shard_map/pallas_call | solution.py:195
  (2 shorter events, 0.1 us)
Async XLA Ops:
  4.2 27.7 %all-to-all-start = ((f32[16,2,4,16,128]{4,3,2,1,0:T(8,128)}), f32[16,2,4,16,128]{4,3,2,1,0:T(8,128)S(1)}, u32[]{:S(2)}, u32[]{:S(2)}) async-start(f32[16,2,4,16,128]{4,3,2,1,0:T(8,128)} %shard_map.68), calls=%async_computation | async-start | bytes 2097152 | tf_op jit(solution)/shard_map/all_to_all | solution.py:288
  31.9 1.5 %copy-start.6 = (bf16[2,5,4,128,128]{4,3,2,1,0:T(8,128)(2,1)S(1)}, bf16[2,5,4,128,128]{4,3,2,1,0:T(8,128)(2,1)}, u32[]{:S(2)}) copy-start(bf16[2,5,4,128,128]{4,3,2,1,0:T(8,128)(2,1)} %get-tuple-element.53.refs_6_.refs_8_) | copy-start | bytes 3932164
  31.9 1.7 %copy-start.7 = (bf16[2,5,4,128,128]{4,3,2,1,0:T(8,128)(2,1)S(1)}, bf16[2,5,4,128,128]{4,3,2,1,0:T(8,128)(2,1)}, u32[]{:S(2)}) copy-start(bf16[2,5,4,128,128]{4,3,2,1,0:T(8,128)(2,1)} %get-tuple-element.54.refs_7_.refs_9_) | copy-start | bytes 3932164
  32.1 13.6 %collective-permute-start = (f32[4,256,128]{2,1,0:T(8,128)S(1)}, f32[4,256,128]{2,1,0:T(8,128)S(1)}, u32[]{:S(2)}, u32[]{:S(2)}) collective-permute-start(f32[4,256,128]{2,1,0:T(8,128)S(1)} %bitcast.12), channel_id=1, source_target_pairs={{0,16},{1,17},{2,18},{3,19},{4,20},{5,21},{6,22},{7,23},{8,24},{9,... | collective-permute-start | bytes 1572872 | tf_op jit(solution)/shard_map/ppermute | solution.py:303
  32.5 13.1 %copy-start = (bf16[2,5,4,128,128]{4,3,2,1,0:T(8,128)(2,1)S(1)}, bf16[2,5,4,128,128]{4,3,2,1,0:T(8,128)(2,1)}, u32[]{:S(2)}) copy-start(bf16[2,5,4,128,128]{4,3,2,1,0:T(8,128)(2,1)} %get-tuple-element.56.hh_ref) | copy-start | bytes 3932164
  32.6 13.1 %copy-start.1 = (bf16[2,5,4,128,128]{4,3,2,1,0:T(8,128)(2,1)S(1)}, bf16[2,5,4,128,128]{4,3,2,1,0:T(8,128)(2,1)}, u32[]{:S(2)}) copy-start(bf16[2,5,4,128,128]{4,3,2,1,0:T(8,128)(2,1)} %get-tuple-element.57.hl_ref) | copy-start | bytes 3932164
  32.6 18.8 %collective-permute-start.2 = (f32[4,256,128]{2,1,0:T(8,128)S(1)}, f32[4,256,128]{2,1,0:T(8,128)S(1)}, u32[]{:S(2)}, u32[]{:S(2)}) collective-permute-start(f32[4,256,128]{2,1,0:T(8,128)S(1)} %bitcast.17), channel_id=1, source_target_pairs={{16,40},{17,41},{18,42},{19,43},{20,44},{21,45},{22,46},{23,47},{2... | collective-permute-start | bytes 1572872 | tf_op jit(solution)/shard_map/ppermute | solution.py:303
  33.6 2.5 %copy-start.3 = (bf16[2,5,512,512]{3,2,1,0:T(8,128)(2,1)S(1)}, bf16[2,5,512,512]{3,2,1,0:T(8,128)(2,1)}, u32[]{:S(2)}) copy-start(bf16[2,5,512,512]{3,2,1,0:T(8,128)(2,1)} %get-tuple-element.51.refs_4_.refs_6_) | copy-start | bytes 15728644
  36.1 2.5 %copy-start.5 = (bf16[2,5,512,512]{3,2,1,0:T(8,128)(2,1)S(1)}, bf16[2,5,512,512]{3,2,1,0:T(8,128)(2,1)}, u32[]{:S(2)}) copy-start(bf16[2,5,512,512]{3,2,1,0:T(8,128)(2,1)} %get-tuple-element.52.refs_5_.refs_7_) | copy-start | bytes 15728644
  45.6 7.8 %copy-start.4 = (bf16[2,5,512,512]{3,2,1,0:T(8,128)(2,1)S(1)}, bf16[2,5,512,512]{3,2,1,0:T(8,128)(2,1)}, u32[]{:S(2)}) copy-start(bf16[2,5,512,512]{3,2,1,0:T(8,128)(2,1)} %get-tuple-element.51.refs_4_.refs_6_) | copy-start | bytes 15728644
  46.8 15.9 %collective-permute-start.1 = (f32[4,256,128]{2,1,0:T(8,128)S(1)}, f32[4,256,128]{2,1,0:T(8,128)S(1)}, u32[]{:S(2)}, u32[]{:S(2)}) collective-permute-start(f32[4,256,128]{2,1,0:T(8,128)S(1)} %get-tuple-element.58.refs_0_.d_ref), channel_id=1, source_target_pairs={{0,16},{1,17},{2,18},{3,19},{4,20},{5,21},{6,22},{7,23},{8,24},{9,... | collective-permute-start | bytes 1572872 | tf_op jit(solution)/shard_map/ppermute | solution.py:303
  52.6 12.6 %collective-permute-start.4 = (f32[4,256,128]{2,1,0:T(8,128)S(1)}, f32[4,256,128]{2,1,0:T(8,128)S(1)}, u32[]{:S(2)}, u32[]{:S(2)}) collective-permute-start(f32[4,256,128]{2,1,0:T(8,128)S(1)} %get-tuple-element.61.refs_1_.d_ref), channel_id=1, source_target_pairs={{16,40},{17,41},{18,42},{19,43},{20,44},{21,45},{22,46},{23,47},{2... | collective-permute-start | bytes 1572872 | tf_op jit(solution)/shard_map/ppermute | solution.py:303
  64.0 12.0 %collective-permute-start.3 = (f32[4,256,128]{2,1,0:T(8,128)S(1)}, f32[4,256,128]{2,1,0:T(8,128)S(1)}, u32[]{:S(2)}, u32[]{:S(2)}) collective-permute-start(f32[4,256,128]{2,1,0:T(8,128)S(1)} %get-tuple-element.65.refs_0_.d_ref), channel_id=1, source_target_pairs={{0,16},{1,17},{2,18},{3,19},{4,20},{5,21},{6,22},{7,23},{8,24},{9,... | collective-permute-start | bytes 1572872 | tf_op jit(solution)/shard_map/ppermute | solution.py:303
  66.4 10.8 %collective-permute-start.6 = (f32[4,256,128]{2,1,0:T(8,128)S(1)}, f32[4,256,128]{2,1,0:T(8,128)S(1)}, u32[]{:S(2)}, u32[]{:S(2)}) collective-permute-start(f32[4,256,128]{2,1,0:T(8,128)S(1)} %get-tuple-element.68.refs_1_.d_ref), channel_id=1, source_target_pairs={{16,40},{17,41},{18,42},{19,43},{20,44},{21,45},{22,46},{23,47},{2... | collective-permute-start | bytes 1572872 | tf_op jit(solution)/shard_map/ppermute | solution.py:303
  78.4 16.1 %collective-permute-start.7 = (f32[4,256,128]{2,1,0:T(8,128)S(1)}, f32[4,256,128]{2,1,0:T(8,128)S(1)}, u32[]{:S(2)}, u32[]{:S(2)}) collective-permute-start(f32[4,256,128]{2,1,0:T(8,128)S(1)} %get-tuple-element.77.refs_1_), channel_id=1, source_target_pairs={{16,40},{17,41},{18,42},{19,43},{20,44},{21,45},{22,46},{23,47},{2... | collective-permute-start | bytes 1572872 | tf_op jit(solution)/shard_map/ppermute | solution.py:303
  79.1 18.1 %collective-permute-start.5 = (f32[4,256,128]{2,1,0:T(8,128)S(1)}, f32[4,256,128]{2,1,0:T(8,128)S(1)}, u32[]{:S(2)}, u32[]{:S(2)}) collective-permute-start(f32[4,256,128]{2,1,0:T(8,128)S(1)} %get-tuple-element.74.refs_0_), channel_id=1, source_target_pairs={{0,16},{1,17},{2,18},{3,19},{4,20},{5,21},{6,22},{7,23},{8,24},{9,... | collective-permute-start | bytes 1572872 | tf_op jit(solution)/shard_map/ppermute | solution.py:303
  99.8 41.2 %copy-start.2 = (s32[2]{0:T(128)S(1)}, s32[2]{0:T(128)}, u32[]{:S(2)}) copy-start(s32[2]{0:T(128)} %pad_add_fusion.where_ref) | copy-start | bytes 28

commit v3 on v2

--- a/solution.py
+++ b/solution.py
@@ -38,23 +38,43 @@
     return value if op == 0 else swap_rows(value, op - 1, group)
 
 
-def split_kernel(where_ref, field_ref, out_ref):
-    pieces, _, faces, group, blk = out_ref.shape
+def place():
+    slab = lax.axis_index("space").astype(jnp.int32)
+    return lax.shift_right_logical(slab, 1) & 1, 1 - (slab & 1)
+
+
+def split_kernel(field_ref, out_ref, arrived, laid, in_sems, out_sems):
+    pieces, layers, faces, group, blk = out_ref.shape
     half = pieces // 2
-    first = where_ref[0] * half
+    flip, lead = place()
+    first = flip * half
     second = half - first
-    for f in range(faces):
-        rows = field_ref[0, f].T.reshape(pieces, group, blk)
-        out_ref[pl.ds(first, half), 0, f] = rows[:half]
-        out_ref[pl.ds(second, half), 0, f] = rows[half:]
-
-
-def join_kernel(where_ref, in_ref, x_ref, r_ref, buffer, sems):
+    ins, outs = [], []
+    for l in range(layers):
+        at = lead if l == 0 else 1 - lead
+        for f in range(faces):
+            ins.append(
+                pltpu.make_async_copy(field_ref.at[at, f], arrived.at[l, f], in_sems.at[l, f])
+            )
+            ins[-1].start()
+    for l in range(layers):
+        for f in range(faces):
+            ins[l * faces + f].wait()
+            rows = arrived[l, f].T.reshape(pieces, group, blk)
+            laid[pl.ds(first, half), l, f] = rows[:half]
+            laid[pl.ds(second, half), l, f] = rows[half:]
+        outs.append(pltpu.make_async_copy(laid.at[:, l], out_ref.at[:, l], out_sems.at[l]))
+        outs[-1].start()
+    for copy in outs:
+        copy.wait()
+
+
+def join_kernel(in_ref, x_ref, r_ref, buffer, sems):
     pieces, fields, layers, faces, group, blk = in_ref.shape
     half = pieces // 2
-    first = where_ref[0] * half
+    flip, lead = place()
+    first = flip * half
     second = half - first
-    lead = where_ref[1]
     copies = []
     for k, out_ref in enumerate((x_ref, r_ref)):
         for l in range(layers):
@@ -78,13 +98,13 @@
 
 
 def prepare_kernel(
-    masks_ref, adj_ref, where_ref, mean_ref, field_ref,
+    masks_ref, adj_ref, mean_ref, field_ref,
     dh_ref, dl_ref, hh_ref, hl_ref, ch_ref, cl_ref, dense,
 ):
     spot = pl.program_id(0)
     op = pl.program_id(1)
     faces, blk = mean_ref.shape[1], mean_ref.shape[2]
-    lead = where_ref[1]
+    lead = place()[1]
     layer = jnp.where(spot == 0, lead, 1 - lead)
     halo_at = pl.multiple_of((1 + layer) * blk, blk)
     cross_at = pl.multiple_of((2 - layer) * blk, blk)
@@ -150,36 +170,38 @@
                 x_outs[l][f] = x_refs[l][f] + d_refs[l][f]
 
 
-def finish_kernel(group, coef, layer, halo_ref, pre_ref, hh_ref, hl_ref, d_ref, r_out, d_out):
-    c_d, c_r = coef
+def finish_kernel(group, coef, layer, halo_ref, pre_ref, hh_ref, hl_ref, *rest):
     for f in range(halo_ref.shape[0]):
         residual = pre_ref[f] - off_layer(0.0, halo_ref[f], hh_ref, hl_ref, layer, f, group)
-        r_out[f] = residual
-        d_out[f] = c_d * d_ref[f] + c_r * residual
+        if coef is None:
+            rest[0][f] = residual
+        else:
+            d_ref, r_out, d_out = rest
+            r_out[f] = residual
+            d_out[f] = coef[0] * d_ref[f] + coef[1] * residual
 
 
 def last_kernel(
-    group, halo0_ref, halo1_ref, pre0_ref, pre1_ref, x0_ref, x1_ref, hh_ref, hl_ref,
-    send_ref, buffer, sems,
+    group, halo_ref, pre_ref, r0_ref, x0_ref, x1_ref, hh_ref, hl_ref, send_ref, buffer, sems
 ):
     copies = []
 
-    def send(k, l):
+    def send(k, l, value):
+        for f in range(halo_ref.shape[0]):
+            buffer[:, k, l, f] = value(f).reshape(-1, group, value(f).shape[-1])
         copies.append(
             pltpu.make_async_copy(buffer.at[:, k, l], send_ref.at[:, k, l], sems.at[k, l])
         )
         copies[-1].start()
 
-    faces, _, blk = halo0_ref.shape
-    for l, x_ref in enumerate((x0_ref, x1_ref)):
-        for f in range(faces):
-            buffer[:, 0, l, f] = x_ref[f].reshape(-1, group, blk)
-        send(0, l)
-    for l, (halo_ref, pre_ref) in enumerate(((halo0_ref, pre0_ref), (halo1_ref, pre1_ref))):
-        for f in range(faces):
-            share = off_layer(0.0, halo_ref[f], hh_ref, hl_ref, l, f, group)
-            buffer[:, 1, l, f] = (pre_ref[f] - share).reshape(-1, group, blk)
-        send(1, l)
+    send(0, 0, lambda f: x0_ref[f])
+    send(0, 1, lambda f: x1_ref[f])
+    send(1, 0, lambda f: r0_ref[f])
+    ends = [
+        pre_ref[f] - off_layer(0.0, halo_ref[f], hh_ref, hl_ref, 1, f, group)
+        for f in range(halo_ref.shape[0])
+    ]
+    send(1, 1, lambda f: ends[f])
     for copy in copies:
         copy.wait()
 
@@ -187,15 +209,16 @@
 MIB = 1 << 20
 
 
-def call(body, outs, args, smem=0, flops=0, limit=6, out_space=pltpu.VMEM, scratch=()):
-    spaces = [pltpu.SMEM] * smem + [pltpu.VMEM] * (len(args) - smem)
+def call(
+    body, outs, args, flops=0, limit=6, in_space=pltpu.VMEM, out_space=pltpu.VMEM, scratch=()
+):
     size = sum(a.size * a.dtype.itemsize for a in args) + sum(
         o.size * o.dtype.itemsize for o in outs
     )
     return pl.pallas_call(
         body,
         out_shape=outs,
-        in_specs=[pl.BlockSpec(memory_space=s) for s in spaces],
+        in_specs=[pl.BlockSpec(memory_space=in_space) for _ in args],
         out_specs=[pl.BlockSpec(memory_space=out_space) for _ in outs],
         scratch_shapes=list(scratch),
         compiler_params=pltpu.CompilerParams(vmem_limit_bytes=limit * MIB),
@@ -207,28 +230,27 @@
     return jax.ShapeDtypeStruct(tuple(dims), dtype)
 
 
-def prepare(where, mean_operator, field_operators, adjacency, mode_masks, modes_dev, bits):
+def prepare(mean_operator, field_operators, adjacency, mode_masks, modes_dev, bits):
     layers, faces, blk, wide = mean_operator.shape
     ops = bits + 1
     full = faces * blk
 
-    def layer_of(spot, where):
-        return jnp.where(spot == 0, where[1], 1 - where[1])
+    def layer_of(spot):
+        lead = place()[1]
+        return jnp.where(spot == 0, lead, 1 - lead)
 
     dense_spec = pl.BlockSpec((1, 1, full, full), lambda l, op, *_: (l, op, 0, 0))
     side_spec = pl.BlockSpec((1, 1, faces, blk, blk), lambda l, op, *_: (l, op, 0, 0, 0))
     grid_spec = pltpu.PrefetchScalarGridSpec(
-        num_scalar_prefetch=3,
+        num_scalar_prefetch=2,
         grid=(layers, ops),
         in_specs=[
             pl.BlockSpec(
-                (1, faces, blk, wide), lambda l, op, masks, adj, where: (layer_of(l, where), 0, 0, 0)
+                (1, faces, blk, wide), lambda l, op, masks, adj: (layer_of(l), 0, 0, 0)
             ),
             pl.BlockSpec(
                 (1, 1, faces, blk, wide),
-                lambda l, op, masks, adj, where: (
-                    field_of(masks, op, modes_dev), layer_of(l, where), 0, 0, 0,
-                ),
+                lambda l, op, masks, adj: (field_of(masks, op, modes_dev), layer_of(l), 0, 0, 0),
             ),
         ],
         out_specs=[dense_spec] * 2 + [side_spec] * 4,
@@ -242,7 +264,7 @@
         out_shape=[dense] * 2 + [side] * 4,
         compiler_params=pltpu.CompilerParams(vmem_limit_bytes=56 * MIB),
         cost_estimate=pl.CostEstimate(flops=10**8, bytes_accessed=36 * MIB, transcendentals=0),
-    )(mode_masks, adjacency, where, mean_operator, field_operators)
+    )(mode_masks, adjacency, mean_operator, field_operators)
 
 
 def pair_list(count, modes, inner):
@@ -262,32 +284,26 @@
     bits = modes.bit_length() - 1
     group = modes_dev // modes
     rows = modes * group
-    slab = lax.axis_index("space").astype(jnp.int32)
-    flip = lax.shift_right_logical(slab, 1) & 1
-    where = jnp.stack([flip, 1 - (slab & 1)])
     pieces = shape((modes, layers, faces, group, blk))
     layer = shape((faces, rows, blk))
 
-    sent = pl.pallas_call(
+    (sent,) = call(
         split_kernel,
-        grid_spec=pltpu.PrefetchScalarGridSpec(
-            num_scalar_prefetch=1,
-            grid=(layers,),
-            in_specs=[
-                pl.BlockSpec(
-                    (1, faces, blk, modes_dev),
-                    lambda l, where: (jnp.where(l == 0, where[1], 1 - where[1]), 0, 0, 0),
-                )
-            ],
-            out_specs=pl.BlockSpec((modes, 1, faces, group, blk), lambda l, where: (0, l, 0, 0, 0)),
-        ),
-        out_shape=pieces,
-        compiler_params=pltpu.CompilerParams(vmem_limit_bytes=60 * MIB),
-        cost_estimate=pl.CostEstimate(flops=0, bytes_accessed=2 * MIB, transcendentals=0),
-    )(where, source_field)
+        [pieces],
+        [source_field],
+        limit=60,
+        in_space=pltpu.HBM,
+        out_space=pltpu.HBM,
+        scratch=[
+            pltpu.VMEM(source_field.shape, F32),
+            pltpu.VMEM(pieces.shape, F32),
+            pltpu.SemaphoreType.DMA((layers, faces)),
+            pltpu.SemaphoreType.DMA((layers,)),
+        ],
+    )
     got = lax.all_to_all(sent, "mode", 0, 0, tiled=True)
     weights = prepare(
-        where, mean_operator, field_operators, adjacency, mode_masks, modes_dev, bits
+        mean_operator, field_operators, adjacency, mode_masks, modes_dev, bits
     )
     got, *weights = lax.optimization_barrier((got, *weights))
     dh, dl, hh, hl, ch, cl = weights
@@ -305,7 +321,6 @@
             functools.partial(local_kernel, group, step > 0),
             [layer] * (4 if step else 2),
             [*d, *r, *(x if step else []), dh, dl, ch, cl],
-            flops=10 * flops,
         )
         pre = [pre0, pre1]
         x = x_next if step else d
@@ -322,16 +337,17 @@
                         functools.partial(finish_kernel, group, coef, l),
                         [layer, layer],
                         [halo[l], pre[l], hh, hl, d[l]],
-                        flops=2 * flops,
                     )
                 )
             r, d = zip(*fresh)
+    (r_end,) = call(
+        functools.partial(finish_kernel, group, None, 0), [layer], [halo[0], pre[0], hh, hl]
+    )
     both = (modes, 2) + pieces.shape[1:]
     (send,) = call(
         functools.partial(last_kernel, group),
         [shape(both)],
-        [*halo, *pre, *x, hh, hl],
-        flops=4 * flops,
+        [halo[1], pre[1], r_end, *x, hh, hl],
         limit=12,
         out_space=pltpu.HBM,
         scratch=[pltpu.VMEM(both, F32), pltpu.SemaphoreType.DMA((2, layers))],
@@ -342,8 +358,7 @@
         call(
             join_kernel,
             [field, field],
-            [where, back],
-            smem=1,
+            [back],
             limit=12,
             out_space=pltpu.HBM,
             scratch=[

time: 144 us -> 140 us (0.972)
  the two profiles are of different devices: /device:TPU:1 before, /device:TPU:8 now
where the time goes in v3:
time: 140 us; the launch traced here: 139 us
  Pallas kernels  57.8 us (41%)
  blocking collectives  33.4 us (24%)
  starting transfers between devices  27 us (19%)
  waiting for transfers between devices  14.6 us (10%)
  local copies, waits for them, and re-layouts  5.14 us (4%)
    pallas_call x14, Pallas kernels, call(): pl.pallas_call(body, out_shape=outs, in_specs=[pl.BlockSpec(memory_space=...  39.3 us
    all_to_all x1, blocking collectives, per_device(): back = lax.all_to_all(send, 'mode', 0, 0, tiled=True)  33.4 us
    ppermute x8, starting transfers between devices, per_device(): halo = [lax.ppermute(d[l], AXES, links[l]) for l in range(layers)]  19.2 us
    pallas_call x1, Pallas kernels, prepare(): pl.pallas_call(prepare_kernel, grid_spec=grid_spec, out_shape=[dense] * 2...  18.5 us
    ppermute x8, waiting for transfers between devices, per_device(): halo = [lax.ppermute(d[l], AXES, links[l]) for l in range(layers)]  14.6 us
    all_to_all x1, starting transfers between devices, per_device(): got = lax.all_to_all(sent, 'mode', 0, 0, tiled=True)  7.89 us
    unnamed x14, local copies, waits for them, and re-layouts  4.99 us
  transfers between devices with their start and end apart: 9, of which 4 were waited for; matrix products, arithmetic and copies ran while one was open for 0% of the time, Pallas kernels for 37%

profile of v3, /device:TPU:8, one launch (start us, length us, event | category | flops | bytes accessed | tf_op | source)
XLA Modules:
  0.0 139.0 jit_solution(9302248595505194587)
XLA Ops:
  0.6 2.6 %shard_map.68 = f32[16,2,4,16,128]{4,3,2,1,0:T(8,128)} custom-call(f32[2,4,128,256]{3,2,1,0:T(8,128)} %field_ref.2), custom_call_target="tpu_custom_call" | custom-call | bytes 2097152 | tf_op jit(solution)/shard_map/pallas_call | solution.py:218
  3.2 7.9 %all-to-all-start = ((f32[16,2,4,16,128]{4,3,2,1,0:T(8,128)}), f32[16,2,4,16,128]{4,3,2,1,0:T(8,128)S(1)}, u32[]{:S(2)}, u32[]{:S(2)}) async-start(f32[16,2,4,16,128]{4,3,2,1,0:T(8,128)} %shard_map.68), calls=%async_computation | async-start | bytes 2097152 | tf_op jit(solution)/shard_map/all_to_all | solution.py:304
  11.1 18.5 %shard_map.69 = (bf16[2,5,512,512]{3,2,1,0:T(8,128)(2,1)}, bf16[2,5,512,512]{3,2,1,0:T(8,128)(2,1)}, bf16[2,5,4,128,128]{4,3,2,1,0:T(8,128)(2,1)}, bf16[2,5,4,12...) custom-call(s32[4]{0:T(128)} %masks_ref.1, ...), custom_call_target="tpu_custom_call" | custom-call | flops 100000000 | bytes 37748736 | tf_op jit(solution)/shard_map/pallas_call | solution.py:261
  29.6 0.0 all-to-all-done
  29.6 0.0 copy-start.5
  29.6 0.0 copy-start.6
  29.6 0.1 slice_bitcast_fusion
  29.8 0.7 collective-permute-start.1
  30.5 0.0 copy-start
  30.5 0.0 copy-start.1
  30.5 5.3 %collective-permute-start = (f32[4,256,128]{2,1,0:T(8,128)S(1)}, f32[4,256,128]{2,1,0:T(8,128)S(1)}, u32[]{:S(2)}, u32[]{:S(2)}) collective-permute-start(f32[4,256,128]{2,1,0:T(8,128)S(1)} %bitcast.15), channel_id=1, source_target_pairs={{16,40},{17,41},{18,42},{19,43},{20,44},{21,45},{22,46},{23,47},{2... | collective-permute-start | bytes 1572872 | tf_op jit(solution)/shard_map/ppermute | solution.py:319
  35.8 0.0 copy-done.5
  35.8 0.0 copy-done.6
  35.9 0.0 copy-start.2
  35.9 2.5 %copy-done.2 = bf16[2,5,512,512]{3,2,1,0:T(8,128)(2,1)S(1)} copy-done((bf16[2,5,512,512]{3,2,1,0:T(8,128)(2,1)S(1)}, bf16[2,5,512,512]{3,2,1,0:T(8,128)(2,1)}, u32[]{:S(2)}) %copy-start.2) | copy-done | bytes 5242904
  38.3 0.0 copy-start.4
  38.3 2.5 %copy-done.4 = bf16[2,5,512,512]{3,2,1,0:T(8,128)(2,1)S(1)} copy-done((bf16[2,5,512,512]{3,2,1,0:T(8,128)(2,1)S(1)}, bf16[2,5,512,512]{3,2,1,0:T(8,128)(2,1)}, u32[]{:S(2)}) %copy-start.4) | copy-done | bytes 5242904
  40.8 6.3 %shard_map.70 = (f32[4,256,128]{2,1,0:T(8,128)S(1)}, f32[4,256,128]{2,1,0:T(8,128)S(1)}) custom-call(f32[4,256,128]{2,1,0:T(8,128)S(1)} %bitcast.11, f32[4,256,128]{2,1,0:T(8,128)S(1)} %bitcast.16, f32[4,256,128]{2,1,0:T(8,128)S(1)} %bitcast.12, f32[4,256,128]{2,1,0:T(8,128)S(1)} %bitcast.17, bf16[2,5,512,512]{3,2,1,0:T(8,128)(2,1)S(1)} %copy-done.2, ...), custom_call_target="tpu_custom_call" | custom-call | bytes 16252928 | tf_op jit(solution)/shard_map/pallas_call | solution.py:218
  47.2 0.0 collective-permute-done.1.halo_ref
  47.2 0.0 copy-done
  47.2 0.0 copy-done.1
  47.2 0.0 copy-start.3
  47.2 1.2 shard_map.71
  48.4 1.8 %collective-permute-start.3 = (f32[4,256,128]{2,1,0:T(8,128)S(1)}, f32[4,256,128]{2,1,0:T(8,128)S(1)}, u32[]{:S(2)}, u32[]{:S(2)}) collective-permute-start(f32[4,256,128]{2,1,0:T(8,128)S(1)} %get-tuple-element.59.refs_0_.rest_0_), channel_id=1, source_target_pairs={{0,16},{1,17},{2,18},{3,19},{4,20},{5,21},{6,22},{7,23},{8,24},{9,... | collective-permute-start | bytes 1572872 | tf_op jit(solution)/shard_map/ppermute | solution.py:319
  50.2 0.0 collective-permute-done.halo_ref
  50.2 1.2 shard_map.72
  51.4 3.5 %collective-permute-start.2 = (f32[4,256,128]{2,1,0:T(8,128)S(1)}, f32[4,256,128]{2,1,0:T(8,128)S(1)}, u32[]{:S(2)}, u32[]{:S(2)}) collective-permute-start(f32[4,256,128]{2,1,0:T(8,128)S(1)} %get-tuple-element.61.refs_1_.rest_0_), channel_id=1, source_target_pairs={{16,40},{17,41},{18,42},{19,43},{20,44},{21,45},{22,46},{23,47},{2... | collective-permute-start | bytes 1572872 | tf_op jit(solution)/shard_map/ppermute | solution.py:319
  54.9 0.0 copy-done.3
  54.9 6.3 %shard_map.73 = (f32[4,256,128]{2,1,0:T(8,128)S(1)}, f32[4,256,128]{2,1,0:T(8,128)S(1)}, f32[4,256,128]{2,1,0:T(8,128)S(1)}, f32[4,256,128]{2,1,0:T(8,128)S(1)}) custom-call(f32[4,256,128]{2,1,0:T(8,128)S(1)} %get-tuple-element.59.refs_0_.rest_0_, f32[4,256,128]{2,1,0:T(8,128)S(1)} %get-tuple-element.61.refs_1_.rest_0_, ...), custom_call_target="tpu_custom_call" | custom-call | bytes 18350080 | tf_op jit(solution)/shard_map/pallas_call | solution.py:218
  61.3 0.6 collective-permute-done.3.halo_ref
  61.9 1.2 shard_map.74
  63.1 1.8 %collective-permute-start.5 = (f32[4,256,128]{2,1,0:T(8,128)S(1)}, f32[4,256,128]{2,1,0:T(8,128)S(1)}, u32[]{:S(2)}, u32[]{:S(2)}) collective-permute-start(f32[4,256,128]{2,1,0:T(8,128)S(1)} %get-tuple-element.66.refs_0_.rest_0_), channel_id=1, source_target_pairs={{0,16},{1,17},{2,18},{3,19},{4,20},{5,21},{6,22},{7,23},{8,24},{9,... | collective-permute-start | bytes 1572872 | tf_op jit(solution)/shard_map/ppermute | solution.py:319
  64.9 3.7 %collective-permute-done.2.halo_ref = f32[4,256,128]{2,1,0:T(8,128)S(1)} collective-permute-done((f32[4,256,128]{2,1,0:T(8,128)S(1)}, f32[4,256,128]{2,1,0:T(8,128)S(1)}, u32[]{:S(2)}, u32[]{:S(2)}) %collective-permute-start.2) | collective-permute-done | bytes 524320 | tf_op jit(solution)/shard_map/ppermute | solution.py:319
  68.5 1.2 shard_map.75
  69.7 3.0 %collective-permute-start.4 = (f32[4,256,128]{2,1,0:T(8,128)S(1)}, f32[4,256,128]{2,1,0:T(8,128)S(1)}, u32[]{:S(2)}, u32[]{:S(2)}) collective-permute-start(f32[4,256,128]{2,1,0:T(8,128)S(1)} %get-tuple-element.68.refs_1_.rest_0_), channel_id=1, source_target_pairs={{16,40},{17,41},{18,42},{19,43},{20,44},{21,45},{22,46},{23,47},{2... | collective-permute-start | bytes 1572872 | tf_op jit(solution)/shard_map/ppermute | solution.py:319
  72.8 6.3 %shard_map.76 = (f32[4,256,128]{2,1,0:T(8,128)S(1)}, f32[4,256,128]{2,1,0:T(8,128)S(1)}, f32[4,256,128]{2,1,0:T(8,128)S(1)}, f32[4,256,128]{2,1,0:T(8,128)S(1)}) custom-call(f32[4,256,128]{2,1,0:T(8,128)S(1)} %get-tuple-element.66.refs_0_.rest_0_, f32[4,256,128]{2,1,0:T(8,128)S(1)} %get-tuple-element.68.refs_1_.rest_0_, ...), custom_call_target="tpu_custom_call" | custom-call | bytes 18350080 | tf_op jit(solution)/shard_map/pallas_call | solution.py:218
  79.1 0.0 collective-permute-done.5.halo_ref
  79.1 1.2 shard_map.77
  80.3 0.3 collective-permute-start.7
  80.6 5.3 %collective-permute-done.4.halo_ref = f32[4,256,128]{2,1,0:T(8,128)S(1)} collective-permute-done((f32[4,256,128]{2,1,0:T(8,128)S(1)}, f32[4,256,128]{2,1,0:T(8,128)S(1)}, u32[]{:S(2)}, u32[]{:S(2)}) %collective-permute-start.4) | collective-permute-done | bytes 524320 | tf_op jit(solution)/shard_map/ppermute | solution.py:319
  85.9 1.2 shard_map.78
  87.1 2.7 %collective-permute-start.6 = (f32[4,256,128]{2,1,0:T(8,128)S(1)}, f32[4,256,128]{2,1,0:T(8,128)S(1)}, u32[]{:S(2)}, u32[]{:S(2)}) collective-permute-start(f32[4,256,128]{2,1,0:T(8,128)S(1)} %get-tuple-element.77.refs_1_), channel_id=1, source_target_pairs={{16,40},{17,41},{18,42},{19,43},{20,44},{21,45},{22,46},{23,47},{2... | collective-permute-start | bytes 1572872 | tf_op jit(solution)/shard_map/ppermute | solution.py:319
  89.9 6.3 %shard_map.79 = (f32[4,256,128]{2,1,0:T(8,128)S(1)}, f32[4,256,128]{2,1,0:T(8,128)S(1)}, f32[4,256,128]{2,1,0:T(8,128)S(1)}, f32[4,256,128]{2,1,0:T(8,128)S(1)}) custom-call(f32[4,256,128]{2,1,0:T(8,128)S(1)} %get-tuple-element.75.refs_0_, f32[4,256,128]{2,1,0:T(8,128)S(1)} %get-tuple-element.77.refs_1_, f32[4,256,128]{2,1,0:T(8,128)S(1)} %get-tuple-element.78.refs_2_, ...), custom_call_target="tpu_custom_call" | custom-call | bytes 18350080 | tf_op jit(solution)/shard_map/pallas_call | solution.py:218
  96.2 0.0 collective-permute-done.7.halo_ref
  96.2 1.2 shard_map.80.r0_ref
  97.4 5.0 %collective-permute-done.6.halo_ref = f32[4,256,128]{2,1,0:T(8,128)S(1)} collective-permute-done((f32[4,256,128]{2,1,0:T(8,128)S(1)}, f32[4,256,128]{2,1,0:T(8,128)S(1)}, u32[]{:S(2)}, u32[]{:S(2)}) %collective-permute-start.6) | collective-permute-done | bytes 524320 | tf_op jit(solution)/shard_map/ppermute | solution.py:319
  102.4 1.5 %shard_map.81 = f32[16,2,2,4,16,128]{5,4,3,2,1,0:T(8,128)S(1)} custom-call(f32[4,256,128]{2,1,0:T(8,128)S(1)} %collective-permute-done.6.halo_ref, f32[4,256,128]{2,1,0:T(8,128)S(1)} %get-tuple-element.82.pre_ref, f32[4,256,128]{2,1,0:T(8,128)S(1)} %shard_map.80.r0_ref, f32[4,256,128]{2,1,0:T(8,128)S(1)} %get-tuple-element.84.x0_ref, ...), custom_call_target="tpu_custom_call" | custom-call | bytes 7340032 | tf_op jit(solution)/shard_map/pallas_call | solution.py:218
  103.9 33.4 %all_to_all.10.in_ref = f32[16,2,2,4,16,128]{5,4,3,2,1,0:T(8,128)S(1)} all-to-all(f32[16,2,2,4,16,128]{5,4,3,2,1,0:T(8,128)S(1)} %shard_map.81), channel_id=1, replica_groups=mesh['space'=8,'mode'=16] {'mode'}, dimensions={0} | all-to-all | bytes 4194304 | tf_op jit(solution)/shard_map/all_to_all | solution.py:355
  137.3 1.5 %shard_map.82 = (f32[2,4,128,256]{3,2,1,0:T(8,128)}, f32[2,4,128,256]{3,2,1,0:T(8,128)}) custom-call(f32[16,2,2,4,16,128]{5,4,3,2,1,0:T(8,128)S(1)} %all_to_all.10.in_ref), custom_call_target="tpu_custom_call" | custom-call | bytes 4194304 | tf_op jit(solution)/shard_map/pallas_call | solution.py:218
  (2 shorter events, 0.1 us)
Async XLA Ops:
  3.2 26.4 %all-to-all-start = ((f32[16,2,4,16,128]{4,3,2,1,0:T(8,128)}), f32[16,2,4,16,128]{4,3,2,1,0:T(8,128)S(1)}, u32[]{:S(2)}, u32[]{:S(2)}) async-start(f32[16,2,4,16,128]{4,3,2,1,0:T(8,128)} %shard_map.68), calls=%async_computation | async-start | bytes 2097152 | tf_op jit(solution)/shard_map/all_to_all | solution.py:304
  29.6 6.2 %copy-start.5 = (bf16[2,5,4,128,128]{4,3,2,1,0:T(8,128)(2,1)S(1)}, bf16[2,5,4,128,128]{4,3,2,1,0:T(8,128)(2,1)}, u32[]{:S(2)}) copy-start(bf16[2,5,4,128,128]{4,3,2,1,0:T(8,128)(2,1)} %get-tuple-element.53.refs_6_.refs_8_) | copy-start | bytes 3932164
  29.6 6.2 %copy-start.6 = (bf16[2,5,4,128,128]{4,3,2,1,0:T(8,128)(2,1)S(1)}, bf16[2,5,4,128,128]{4,3,2,1,0:T(8,128)(2,1)}, u32[]{:S(2)}) copy-start(bf16[2,5,4,128,128]{4,3,2,1,0:T(8,128)(2,1)} %get-tuple-element.54.refs_7_.refs_9_) | copy-start | bytes 3932164
  29.8 17.4 %collective-permute-start.1 = (f32[4,256,128]{2,1,0:T(8,128)S(1)}, f32[4,256,128]{2,1,0:T(8,128)S(1)}, u32[]{:S(2)}, u32[]{:S(2)}) collective-permute-start(f32[4,256,128]{2,1,0:T(8,128)S(1)} %bitcast.10), channel_id=1, source_target_pairs={{0,16},{1,17},{2,18},{3,19},{4,20},{5,21},{6,22},{7,23},{8,24},{9,... | collective-permute-start | bytes 1572872 | tf_op jit(solution)/shard_map/ppermute | solution.py:319
  30.5 16.7 %copy-start = (bf16[2,5,4,128,128]{4,3,2,1,0:T(8,128)(2,1)S(1)}, bf16[2,5,4,128,128]{4,3,2,1,0:T(8,128)(2,1)}, u32[]{:S(2)}) copy-start(bf16[2,5,4,128,128]{4,3,2,1,0:T(8,128)(2,1)} %get-tuple-element.57.hh_ref) | copy-start | bytes 3932164
  30.5 16.7 %copy-start.1 = (bf16[2,5,4,128,128]{4,3,2,1,0:T(8,128)(2,1)S(1)}, bf16[2,5,4,128,128]{4,3,2,1,0:T(8,128)(2,1)}, u32[]{:S(2)}) copy-start(bf16[2,5,4,128,128]{4,3,2,1,0:T(8,128)(2,1)} %get-tuple-element.58.hl_ref) | copy-start | bytes 3932164
  30.5 19.7 %collective-permute-start = (f32[4,256,128]{2,1,0:T(8,128)S(1)}, f32[4,256,128]{2,1,0:T(8,128)S(1)}, u32[]{:S(2)}, u32[]{:S(2)}) collective-permute-start(f32[4,256,128]{2,1,0:T(8,128)S(1)} %bitcast.15), channel_id=1, source_target_pairs={{16,40},{17,41},{18,42},{19,43},{20,44},{21,45},{22,46},{23,47},{2... | collective-permute-start | bytes 1572872 | tf_op jit(solution)/shard_map/ppermute | solution.py:319
  35.9 2.5 %copy-start.2 = (bf16[2,5,512,512]{3,2,1,0:T(8,128)(2,1)S(1)}, bf16[2,5,512,512]{3,2,1,0:T(8,128)(2,1)}, u32[]{:S(2)}) copy-start(bf16[2,5,512,512]{3,2,1,0:T(8,128)(2,1)} %get-tuple-element.51.refs_4_.refs_6_) | copy-start | bytes 15728644
  38.3 2.5 %copy-start.4 = (bf16[2,5,512,512]{3,2,1,0:T(8,128)(2,1)S(1)}, bf16[2,5,512,512]{3,2,1,0:T(8,128)(2,1)}, u32[]{:S(2)}) copy-start(bf16[2,5,512,512]{3,2,1,0:T(8,128)(2,1)} %get-tuple-element.52.refs_5_.refs_7_) | copy-start | bytes 15728644
  47.2 7.7 %copy-start.3 = (bf16[2,5,512,512]{3,2,1,0:T(8,128)(2,1)S(1)}, bf16[2,5,512,512]{3,2,1,0:T(8,128)(2,1)}, u32[]{:S(2)}) copy-start(bf16[2,5,512,512]{3,2,1,0:T(8,128)(2,1)} %get-tuple-element.51.refs_4_.refs_6_) | copy-start | bytes 15728644
  48.4 13.5 %collective-permute-start.3 = (f32[4,256,128]{2,1,0:T(8,128)S(1)}, f32[4,256,128]{2,1,0:T(8,128)S(1)}, u32[]{:S(2)}, u32[]{:S(2)}) collective-permute-start(f32[4,256,128]{2,1,0:T(8,128)S(1)} %get-tuple-element.59.refs_0_.rest_0_), channel_id=1, source_target_pairs={{0,16},{1,17},{2,18},{3,19},{4,20},{5,21},{6,22},{7,23},{8,24},{9,... | collective-permute-start | bytes 1572872 | tf_op jit(solution)/shard_map/ppermute | solution.py:319
  51.4 17.1 %collective-permute-start.2 = (f32[4,256,128]{2,1,0:T(8,128)S(1)}, f32[4,256,128]{2,1,0:T(8,128)S(1)}, u32[]{:S(2)}, u32[]{:S(2)}) collective-permute-start(f32[4,256,128]{2,1,0:T(8,128)S(1)} %get-tuple-element.61.refs_1_.rest_0_), channel_id=1, source_target_pairs={{16,40},{17,41},{18,42},{19,43},{20,44},{21,45},{22,46},{23,47},{2... | collective-permute-start | bytes 1572872 | tf_op jit(solution)/shard_map/ppermute | solution.py:319
  63.1 16.0 %collective-permute-start.5 = (f32[4,256,128]{2,1,0:T(8,128)S(1)}, f32[4,256,128]{2,1,0:T(8,128)S(1)}, u32[]{:S(2)}, u32[]{:S(2)}) collective-permute-start(f32[4,256,128]{2,1,0:T(8,128)S(1)} %get-tuple-element.66.refs_0_.rest_0_), channel_id=1, source_target_pairs={{0,16},{1,17},{2,18},{3,19},{4,20},{5,21},{6,22},{7,23},{8,24},{9,... | collective-permute-start | bytes 1572872 | tf_op jit(solution)/shard_map/ppermute | solution.py:319
  69.7 16.2 %collective-permute-start.4 = (f32[4,256,128]{2,1,0:T(8,128)S(1)}, f32[4,256,128]{2,1,0:T(8,128)S(1)}, u32[]{:S(2)}, u32[]{:S(2)}) collective-permute-start(f32[4,256,128]{2,1,0:T(8,128)S(1)} %get-tuple-element.68.refs_1_.rest_0_), channel_id=1, source_target_pairs={{16,40},{17,41},{18,42},{19,43},{20,44},{21,45},{22,46},{23,47},{2... | collective-permute-start | bytes 1572872 | tf_op jit(solution)/shard_map/ppermute | solution.py:319
  80.3 15.9 %collective-permute-start.7 = (f32[4,256,128]{2,1,0:T(8,128)S(1)}, f32[4,256,128]{2,1,0:T(8,128)S(1)}, u32[]{:S(2)}, u32[]{:S(2)}) collective-permute-start(f32[4,256,128]{2,1,0:T(8,128)S(1)} %get-tuple-element.75.refs_0_), channel_id=1, source_target_pairs={{0,16},{1,17},{2,18},{3,19},{4,20},{5,21},{6,22},{7,23},{8,24},{9,... | collective-permute-start | bytes 1572872 | tf_op jit(solution)/shard_map/ppermute | solution.py:319
  87.1 15.3 %collective-permute-start.6 = (f32[4,256,128]{2,1,0:T(8,128)S(1)}, f32[4,256,128]{2,1,0:T(8,128)S(1)}, u32[]{:S(2)}, u32[]{:S(2)}) collective-permute-start(f32[4,256,128]{2,1,0:T(8,128)S(1)} %get-tuple-element.77.refs_1_), channel_id=1, source_target_pairs={{16,40},{17,41},{18,42},{19,43},{20,44},{21,45},{22,46},{23,47},{2... | collective-permute-start | bytes 1572872 | tf_op jit(solution)/shard_map/ppermute | solution.py:319

commit v4 on v3

--- a/solution.py
+++ b/solution.py
@@ -108,6 +108,9 @@
     layer = jnp.where(spot == 0, lead, 1 - lead)
     halo_at = pl.multiple_of((1 + layer) * blk, blk)
     cross_at = pl.multiple_of((2 - layer) * blk, blk)
+    slab = lax.axis_index("space").astype(jnp.int32)
+    ends = (slab == 0) | (slab == lax.axis_size("space") - 1)
+    inside = jnp.where((spot == 1) & ends, 0.0, 1.0).astype(F32)
 
     def build(src, scale):
         dense[...] = jnp.zeros_like(dense)
@@ -122,7 +125,7 @@
             dh_ref[0, 0, :, g * blk : g * blk + blk] = high
             dl_ref[0, 0, :, g * blk : g * blk + blk] = low
         for f in range(faces):
-            hh_ref[0, 0, f], hl_ref[0, 0, f] = split2(src(f, halo_at) * scale)
+            hh_ref[0, 0, f], hl_ref[0, 0, f] = split2(src(f, halo_at) * scale * inside)
             ch_ref[0, 0, f], cl_ref[0, 0, f] = split2(src(f, cross_at) * scale)
 
     @pl.when(op == 0)
@@ -136,13 +139,15 @@
 
 def off_layer(total, field, op_h, op_l, layer, f, group):
     high, low = split2(field)
-    lefts, rights = [], []
-    for op in range(op_h.shape[1]):
-        ph, plow = permuted(high, op, group), permuted(low, op, group)
-        wh, wl = op_h[layer, op, f], op_l[layer, op, f]
-        lefts += [ph, plow, ph]
-        rights += [wh, wh, wl]
-    return total + dot_nt(jnp.concatenate(lefts, axis=1), jnp.concatenate(rights, axis=1))
+    ops = range(op_h.shape[1])
+    heavy = [op_h[layer, op, f] for op in ops]
+    wide = [jnp.concatenate([op_h[layer, op, f], op_l[layer, op, f]], axis=0) for op in ops]
+    tops = jnp.concatenate([permuted(high, op, group) for op in ops], axis=1)
+    rest = jnp.concatenate([permuted(low, op, group) for op in ops], axis=1)
+    both = dot_nt(tops, jnp.concatenate(wide, axis=1))
+    blk = field.shape[1]
+    small = both[:, blk:] + dot_nt(rest, jnp.concatenate(heavy, axis=1))
+    return total + (both[:, :blk] + small)
 
 
 def local_kernel(group, with_x, *refs):
@@ -271,10 +276,9 @@
     half = modes // 2
     pairs = []
     for s in range(count):
-        t = s + 1 if (s % 2 == 0) == inner else s - 1
-        if 0 <= t < count:
-            turn = half if (s // 2 - t // 2) % 2 else 0
-            pairs += [(s * modes + m, t * modes + (m ^ turn)) for m in range(modes)]
+        t = (s + 1 if (s % 2 == 0) == inner else s - 1) % count
+        turn = half if (s // 2 - t // 2) % 2 else 0
+        pairs += [(s * modes + m, t * modes + (m ^ turn)) for m in range(modes)]
     return pairs
 
 

time: 140 us -> 136 us (0.971)
  the two profiles are of different devices: /device:TPU:8 before, /device:TPU:1 now
where the time goes in v4:
time: 136 us
  Pallas kernels  54.1 us (40%)
  blocking collectives  36 us (26%)
  starting transfers between devices  27.2 us (20%)
  waiting for transfers between devices  12.5 us (9%)
  local copies, waits for them, and re-layouts  5.15 us (4%)
    all_to_all x1, blocking collectives, per_device(): back = lax.all_to_all(send, 'mode', 0, 0, tiled=True)  36 us
    pallas_call x14, Pallas kernels, call(): pl.pallas_call(body, out_shape=outs, in_specs=[pl.BlockSpec(memory_space=...  35.7 us
    pallas_call x1, Pallas kernels, prepare(): pl.pallas_call(prepare_kernel, grid_spec=grid_spec, out_shape=[dense] * 2...  18.5 us
    ppermute x8, starting transfers between devices, per_device(): halo = [lax.ppermute(d[l], AXES, links[l]) for l in range(layers)]  17.9 us
    ppermute x8, waiting for transfers between devices, per_device(): halo = [lax.ppermute(d[l], AXES, links[l]) for l in range(layers)]  12.5 us
    all_to_all x1, starting transfers between devices, per_device(): got = lax.all_to_all(sent, 'mode', 0, 0, tiled=True)  9.3 us
    unnamed x14, local copies, waits for them, and re-layouts  4.99 us
  transfers between devices with their start and end apart: 9, of which 4 were waited for; matrix products, arithmetic and copies ran while one was open for 0% of the time, Pallas kernels for 36%

profile of v4, /device:TPU:1, one launch (start us, length us, event | category | flops | bytes accessed | tf_op | source)
XLA Modules:
  0.0 136.0 jit_solution(13562647430300457732)
XLA Ops:
  0.6 2.6 %shard_map.68 = f32[16,2,4,16,128]{4,3,2,1,0:T(8,128)} custom-call(f32[2,4,128,256]{3,2,1,0:T(8,128)} %field_ref.2), custom_call_target="tpu_custom_call" | custom-call | bytes 2097152 | tf_op jit(solution)/shard_map/pallas_call | solution.py:223
  3.2 9.3 %all-to-all-start = ((f32[16,2,4,16,128]{4,3,2,1,0:T(8,128)}), f32[16,2,4,16,128]{4,3,2,1,0:T(8,128)S(1)}, u32[]{:S(2)}, u32[]{:S(2)}) async-start(f32[16,2,4,16,128]{4,3,2,1,0:T(8,128)} %shard_map.68), calls=%async_computation | async-start | bytes 2097152 | tf_op jit(solution)/shard_map/all_to_all | solution.py:308
  12.5 18.5 %shard_map.69 = (bf16[2,5,512,512]{3,2,1,0:T(8,128)(2,1)}, bf16[2,5,512,512]{3,2,1,0:T(8,128)(2,1)}, bf16[2,5,4,128,128]{4,3,2,1,0:T(8,128)(2,1)}, bf16[2,5,4,12...) custom-call(s32[4]{0:T(128)} %masks_ref.1, ...), custom_call_target="tpu_custom_call" | custom-call | flops 100000000 | bytes 37748736 | tf_op jit(solution)/shard_map/pallas_call | solution.py:266
  31.0 0.0 all-to-all-done
  31.0 0.0 copy-start.5
  31.0 0.0 copy-start.6
  31.0 0.1 slice_bitcast_fusion
  31.2 0.4 collective-permute-start.1
  31.7 0.0 copy-start
  31.7 0.0 copy-start.1
  31.7 5.3 %collective-permute-start = (f32[4,256,128]{2,1,0:T(8,128)S(1)}, f32[4,256,128]{2,1,0:T(8,128)S(1)}, u32[]{:S(2)}, u32[]{:S(2)}) collective-permute-start(f32[4,256,128]{2,1,0:T(8,128)S(1)} %bitcast.15), channel_id=1, source_target_pairs={{0,120},{1,121},{2,122},{3,123},{4,124},{5,125},{6,126},{7,127},{8... | collective-permute-start | bytes 1572872 | tf_op jit(solution)/shard_map/ppermute | solution.py:323
  37.0 0.0 copy-done.5
  37.0 0.0 copy-done.6
  37.0 0.0 copy-start.2
  37.0 2.5 %copy-done.2 = bf16[2,5,512,512]{3,2,1,0:T(8,128)(2,1)S(1)} copy-done((bf16[2,5,512,512]{3,2,1,0:T(8,128)(2,1)S(1)}, bf16[2,5,512,512]{3,2,1,0:T(8,128)(2,1)}, u32[]{:S(2)}) %copy-start.2) | copy-done | bytes 5242904
  39.5 0.0 copy-start.4
  39.5 2.5 %copy-done.4 = bf16[2,5,512,512]{3,2,1,0:T(8,128)(2,1)S(1)} copy-done((bf16[2,5,512,512]{3,2,1,0:T(8,128)(2,1)S(1)}, bf16[2,5,512,512]{3,2,1,0:T(8,128)(2,1)}, u32[]{:S(2)}) %copy-start.4) | copy-done | bytes 5242904
  42.0 5.8 %shard_map.70 = (f32[4,256,128]{2,1,0:T(8,128)S(1)}, f32[4,256,128]{2,1,0:T(8,128)S(1)}) custom-call(f32[4,256,128]{2,1,0:T(8,128)S(1)} %bitcast.11, f32[4,256,128]{2,1,0:T(8,128)S(1)} %bitcast.16, f32[4,256,128]{2,1,0:T(8,128)S(1)} %bitcast.12, f32[4,256,128]{2,1,0:T(8,128)S(1)} %bitcast.17, bf16[2,5,512,512]{3,2,1,0:T(8,128)(2,1)S(1)} %copy-done.2, ...), custom_call_target="tpu_custom_call" | custom-call | bytes 16252928 | tf_op jit(solution)/shard_map/pallas_call | solution.py:223
  47.8 0.0 collective-permute-done.1.halo_ref
  47.8 0.0 copy-done
  47.9 0.0 copy-done.1
  47.9 0.0 copy-start.3
  47.9 1.0 shard_map.71
  48.9 0.1 collective-permute-start.3
  49.0 0.0 collective-permute-done.halo_ref
  49.0 1.0 shard_map.72
  49.9 4.5 %collective-permute-start.2 = (f32[4,256,128]{2,1,0:T(8,128)S(1)}, f32[4,256,128]{2,1,0:T(8,128)S(1)}, u32[]{:S(2)}, u32[]{:S(2)}) collective-permute-start(f32[4,256,128]{2,1,0:T(8,128)S(1)} %get-tuple-element.61.refs_1_.rest_0_), channel_id=1, source_target_pairs={{0,120},{1,121},{2,122},{3,123},{4,124},{5,125},{6,126},{7,127},{8... | collective-permute-start | bytes 1572872 | tf_op jit(solution)/shard_map/ppermute | solution.py:323
  54.4 0.0 copy-done.3
  54.4 5.8 %shard_map.73 = (f32[4,256,128]{2,1,0:T(8,128)S(1)}, f32[4,256,128]{2,1,0:T(8,128)S(1)}, f32[4,256,128]{2,1,0:T(8,128)S(1)}, f32[4,256,128]{2,1,0:T(8,128)S(1)}) custom-call(f32[4,256,128]{2,1,0:T(8,128)S(1)} %get-tuple-element.59.refs_0_.rest_0_, f32[4,256,128]{2,1,0:T(8,128)S(1)} %get-tuple-element.61.refs_1_.rest_0_, ...), custom_call_target="tpu_custom_call" | custom-call | bytes 18350080 | tf_op jit(solution)/shard_map/pallas_call | solution.py:223
  60.3 1.2 collective-permute-done.3.halo_ref
  61.4 1.0 shard_map.74
  62.4 0.4 collective-permute-start.5
  62.9 3.2 %collective-permute-done.2.halo_ref = f32[4,256,128]{2,1,0:T(8,128)S(1)} collective-permute-done((f32[4,256,128]{2,1,0:T(8,128)S(1)}, f32[4,256,128]{2,1,0:T(8,128)S(1)}, u32[]{:S(2)}, u32[]{:S(2)}) %collective-permute-start.2) | collective-permute-done | bytes 524320 | tf_op jit(solution)/shard_map/ppermute | solution.py:323
  66.0 1.0 shard_map.75
  67.0 3.7 %collective-permute-start.4 = (f32[4,256,128]{2,1,0:T(8,128)S(1)}, f32[4,256,128]{2,1,0:T(8,128)S(1)}, u32[]{:S(2)}, u32[]{:S(2)}) collective-permute-start(f32[4,256,128]{2,1,0:T(8,128)S(1)} %get-tuple-element.68.refs_1_.rest_0_), channel_id=1, source_target_pairs={{0,120},{1,121},{2,122},{3,123},{4,124},{5,125},{6,126},{7,127},{8... | collective-permute-start | bytes 1572872 | tf_op jit(solution)/shard_map/ppermute | solution.py:323
  70.7 5.8 %shard_map.76 = (f32[4,256,128]{2,1,0:T(8,128)S(1)}, f32[4,256,128]{2,1,0:T(8,128)S(1)}, f32[4,256,128]{2,1,0:T(8,128)S(1)}, f32[4,256,128]{2,1,0:T(8,128)S(1)}) custom-call(f32[4,256,128]{2,1,0:T(8,128)S(1)} %get-tuple-element.66.refs_0_.rest_0_, f32[4,256,128]{2,1,0:T(8,128)S(1)} %get-tuple-element.68.refs_1_.rest_0_, ...), custom_call_target="tpu_custom_call" | custom-call | bytes 18350080 | tf_op jit(solution)/shard_map/pallas_call | solution.py:223
  76.5 0.0 collective-permute-done.5.halo_ref
  76.6 1.0 shard_map.77
  77.5 0.3 collective-permute-start.7
  77.9 4.1 %collective-permute-done.4.halo_ref = f32[4,256,128]{2,1,0:T(8,128)S(1)} collective-permute-done((f32[4,256,128]{2,1,0:T(8,128)S(1)}, f32[4,256,128]{2,1,0:T(8,128)S(1)}, u32[]{:S(2)}, u32[]{:S(2)}) %collective-permute-start.4) | collective-permute-done | bytes 524320 | tf_op jit(solution)/shard_map/ppermute | solution.py:323
  82.0 1.0 shard_map.78
  82.9 3.1 %collective-permute-start.6 = (f32[4,256,128]{2,1,0:T(8,128)S(1)}, f32[4,256,128]{2,1,0:T(8,128)S(1)}, u32[]{:S(2)}, u32[]{:S(2)}) collective-permute-start(f32[4,256,128]{2,1,0:T(8,128)S(1)} %get-tuple-element.77.refs_1_), channel_id=1, source_target_pairs={{0,120},{1,121},{2,122},{3,123},{4,124},{5,125},{6,126},{7,127},{8... | collective-permute-start | bytes 1572872 | tf_op jit(solution)/shard_map/ppermute | solution.py:323
  86.1 5.8 %shard_map.79 = (f32[4,256,128]{2,1,0:T(8,128)S(1)}, f32[4,256,128]{2,1,0:T(8,128)S(1)}, f32[4,256,128]{2,1,0:T(8,128)S(1)}, f32[4,256,128]{2,1,0:T(8,128)S(1)}) custom-call(f32[4,256,128]{2,1,0:T(8,128)S(1)} %get-tuple-element.75.refs_0_, f32[4,256,128]{2,1,0:T(8,128)S(1)} %get-tuple-element.77.refs_1_, f32[4,256,128]{2,1,0:T(8,128)S(1)} %get-tuple-element.78.refs_2_, ...), custom_call_target="tpu_custom_call" | custom-call | bytes 18350080 | tf_op jit(solution)/shard_map/pallas_call | solution.py:223
  91.9 0.0 collective-permute-done.7.halo_ref
  91.9 1.0 shard_map.80.r0_ref
  92.9 4.1 %collective-permute-done.6.halo_ref = f32[4,256,128]{2,1,0:T(8,128)S(1)} collective-permute-done((f32[4,256,128]{2,1,0:T(8,128)S(1)}, f32[4,256,128]{2,1,0:T(8,128)S(1)}, u32[]{:S(2)}, u32[]{:S(2)}) %collective-permute-start.6) | collective-permute-done | bytes 524320 | tf_op jit(solution)/shard_map/ppermute | solution.py:323
  97.0 1.3 shard_map.81
  98.3 36.0 %all_to_all.10.in_ref = f32[16,2,2,4,16,128]{5,4,3,2,1,0:T(8,128)S(1)} all-to-all(f32[16,2,2,4,16,128]{5,4,3,2,1,0:T(8,128)S(1)} %shard_map.81), channel_id=1, replica_groups=mesh['space'=8,'mode'=16] {'mode'}, dimensions={0} | all-to-all | bytes 4194304 | tf_op jit(solution)/shard_map/all_to_all | solution.py:359
  134.2 1.5 %shard_map.82 = (f32[2,4,128,256]{3,2,1,0:T(8,128)}, f32[2,4,128,256]{3,2,1,0:T(8,128)}) custom-call(f32[16,2,2,4,16,128]{5,4,3,2,1,0:T(8,128)S(1)} %all_to_all.10.in_ref), custom_call_target="tpu_custom_call" | custom-call | bytes 4194304 | tf_op jit(solution)/shard_map/pallas_call | solution.py:223
  (2 shorter events, 0.1 us)
Async XLA Ops:
  3.2 27.8 %all-to-all-start = ((f32[16,2,4,16,128]{4,3,2,1,0:T(8,128)}), f32[16,2,4,16,128]{4,3,2,1,0:T(8,128)S(1)}, u32[]{:S(2)}, u32[]{:S(2)}) async-start(f32[16,2,4,16,128]{4,3,2,1,0:T(8,128)} %shard_map.68), calls=%async_computation | async-start | bytes 2097152 | tf_op jit(solution)/shard_map/all_to_all | solution.py:308
  31.0 6.0 %copy-start.5 = (bf16[2,5,4,128,128]{4,3,2,1,0:T(8,128)(2,1)S(1)}, bf16[2,5,4,128,128]{4,3,2,1,0:T(8,128)(2,1)}, u32[]{:S(2)}) copy-start(bf16[2,5,4,128,128]{4,3,2,1,0:T(8,128)(2,1)} %get-tuple-element.53.refs_6_.refs_8_) | copy-start | bytes 3932164
  31.0 6.0 %copy-start.6 = (bf16[2,5,4,128,128]{4,3,2,1,0:T(8,128)(2,1)S(1)}, bf16[2,5,4,128,128]{4,3,2,1,0:T(8,128)(2,1)}, u32[]{:S(2)}) copy-start(bf16[2,5,4,128,128]{4,3,2,1,0:T(8,128)(2,1)} %get-tuple-element.54.refs_7_.refs_9_) | copy-start | bytes 3932164
  31.2 16.7 %collective-permute-start.1 = (f32[4,256,128]{2,1,0:T(8,128)S(1)}, f32[4,256,128]{2,1,0:T(8,128)S(1)}, u32[]{:S(2)}, u32[]{:S(2)}) collective-permute-start(f32[4,256,128]{2,1,0:T(8,128)S(1)} %bitcast.10), channel_id=1, source_target_pairs={{0,16},{1,17},{2,18},{3,19},{4,20},{5,21},{6,22},{7,23},{8,24},{9,... | collective-permute-start | bytes 1572872 | tf_op jit(solution)/shard_map/ppermute | solution.py:323
  31.7 16.2 %copy-start = (bf16[2,5,4,128,128]{4,3,2,1,0:T(8,128)(2,1)S(1)}, bf16[2,5,4,128,128]{4,3,2,1,0:T(8,128)(2,1)}, u32[]{:S(2)}) copy-start(bf16[2,5,4,128,128]{4,3,2,1,0:T(8,128)(2,1)} %get-tuple-element.57.hh_ref) | copy-start | bytes 3932164
  31.7 16.2 %copy-start.1 = (bf16[2,5,4,128,128]{4,3,2,1,0:T(8,128)(2,1)S(1)}, bf16[2,5,4,128,128]{4,3,2,1,0:T(8,128)(2,1)}, u32[]{:S(2)}) copy-start(bf16[2,5,4,128,128]{4,3,2,1,0:T(8,128)(2,1)} %get-tuple-element.58.hl_ref) | copy-start | bytes 3932164
  31.7 17.3 %collective-permute-start = (f32[4,256,128]{2,1,0:T(8,128)S(1)}, f32[4,256,128]{2,1,0:T(8,128)S(1)}, u32[]{:S(2)}, u32[]{:S(2)}) collective-permute-start(f32[4,256,128]{2,1,0:T(8,128)S(1)} %bitcast.15), channel_id=1, source_target_pairs={{0,120},{1,121},{2,122},{3,123},{4,124},{5,125},{6,126},{7,127},{8... | collective-permute-start | bytes 1572872 | tf_op jit(solution)/shard_map/ppermute | solution.py:323
  37.0 2.5 %copy-start.2 = (bf16[2,5,512,512]{3,2,1,0:T(8,128)(2,1)S(1)}, bf16[2,5,512,512]{3,2,1,0:T(8,128)(2,1)}, u32[]{:S(2)}) copy-start(bf16[2,5,512,512]{3,2,1,0:T(8,128)(2,1)} %get-tuple-element.51.refs_4_.refs_6_) | copy-start | bytes 15728644
  39.5 2.5 %copy-start.4 = (bf16[2,5,512,512]{3,2,1,0:T(8,128)(2,1)S(1)}, bf16[2,5,512,512]{3,2,1,0:T(8,128)(2,1)}, u32[]{:S(2)}) copy-start(bf16[2,5,512,512]{3,2,1,0:T(8,128)(2,1)} %get-tuple-element.52.refs_5_.refs_7_) | copy-start | bytes 15728644
  47.9 6.6 %copy-start.3 = (bf16[2,5,512,512]{3,2,1,0:T(8,128)(2,1)S(1)}, bf16[2,5,512,512]{3,2,1,0:T(8,128)(2,1)}, u32[]{:S(2)}) copy-start(bf16[2,5,512,512]{3,2,1,0:T(8,128)(2,1)} %get-tuple-element.51.refs_4_.refs_6_) | copy-start | bytes 15728644
  48.9 12.6 %collective-permute-start.3 = (f32[4,256,128]{2,1,0:T(8,128)S(1)}, f32[4,256,128]{2,1,0:T(8,128)S(1)}, u32[]{:S(2)}, u32[]{:S(2)}) collective-permute-start(f32[4,256,128]{2,1,0:T(8,128)S(1)} %get-tuple-element.59.refs_0_.rest_0_), channel_id=1, source_target_pairs={{0,16},{1,17},{2,18},{3,19},{4,20},{5,21},{6,22},{7,23},{8,24},{9,... | collective-permute-start | bytes 1572872 | tf_op jit(solution)/shard_map/ppermute | solution.py:323
  49.9 16.1 %collective-permute-start.2 = (f32[4,256,128]{2,1,0:T(8,128)S(1)}, f32[4,256,128]{2,1,0:T(8,128)S(1)}, u32[]{:S(2)}, u32[]{:S(2)}) collective-permute-start(f32[4,256,128]{2,1,0:T(8,128)S(1)} %get-tuple-element.61.refs_1_.rest_0_), channel_id=1, source_target_pairs={{0,120},{1,121},{2,122},{3,123},{4,124},{5,125},{6,126},{7,127},{8... | collective-permute-start | bytes 1572872 | tf_op jit(solution)/shard_map/ppermute | solution.py:323
  62.4 14.1 %collective-permute-start.5 = (f32[4,256,128]{2,1,0:T(8,128)S(1)}, f32[4,256,128]{2,1,0:T(8,128)S(1)}, u32[]{:S(2)}, u32[]{:S(2)}) collective-permute-start(f32[4,256,128]{2,1,0:T(8,128)S(1)} %get-tuple-element.66.refs_0_.rest_0_), channel_id=1, source_target_pairs={{0,16},{1,17},{2,18},{3,19},{4,20},{5,21},{6,22},{7,23},{8,24},{9,... | collective-permute-start | bytes 1572872 | tf_op jit(solution)/shard_map/ppermute | solution.py:323
  67.0 15.0 %collective-permute-start.4 = (f32[4,256,128]{2,1,0:T(8,128)S(1)}, f32[4,256,128]{2,1,0:T(8,128)S(1)}, u32[]{:S(2)}, u32[]{:S(2)}) collective-permute-start(f32[4,256,128]{2,1,0:T(8,128)S(1)} %get-tuple-element.68.refs_1_.rest_0_), channel_id=1, source_target_pairs={{0,120},{1,121},{2,122},{3,123},{4,124},{5,125},{6,126},{7,127},{8... | collective-permute-start | bytes 1572872 | tf_op jit(solution)/shard_map/ppermute | solution.py:323
  77.5 14.4 %collective-permute-start.7 = (f32[4,256,128]{2,1,0:T(8,128)S(1)}, f32[4,256,128]{2,1,0:T(8,128)S(1)}, u32[]{:S(2)}, u32[]{:S(2)}) collective-permute-start(f32[4,256,128]{2,1,0:T(8,128)S(1)} %get-tuple-element.75.refs_0_), channel_id=1, source_target_pairs={{0,16},{1,17},{2,18},{3,19},{4,20},{5,21},{6,22},{7,23},{8,24},{9,... | collective-permute-start | bytes 1572872 | tf_op jit(solution)/shard_map/ppermute | solution.py:323
  82.9 14.0 %collective-permute-start.6 = (f32[4,256,128]{2,1,0:T(8,128)S(1)}, f32[4,256,128]{2,1,0:T(8,128)S(1)}, u32[]{:S(2)}, u32[]{:S(2)}) collective-permute-start(f32[4,256,128]{2,1,0:T(8,128)S(1)} %get-tuple-element.77.refs_1_), channel_id=1, source_target_pairs={{0,120},{1,121},{2,122},{3,123},{4,124},{5,125},{6,126},{7,127},{8... | collective-permute-start | bytes 1572872 | tf_op jit(solution)/shard_map/ppermute | solution.py:323

commit v5 on v4

--- a/solution.py
+++ b/solution.py
@@ -60,9 +60,9 @@
     for l in range(layers):
         for f in range(faces):
             ins[l * faces + f].wait()
-            rows = arrived[l, f].T.reshape(pieces, group, blk)
-            laid[pl.ds(first, half), l, f] = rows[:half]
-            laid[pl.ds(second, half), l, f] = rows[half:]
+            for at, start in enumerate((first, second)):
+                columns = arrived[l, f, :, at * half * group : (at + 1) * half * group]
+                laid[pl.ds(start, half), l, f] = columns.T.reshape(half, group, blk)
         outs.append(pltpu.make_async_copy(laid.at[:, l], out_ref.at[:, l], out_sems.at[l]))
         outs[-1].start()
     for copy in outs:

time: 136 us -> 136 us (level)
  no operation moved by 1% of the time
where the time goes in v5:
time: 136 us
  Pallas kernels  54.1 us (40%)
  blocking collectives  36 us (26%)
  starting transfers between devices  27.2 us (20%)
  waiting for transfers between devices  12.5 us (9%)
  local copies, waits for them, and re-layouts  5.15 us (4%)
    all_to_all x1, blocking collectives, per_device(): back = lax.all_to_all(send, 'mode', 0, 0, tiled=True)  36 us
    pallas_call x14, Pallas kernels, call(): pl.pallas_call(body, out_shape=outs, in_specs=[pl.BlockSpec(memory_space=...  35.7 us
    pallas_call x1, Pallas kernels, prepare(): pl.pallas_call(prepare_kernel, grid_spec=grid_spec, out_shape=[dense] * 2...  18.5 us
    ppermute x8, starting transfers between devices, per_device(): halo = [lax.ppermute(d[l], AXES, links[l]) for l in range(layers)]  17.9 us
    ppermute x8, waiting for transfers between devices, per_device(): halo = [lax.ppermute(d[l], AXES, links[l]) for l in range(layers)]  12.5 us
    all_to_all x1, starting transfers between devices, per_device(): got = lax.all_to_all(sent, 'mode', 0, 0, tiled=True)  9.3 us
    unnamed x14, local copies, waits for them, and re-layouts  4.99 us
  transfers between devices with their start and end apart: 9, of which 4 were waited for; matrix products, arithmetic and copies ran while one was open for 0% of the time, Pallas kernels for 36%

profile of v5, /device:TPU:1, one launch (start us, length us, event | category | flops | bytes accessed | tf_op | source)
XLA Modules:
  0.0 136.0 jit_solution(13562647430300457732)
XLA Ops:
  0.6 2.6 %shard_map.68 = f32[16,2,4,16,128]{4,3,2,1,0:T(8,128)} custom-call(f32[2,4,128,256]{3,2,1,0:T(8,128)} %field_ref.2), custom_call_target="tpu_custom_call" | custom-call | bytes 2097152 | tf_op jit(solution)/shard_map/pallas_call | solution.py:223
  3.2 9.3 %all-to-all-start = ((f32[16,2,4,16,128]{4,3,2,1,0:T(8,128)}), f32[16,2,4,16,128]{4,3,2,1,0:T(8,128)S(1)}, u32[]{:S(2)}, u32[]{:S(2)}) async-start(f32[16,2,4,16,128]{4,3,2,1,0:T(8,128)} %shard_map.68), calls=%async_computation | async-start | bytes 2097152 | tf_op jit(solution)/shard_map/all_to_all | solution.py:308
  12.5 18.5 %shard_map.69 = (bf16[2,5,512,512]{3,2,1,0:T(8,128)(2,1)}, bf16[2,5,512,512]{3,2,1,0:T(8,128)(2,1)}, bf16[2,5,4,128,128]{4,3,2,1,0:T(8,128)(2,1)}, bf16[2,5,4,12...) custom-call(s32[4]{0:T(128)} %masks_ref.1, ...), custom_call_target="tpu_custom_call" | custom-call | flops 100000000 | bytes 37748736 | tf_op jit(solution)/shard_map/pallas_call | solution.py:266
  31.0 0.0 all-to-all-done
  31.0 0.0 copy-start.5
  31.0 0.0 copy-start.6
  31.0 0.1 slice_bitcast_fusion
  31.2 0.4 collective-permute-start.1
  31.7 0.0 copy-start
  31.7 0.0 copy-start.1
  31.7 5.3 %collective-permute-start = (f32[4,256,128]{2,1,0:T(8,128)S(1)}, f32[4,256,128]{2,1,0:T(8,128)S(1)}, u32[]{:S(2)}, u32[]{:S(2)}) collective-permute-start(f32[4,256,128]{2,1,0:T(8,128)S(1)} %bitcast.15), channel_id=1, source_target_pairs={{0,120},{1,121},{2,122},{3,123},{4,124},{5,125},{6,126},{7,127},{8... | collective-permute-start | bytes 1572872 | tf_op jit(solution)/shard_map/ppermute | solution.py:323
  37.0 0.0 copy-done.5
  37.0 0.0 copy-done.6
  37.0 0.0 copy-start.2
  37.0 2.5 %copy-done.2 = bf16[2,5,512,512]{3,2,1,0:T(8,128)(2,1)S(1)} copy-done((bf16[2,5,512,512]{3,2,1,0:T(8,128)(2,1)S(1)}, bf16[2,5,512,512]{3,2,1,0:T(8,128)(2,1)}, u32[]{:S(2)}) %copy-start.2) | copy-done | bytes 5242904
  39.5 0.0 copy-start.4
  39.5 2.5 %copy-done.4 = bf16[2,5,512,512]{3,2,1,0:T(8,128)(2,1)S(1)} copy-done((bf16[2,5,512,512]{3,2,1,0:T(8,128)(2,1)S(1)}, bf16[2,5,512,512]{3,2,1,0:T(8,128)(2,1)}, u32[]{:S(2)}) %copy-start.4) | copy-done | bytes 5242904
  42.0 5.8 %shard_map.70 = (f32[4,256,128]{2,1,0:T(8,128)S(1)}, f32[4,256,128]{2,1,0:T(8,128)S(1)}) custom-call(f32[4,256,128]{2,1,0:T(8,128)S(1)} %bitcast.11, f32[4,256,128]{2,1,0:T(8,128)S(1)} %bitcast.16, f32[4,256,128]{2,1,0:T(8,128)S(1)} %bitcast.12, f32[4,256,128]{2,1,0:T(8,128)S(1)} %bitcast.17, bf16[2,5,512,512]{3,2,1,0:T(8,128)(2,1)S(1)} %copy-done.2, ...), custom_call_target="tpu_custom_call" | custom-call | bytes 16252928 | tf_op jit(solution)/shard_map/pallas_call | solution.py:223
  47.8 0.0 collective-permute-done.1.halo_ref
  47.8 0.0 copy-done
  47.9 0.0 copy-done.1
  47.9 0.0 copy-start.3
  47.9 1.0 shard_map.71
  48.9 0.1 collective-permute-start.3
  49.0 0.0 collective-permute-done.halo_ref
  49.0 1.0 shard_map.72
  49.9 4.5 %collective-permute-start.2 = (f32[4,256,128]{2,1,0:T(8,128)S(1)}, f32[4,256,128]{2,1,0:T(8,128)S(1)}, u32[]{:S(2)}, u32[]{:S(2)}) collective-permute-start(f32[4,256,128]{2,1,0:T(8,128)S(1)} %get-tuple-element.61.refs_1_.rest_0_), channel_id=1, source_target_pairs={{0,120},{1,121},{2,122},{3,123},{4,124},{5,125},{6,126},{7,127},{8... | collective-permute-start | bytes 1572872 | tf_op jit(solution)/shard_map/ppermute | solution.py:323
  54.4 0.0 copy-done.3
  54.4 5.8 %shard_map.73 = (f32[4,256,128]{2,1,0:T(8,128)S(1)}, f32[4,256,128]{2,1,0:T(8,128)S(1)}, f32[4,256,128]{2,1,0:T(8,128)S(1)}, f32[4,256,128]{2,1,0:T(8,128)S(1)}) custom-call(f32[4,256,128]{2,1,0:T(8,128)S(1)} %get-tuple-element.59.refs_0_.rest_0_, f32[4,256,128]{2,1,0:T(8,128)S(1)} %get-tuple-element.61.refs_1_.rest_0_, ...), custom_call_target="tpu_custom_call" | custom-call | bytes 18350080 | tf_op jit(solution)/shard_map/pallas_call | solution.py:223
  60.3 1.2 collective-permute-done.3.halo_ref
  61.4 1.0 shard_map.74
  62.4 0.4 collective-permute-start.5
  62.8 3.2 %collective-permute-done.2.halo_ref = f32[4,256,128]{2,1,0:T(8,128)S(1)} collective-permute-done((f32[4,256,128]{2,1,0:T(8,128)S(1)}, f32[4,256,128]{2,1,0:T(8,128)S(1)}, u32[]{:S(2)}, u32[]{:S(2)}) %collective-permute-start.2) | collective-permute-done | bytes 524320 | tf_op jit(solution)/shard_map/ppermute | solution.py:323
  66.0 1.0 shard_map.75
  67.0 3.7 %collective-permute-start.4 = (f32[4,256,128]{2,1,0:T(8,128)S(1)}, f32[4,256,128]{2,1,0:T(8,128)S(1)}, u32[]{:S(2)}, u32[]{:S(2)}) collective-permute-start(f32[4,256,128]{2,1,0:T(8,128)S(1)} %get-tuple-element.68.refs_1_.rest_0_), channel_id=1, source_target_pairs={{0,120},{1,121},{2,122},{3,123},{4,124},{5,125},{6,126},{7,127},{8... | collective-permute-start | bytes 1572872 | tf_op jit(solution)/shard_map/ppermute | solution.py:323
  70.7 5.8 %shard_map.76 = (f32[4,256,128]{2,1,0:T(8,128)S(1)}, f32[4,256,128]{2,1,0:T(8,128)S(1)}, f32[4,256,128]{2,1,0:T(8,128)S(1)}, f32[4,256,128]{2,1,0:T(8,128)S(1)}) custom-call(f32[4,256,128]{2,1,0:T(8,128)S(1)} %get-tuple-element.66.refs_0_.rest_0_, f32[4,256,128]{2,1,0:T(8,128)S(1)} %get-tuple-element.68.refs_1_.rest_0_, ...), custom_call_target="tpu_custom_call" | custom-call | bytes 18350080 | tf_op jit(solution)/shard_map/pallas_call | solution.py:223
  76.6 0.0 collective-permute-done.5.halo_ref
  76.6 1.0 shard_map.77
  77.6 0.3 collective-permute-start.7
  77.9 4.1 %collective-permute-done.4.halo_ref = f32[4,256,128]{2,1,0:T(8,128)S(1)} collective-permute-done((f32[4,256,128]{2,1,0:T(8,128)S(1)}, f32[4,256,128]{2,1,0:T(8,128)S(1)}, u32[]{:S(2)}, u32[]{:S(2)}) %collective-permute-start.4) | collective-permute-done | bytes 524320 | tf_op jit(solution)/shard_map/ppermute | solution.py:323
  82.0 1.0 shard_map.78
  83.0 3.1 %collective-permute-start.6 = (f32[4,256,128]{2,1,0:T(8,128)S(1)}, f32[4,256,128]{2,1,0:T(8,128)S(1)}, u32[]{:S(2)}, u32[]{:S(2)}) collective-permute-start(f32[4,256,128]{2,1,0:T(8,128)S(1)} %get-tuple-element.77.refs_1_), channel_id=1, source_target_pairs={{0,120},{1,121},{2,122},{3,123},{4,124},{5,125},{6,126},{7,127},{8... | collective-permute-start | bytes 1572872 | tf_op jit(solution)/shard_map/ppermute | solution.py:323
  86.1 5.8 %shard_map.79 = (f32[4,256,128]{2,1,0:T(8,128)S(1)}, f32[4,256,128]{2,1,0:T(8,128)S(1)}, f32[4,256,128]{2,1,0:T(8,128)S(1)}, f32[4,256,128]{2,1,0:T(8,128)S(1)}) custom-call(f32[4,256,128]{2,1,0:T(8,128)S(1)} %get-tuple-element.75.refs_0_, f32[4,256,128]{2,1,0:T(8,128)S(1)} %get-tuple-element.77.refs_1_, f32[4,256,128]{2,1,0:T(8,128)S(1)} %get-tuple-element.78.refs_2_, ...), custom_call_target="tpu_custom_call" | custom-call | bytes 18350080 | tf_op jit(solution)/shard_map/pallas_call | solution.py:223
  91.9 0.0 collective-permute-done.7.halo_ref
  91.9 1.0 shard_map.80.r0_ref
  92.9 4.1 %collective-permute-done.6.halo_ref = f32[4,256,128]{2,1,0:T(8,128)S(1)} collective-permute-done((f32[4,256,128]{2,1,0:T(8,128)S(1)}, f32[4,256,128]{2,1,0:T(8,128)S(1)}, u32[]{:S(2)}, u32[]{:S(2)}) %collective-permute-start.6) | collective-permute-done | bytes 524320 | tf_op jit(solution)/shard_map/ppermute | solution.py:323
  97.0 1.3 shard_map.81
  98.3 36.0 %all_to_all.10.in_ref = f32[16,2,2,4,16,128]{5,4,3,2,1,0:T(8,128)S(1)} all-to-all(f32[16,2,2,4,16,128]{5,4,3,2,1,0:T(8,128)S(1)} %shard_map.81), channel_id=1, replica_groups=mesh['space'=8,'mode'=16] {'mode'}, dimensions={0} | all-to-all | bytes 4194304 | tf_op jit(solution)/shard_map/all_to_all | solution.py:359
  134.3 1.5 %shard_map.82 = (f32[2,4,128,256]{3,2,1,0:T(8,128)}, f32[2,4,128,256]{3,2,1,0:T(8,128)}) custom-call(f32[16,2,2,4,16,128]{5,4,3,2,1,0:T(8,128)S(1)} %all_to_all.10.in_ref), custom_call_target="tpu_custom_call" | custom-call | bytes 4194304 | tf_op jit(solution)/shard_map/pallas_call | solution.py:223
  (2 shorter events, 0.1 us)
Async XLA Ops:
  3.2 27.8 %all-to-all-start = ((f32[16,2,4,16,128]{4,3,2,1,0:T(8,128)}), f32[16,2,4,16,128]{4,3,2,1,0:T(8,128)S(1)}, u32[]{:S(2)}, u32[]{:S(2)}) async-start(f32[16,2,4,16,128]{4,3,2,1,0:T(8,128)} %shard_map.68), calls=%async_computation | async-start | bytes 2097152 | tf_op jit(solution)/shard_map/all_to_all | solution.py:308
  31.0 6.0 %copy-start.5 = (bf16[2,5,4,128,128]{4,3,2,1,0:T(8,128)(2,1)S(1)}, bf16[2,5,4,128,128]{4,3,2,1,0:T(8,128)(2,1)}, u32[]{:S(2)}) copy-start(bf16[2,5,4,128,128]{4,3,2,1,0:T(8,128)(2,1)} %get-tuple-element.53.refs_6_.refs_8_) | copy-start | bytes 3932164
  31.0 6.0 %copy-start.6 = (bf16[2,5,4,128,128]{4,3,2,1,0:T(8,128)(2,1)S(1)}, bf16[2,5,4,128,128]{4,3,2,1,0:T(8,128)(2,1)}, u32[]{:S(2)}) copy-start(bf16[2,5,4,128,128]{4,3,2,1,0:T(8,128)(2,1)} %get-tuple-element.54.refs_7_.refs_9_) | copy-start | bytes 3932164
  31.2 16.7 %collective-permute-start.1 = (f32[4,256,128]{2,1,0:T(8,128)S(1)}, f32[4,256,128]{2,1,0:T(8,128)S(1)}, u32[]{:S(2)}, u32[]{:S(2)}) collective-permute-start(f32[4,256,128]{2,1,0:T(8,128)S(1)} %bitcast.10), channel_id=1, source_target_pairs={{0,16},{1,17},{2,18},{3,19},{4,20},{5,21},{6,22},{7,23},{8,24},{9,... | collective-permute-start | bytes 1572872 | tf_op jit(solution)/shard_map/ppermute | solution.py:323
  31.7 16.2 %copy-start = (bf16[2,5,4,128,128]{4,3,2,1,0:T(8,128)(2,1)S(1)}, bf16[2,5,4,128,128]{4,3,2,1,0:T(8,128)(2,1)}, u32[]{:S(2)}) copy-start(bf16[2,5,4,128,128]{4,3,2,1,0:T(8,128)(2,1)} %get-tuple-element.57.hh_ref) | copy-start | bytes 3932164
  31.7 16.2 %copy-start.1 = (bf16[2,5,4,128,128]{4,3,2,1,0:T(8,128)(2,1)S(1)}, bf16[2,5,4,128,128]{4,3,2,1,0:T(8,128)(2,1)}, u32[]{:S(2)}) copy-start(bf16[2,5,4,128,128]{4,3,2,1,0:T(8,128)(2,1)} %get-tuple-element.58.hl_ref) | copy-start | bytes 3932164
  31.7 17.3 %collective-permute-start = (f32[4,256,128]{2,1,0:T(8,128)S(1)}, f32[4,256,128]{2,1,0:T(8,128)S(1)}, u32[]{:S(2)}, u32[]{:S(2)}) collective-permute-start(f32[4,256,128]{2,1,0:T(8,128)S(1)} %bitcast.15), channel_id=1, source_target_pairs={{0,120},{1,121},{2,122},{3,123},{4,124},{5,125},{6,126},{7,127},{8... | collective-permute-start | bytes 1572872 | tf_op jit(solution)/shard_map/ppermute | solution.py:323
  37.0 2.5 %copy-start.2 = (bf16[2,5,512,512]{3,2,1,0:T(8,128)(2,1)S(1)}, bf16[2,5,512,512]{3,2,1,0:T(8,128)(2,1)}, u32[]{:S(2)}) copy-start(bf16[2,5,512,512]{3,2,1,0:T(8,128)(2,1)} %get-tuple-element.51.refs_4_.refs_6_) | copy-start | bytes 15728644
  39.5 2.5 %copy-start.4 = (bf16[2,5,512,512]{3,2,1,0:T(8,128)(2,1)S(1)}, bf16[2,5,512,512]{3,2,1,0:T(8,128)(2,1)}, u32[]{:S(2)}) copy-start(bf16[2,5,512,512]{3,2,1,0:T(8,128)(2,1)} %get-tuple-element.52.refs_5_.refs_7_) | copy-start | bytes 15728644
  47.9 6.5 %copy-start.3 = (bf16[2,5,512,512]{3,2,1,0:T(8,128)(2,1)S(1)}, bf16[2,5,512,512]{3,2,1,0:T(8,128)(2,1)}, u32[]{:S(2)}) copy-start(bf16[2,5,512,512]{3,2,1,0:T(8,128)(2,1)} %get-tuple-element.51.refs_4_.refs_6_) | copy-start | bytes 15728644
  48.9 12.6 %collective-permute-start.3 = (f32[4,256,128]{2,1,0:T(8,128)S(1)}, f32[4,256,128]{2,1,0:T(8,128)S(1)}, u32[]{:S(2)}, u32[]{:S(2)}) collective-permute-start(f32[4,256,128]{2,1,0:T(8,128)S(1)} %get-tuple-element.59.refs_0_.rest_0_), channel_id=1, source_target_pairs={{0,16},{1,17},{2,18},{3,19},{4,20},{5,21},{6,22},{7,23},{8,24},{9,... | collective-permute-start | bytes 1572872 | tf_op jit(solution)/shard_map/ppermute | solution.py:323
  49.9 16.1 %collective-permute-start.2 = (f32[4,256,128]{2,1,0:T(8,128)S(1)}, f32[4,256,128]{2,1,0:T(8,128)S(1)}, u32[]{:S(2)}, u32[]{:S(2)}) collective-permute-start(f32[4,256,128]{2,1,0:T(8,128)S(1)} %get-tuple-element.61.refs_1_.rest_0_), channel_id=1, source_target_pairs={{0,120},{1,121},{2,122},{3,123},{4,124},{5,125},{6,126},{7,127},{8... | collective-permute-start | bytes 1572872 | tf_op jit(solution)/shard_map/ppermute | solution.py:323
  62.4 14.1 %collective-permute-start.5 = (f32[4,256,128]{2,1,0:T(8,128)S(1)}, f32[4,256,128]{2,1,0:T(8,128)S(1)}, u32[]{:S(2)}, u32[]{:S(2)}) collective-permute-start(f32[4,256,128]{2,1,0:T(8,128)S(1)} %get-tuple-element.66.refs_0_.rest_0_), channel_id=1, source_target_pairs={{0,16},{1,17},{2,18},{3,19},{4,20},{5,21},{6,22},{7,23},{8,24},{9,... | collective-permute-start | bytes 1572872 | tf_op jit(solution)/shard_map/ppermute | solution.py:323
  67.0 15.0 %collective-permute-start.4 = (f32[4,256,128]{2,1,0:T(8,128)S(1)}, f32[4,256,128]{2,1,0:T(8,128)S(1)}, u32[]{:S(2)}, u32[]{:S(2)}) collective-permute-start(f32[4,256,128]{2,1,0:T(8,128)S(1)} %get-tuple-element.68.refs_1_.rest_0_), channel_id=1, source_target_pairs={{0,120},{1,121},{2,122},{3,123},{4,124},{5,125},{6,126},{7,127},{8... | collective-permute-start | bytes 1572872 | tf_op jit(solution)/shard_map/ppermute | solution.py:323
  77.6 14.4 %collective-permute-start.7 = (f32[4,256,128]{2,1,0:T(8,128)S(1)}, f32[4,256,128]{2,1,0:T(8,128)S(1)}, u32[]{:S(2)}, u32[]{:S(2)}) collective-permute-start(f32[4,256,128]{2,1,0:T(8,128)S(1)} %get-tuple-element.75.refs_0_), channel_id=1, source_target_pairs={{0,16},{1,17},{2,18},{3,19},{4,20},{5,21},{6,22},{7,23},{8,24},{9,... | collective-permute-start | bytes 1572872 | tf_op jit(solution)/shard_map/ppermute | solution.py:323
  83.0 14.1 %collective-permute-start.6 = (f32[4,256,128]{2,1,0:T(8,128)S(1)}, f32[4,256,128]{2,1,0:T(8,128)S(1)}, u32[]{:S(2)}, u32[]{:S(2)}) collective-permute-start(f32[4,256,128]{2,1,0:T(8,128)S(1)} %get-tuple-element.77.refs_1_), channel_id=1, source_target_pairs={{0,120},{1,121},{2,122},{3,123},{4,124},{5,125},{6,126},{7,127},{8... | collective-permute-start | bytes 1572872 | tf_op jit(solution)/shard_map/ppermute | solution.py:323

commit v6 on v4

--- a/solution.py
+++ b/solution.py
@@ -40,7 +40,7 @@
 
 def place():
     slab = lax.axis_index("space").astype(jnp.int32)
-    return lax.shift_right_logical(slab, 1) & 1, 1 - (slab & 1)
+    return lax.shift_right_logical(slab + 1, 1) & 1, 1 - (slab & 1)
 
 
 def split_kernel(field_ref, out_ref, arrived, laid, in_sems, out_sems):
@@ -277,7 +277,7 @@
     pairs = []
     for s in range(count):
         t = (s + 1 if (s % 2 == 0) == inner else s - 1) % count
-        turn = half if (s // 2 - t // 2) % 2 else 0
+        turn = half if ((s + 1) // 2 - (t + 1) // 2) % 2 else 0
         pairs += [(s * modes + m, t * modes + (m ^ turn)) for m in range(modes)]
     return pairs
 

time: 136 us -> 133 us (0.978)
  starting transfers between devices: 27.2 us -> 23.5 us
  blocking collectives: 36 us -> 37.7 us
    ppermute x8, starting transfers between devices: 17.9 us -> 14.2 us  [per_device(): halo = [lax.ppermute(d[l], AXES, links[l]) for l in range(layers)]]
    all_to_all x1, blocking collectives: 36 us -> 37.7 us  [per_device(): back = lax.all_to_all(send, 'mode', 0, 0, tiled=True)]
  transfers between devices with their start and end apart: 9 -> 9, of which waited for: 4 -> 6; matrix products, arithmetic and copies ran while one was open for 0% -> 0% of each run, Pallas kernels for 36% -> 37%
where the time goes in v6:
time: 133 us
  Pallas kernels  54.2 us (41%)
  blocking collectives  37.7 us (28%)
  starting transfers between devices  23.5 us (18%)
  waiting for transfers between devices  11.2 us (8%)
  local copies, waits for them, and re-layouts  5.15 us (4%)
    all_to_all x1, blocking collectives, per_device(): back = lax.all_to_all(send, 'mode', 0, 0, tiled=True)  37.7 us
    pallas_call x14, Pallas kernels, call(): pl.pallas_call(body, out_shape=outs, in_specs=[pl.BlockSpec(memory_space=...  35.7 us
    pallas_call x1, Pallas kernels, prepare(): pl.pallas_call(prepare_kernel, grid_spec=grid_spec, out_shape=[dense] * 2...  18.5 us
    ppermute x8, starting transfers between devices, per_device(): halo = [lax.ppermute(d[l], AXES, links[l]) for l in range(layers)]  14.2 us
    ppermute x8, waiting for transfers between devices, per_device(): halo = [lax.ppermute(d[l], AXES, links[l]) for l in range(layers)]  11.2 us
    all_to_all x1, starting transfers between devices, per_device(): got = lax.all_to_all(sent, 'mode', 0, 0, tiled=True)  9.3 us
    unnamed x14, local copies, waits for them, and re-layouts  4.99 us
  transfers between devices with their start and end apart: 9, of which 6 were waited for; matrix products, arithmetic and copies ran while one was open for 0% of the time, Pallas kernels for 37%

profile of v6, /device:TPU:1, one launch (start us, length us, event | category | flops | bytes accessed | tf_op | source)
XLA Modules:
  0.0 132.7 jit_solution(11366115796675499288)
XLA Ops:
  0.6 2.6 %shard_map.68 = f32[16,2,4,16,128]{4,3,2,1,0:T(8,128)} custom-call(f32[2,4,128,256]{3,2,1,0:T(8,128)} %field_ref.2), custom_call_target="tpu_custom_call" | custom-call | bytes 2097152 | tf_op jit(solution)/shard_map/pallas_call | solution.py:223
  3.2 9.3 %all-to-all-start = ((f32[16,2,4,16,128]{4,3,2,1,0:T(8,128)}), f32[16,2,4,16,128]{4,3,2,1,0:T(8,128)S(1)}, u32[]{:S(2)}, u32[]{:S(2)}) async-start(f32[16,2,4,16,128]{4,3,2,1,0:T(8,128)} %shard_map.68), calls=%async_computation | async-start | bytes 2097152 | tf_op jit(solution)/shard_map/all_to_all | solution.py:308
  12.5 18.5 %shard_map.69 = (bf16[2,5,512,512]{3,2,1,0:T(8,128)(2,1)}, bf16[2,5,512,512]{3,2,1,0:T(8,128)(2,1)}, bf16[2,5,4,128,128]{4,3,2,1,0:T(8,128)(2,1)}, bf16[2,5,4,12...) custom-call(s32[4]{0:T(128)} %masks_ref.1, ...), custom_call_target="tpu_custom_call" | custom-call | flops 100000000 | bytes 37748736 | tf_op jit(solution)/shard_map/pallas_call | solution.py:266
  31.0 0.0 all-to-all-done
  31.0 0.0 copy-start.5
  31.1 0.0 copy-start.6
  31.1 0.1 slice_bitcast_fusion
  31.2 2.7 %collective-permute-start.1 = (f32[4,256,128]{2,1,0:T(8,128)S(1)}, f32[4,256,128]{2,1,0:T(8,128)S(1)}, u32[]{:S(2)}, u32[]{:S(2)}) collective-permute-start(f32[4,256,128]{2,1,0:T(8,128)S(1)} %bitcast.10), channel_id=1, source_target_pairs={{0,24},{1,25},{2,26},{3,27},{4,28},{5,29},{6,30},{7,31},{8,16},{9,... | collective-permute-start | bytes 1572872 | tf_op jit(solution)/shard_map/ppermute | solution.py:323
  34.0 0.0 copy-start
  34.0 0.0 copy-start.1
  34.0 2.5 %collective-permute-start = (f32[4,256,128]{2,1,0:T(8,128)S(1)}, f32[4,256,128]{2,1,0:T(8,128)S(1)}, u32[]{:S(2)}, u32[]{:S(2)}) collective-permute-start(f32[4,256,128]{2,1,0:T(8,128)S(1)} %bitcast.15), channel_id=1, source_target_pairs={{0,112},{1,113},{2,114},{3,115},{4,116},{5,117},{6,118},{7,119},{8... | collective-permute-start | bytes 1572872 | tf_op jit(solution)/shard_map/ppermute | solution.py:323
  36.4 0.0 copy-done.5
  36.4 0.0 copy-done.6
  36.4 0.0 copy-start.2
  36.4 2.5 %copy-done.2 = bf16[2,5,512,512]{3,2,1,0:T(8,128)(2,1)S(1)} copy-done((bf16[2,5,512,512]{3,2,1,0:T(8,128)(2,1)S(1)}, bf16[2,5,512,512]{3,2,1,0:T(8,128)(2,1)}, u32[]{:S(2)}) %copy-start.2) | copy-done | bytes 5242904
  38.9 0.0 copy-start.4
  38.9 2.5 %copy-done.4 = bf16[2,5,512,512]{3,2,1,0:T(8,128)(2,1)S(1)} copy-done((bf16[2,5,512,512]{3,2,1,0:T(8,128)(2,1)S(1)}, bf16[2,5,512,512]{3,2,1,0:T(8,128)(2,1)}, u32[]{:S(2)}) %copy-start.4) | copy-done | bytes 5242904
  41.4 5.8 %shard_map.70 = (f32[4,256,128]{2,1,0:T(8,128)S(1)}, f32[4,256,128]{2,1,0:T(8,128)S(1)}) custom-call(f32[4,256,128]{2,1,0:T(8,128)S(1)} %bitcast.11, f32[4,256,128]{2,1,0:T(8,128)S(1)} %bitcast.16, f32[4,256,128]{2,1,0:T(8,128)S(1)} %bitcast.12, f32[4,256,128]{2,1,0:T(8,128)S(1)} %bitcast.17, bf16[2,5,512,512]{3,2,1,0:T(8,128)(2,1)S(1)} %copy-done.2, ...), custom_call_target="tpu_custom_call" | custom-call | bytes 16252928 | tf_op jit(solution)/shard_map/pallas_call | solution.py:223
  47.3 0.0 collective-permute-done.1.halo_ref
  47.3 0.0 copy-done
  47.3 0.0 copy-done.1
  47.3 0.0 copy-start.3
  47.3 1.0 shard_map.71
  48.3 1.1 collective-permute-start.3
  49.3 0.0 collective-permute-done.halo_ref
  49.3 1.0 shard_map.72
  50.3 2.3 %collective-permute-start.2 = (f32[4,256,128]{2,1,0:T(8,128)S(1)}, f32[4,256,128]{2,1,0:T(8,128)S(1)}, u32[]{:S(2)}, u32[]{:S(2)}) collective-permute-start(f32[4,256,128]{2,1,0:T(8,128)S(1)} %get-tuple-element.61.refs_1_.rest_0_), channel_id=1, source_target_pairs={{0,112},{1,113},{2,114},{3,115},{4,116},{5,117},{6,118},{7,119},{8... | collective-permute-start | bytes 1572872 | tf_op jit(solution)/shard_map/ppermute | solution.py:323
  52.6 0.0 copy-done.3
  52.6 5.8 %shard_map.73 = (f32[4,256,128]{2,1,0:T(8,128)S(1)}, f32[4,256,128]{2,1,0:T(8,128)S(1)}, f32[4,256,128]{2,1,0:T(8,128)S(1)}, f32[4,256,128]{2,1,0:T(8,128)S(1)}) custom-call(f32[4,256,128]{2,1,0:T(8,128)S(1)} %get-tuple-element.59.refs_0_.rest_0_, f32[4,256,128]{2,1,0:T(8,128)S(1)} %get-tuple-element.61.refs_1_.rest_0_, ...), custom_call_target="tpu_custom_call" | custom-call | bytes 18350080 | tf_op jit(solution)/shard_map/pallas_call | solution.py:223
  58.5 3.6 %collective-permute-done.3.halo_ref = f32[4,256,128]{2,1,0:T(8,128)S(1)} collective-permute-done((f32[4,256,128]{2,1,0:T(8,128)S(1)}, f32[4,256,128]{2,1,0:T(8,128)S(1)}, u32[]{:S(2)}, u32[]{:S(2)}) %collective-permute-start.3) | collective-permute-done | bytes 524320 | tf_op jit(solution)/shard_map/ppermute | solution.py:323
  62.1 1.0 shard_map.74
  63.1 0.8 collective-permute-start.5
  63.8 0.8 collective-permute-done.2.halo_ref
  64.6 1.0 shard_map.75
  65.6 2.1 %collective-permute-start.4 = (f32[4,256,128]{2,1,0:T(8,128)S(1)}, f32[4,256,128]{2,1,0:T(8,128)S(1)}, u32[]{:S(2)}, u32[]{:S(2)}) collective-permute-start(f32[4,256,128]{2,1,0:T(8,128)S(1)} %get-tuple-element.68.refs_1_.rest_0_), channel_id=1, source_target_pairs={{0,112},{1,113},{2,114},{3,115},{4,116},{5,117},{6,118},{7,119},{8... | collective-permute-start | bytes 1572872 | tf_op jit(solution)/shard_map/ppermute | solution.py:323
  67.7 5.8 %shard_map.76 = (f32[4,256,128]{2,1,0:T(8,128)S(1)}, f32[4,256,128]{2,1,0:T(8,128)S(1)}, f32[4,256,128]{2,1,0:T(8,128)S(1)}, f32[4,256,128]{2,1,0:T(8,128)S(1)}) custom-call(f32[4,256,128]{2,1,0:T(8,128)S(1)} %get-tuple-element.66.refs_0_.rest_0_, f32[4,256,128]{2,1,0:T(8,128)S(1)} %get-tuple-element.68.refs_1_.rest_0_, ...), custom_call_target="tpu_custom_call" | custom-call | bytes 18350080 | tf_op jit(solution)/shard_map/pallas_call | solution.py:223
  73.6 2.4 %collective-permute-done.5.halo_ref = f32[4,256,128]{2,1,0:T(8,128)S(1)} collective-permute-done((f32[4,256,128]{2,1,0:T(8,128)S(1)}, f32[4,256,128]{2,1,0:T(8,128)S(1)}, u32[]{:S(2)}, u32[]{:S(2)}) %collective-permute-start.5) | collective-permute-done | bytes 524320 | tf_op jit(solution)/shard_map/ppermute | solution.py:323
  76.0 1.0 shard_map.77
  76.9 0.7 collective-permute-start.7
  77.6 1.2 collective-permute-done.4.halo_ref
  78.8 1.0 shard_map.78
  79.8 2.1 %collective-permute-start.6 = (f32[4,256,128]{2,1,0:T(8,128)S(1)}, f32[4,256,128]{2,1,0:T(8,128)S(1)}, u32[]{:S(2)}, u32[]{:S(2)}) collective-permute-start(f32[4,256,128]{2,1,0:T(8,128)S(1)} %get-tuple-element.77.refs_1_), channel_id=1, source_target_pairs={{0,112},{1,113},{2,114},{3,115},{4,116},{5,117},{6,118},{7,119},{8... | collective-permute-start | bytes 1572872 | tf_op jit(solution)/shard_map/ppermute | solution.py:323
  81.9 5.8 %shard_map.79 = (f32[4,256,128]{2,1,0:T(8,128)S(1)}, f32[4,256,128]{2,1,0:T(8,128)S(1)}, f32[4,256,128]{2,1,0:T(8,128)S(1)}, f32[4,256,128]{2,1,0:T(8,128)S(1)}) custom-call(f32[4,256,128]{2,1,0:T(8,128)S(1)} %get-tuple-element.75.refs_0_, f32[4,256,128]{2,1,0:T(8,128)S(1)} %get-tuple-element.77.refs_1_, f32[4,256,128]{2,1,0:T(8,128)S(1)} %get-tuple-element.78.refs_2_, ...), custom_call_target="tpu_custom_call" | custom-call | bytes 18350080 | tf_op jit(solution)/shard_map/pallas_call | solution.py:223
  87.7 1.4 %collective-permute-done.7.halo_ref = f32[4,256,128]{2,1,0:T(8,128)S(1)} collective-permute-done((f32[4,256,128]{2,1,0:T(8,128)S(1)}, f32[4,256,128]{2,1,0:T(8,128)S(1)}, u32[]{:S(2)}, u32[]{:S(2)}) %collective-permute-start.7) | collective-permute-done | bytes 524320 | tf_op jit(solution)/shard_map/ppermute | solution.py:323
  89.1 1.0 shard_map.80.r0_ref
  90.1 1.9 %collective-permute-done.6.halo_ref = f32[4,256,128]{2,1,0:T(8,128)S(1)} collective-permute-done((f32[4,256,128]{2,1,0:T(8,128)S(1)}, f32[4,256,128]{2,1,0:T(8,128)S(1)}, u32[]{:S(2)}, u32[]{:S(2)}) %collective-permute-start.6) | collective-permute-done | bytes 524320 | tf_op jit(solution)/shard_map/ppermute | solution.py:323
  92.0 1.3 shard_map.81
  93.3 37.7 %all_to_all.10.in_ref = f32[16,2,2,4,16,128]{5,4,3,2,1,0:T(8,128)S(1)} all-to-all(f32[16,2,2,4,16,128]{5,4,3,2,1,0:T(8,128)S(1)} %shard_map.81), channel_id=1, replica_groups=mesh['space'=8,'mode'=16] {'mode'}, dimensions={0} | all-to-all | bytes 4194304 | tf_op jit(solution)/shard_map/all_to_all | solution.py:359
  131.0 1.5 %shard_map.82 = (f32[2,4,128,256]{3,2,1,0:T(8,128)}, f32[2,4,128,256]{3,2,1,0:T(8,128)}) custom-call(f32[16,2,2,4,16,128]{5,4,3,2,1,0:T(8,128)S(1)} %all_to_all.10.in_ref), custom_call_target="tpu_custom_call" | custom-call | bytes 4194304 | tf_op jit(solution)/shard_map/pallas_call | solution.py:223
  (2 shorter events, 0.1 us)
Async XLA Ops:
  3.2 27.8 %all-to-all-start = ((f32[16,2,4,16,128]{4,3,2,1,0:T(8,128)}), f32[16,2,4,16,128]{4,3,2,1,0:T(8,128)S(1)}, u32[]{:S(2)}, u32[]{:S(2)}) async-start(f32[16,2,4,16,128]{4,3,2,1,0:T(8,128)} %shard_map.68), calls=%async_computation | async-start | bytes 2097152 | tf_op jit(solution)/shard_map/all_to_all | solution.py:308
  31.0 5.4 %copy-start.5 = (bf16[2,5,4,128,128]{4,3,2,1,0:T(8,128)(2,1)S(1)}, bf16[2,5,4,128,128]{4,3,2,1,0:T(8,128)(2,1)}, u32[]{:S(2)}) copy-start(bf16[2,5,4,128,128]{4,3,2,1,0:T(8,128)(2,1)} %get-tuple-element.53.refs_6_.refs_8_) | copy-start | bytes 3932164
  31.1 5.4 %copy-start.6 = (bf16[2,5,4,128,128]{4,3,2,1,0:T(8,128)(2,1)S(1)}, bf16[2,5,4,128,128]{4,3,2,1,0:T(8,128)(2,1)}, u32[]{:S(2)}) copy-start(bf16[2,5,4,128,128]{4,3,2,1,0:T(8,128)(2,1)} %get-tuple-element.54.refs_7_.refs_9_) | copy-start | bytes 3932164
  31.2 16.1 %collective-permute-start.1 = (f32[4,256,128]{2,1,0:T(8,128)S(1)}, f32[4,256,128]{2,1,0:T(8,128)S(1)}, u32[]{:S(2)}, u32[]{:S(2)}) collective-permute-start(f32[4,256,128]{2,1,0:T(8,128)S(1)} %bitcast.10), channel_id=1, source_target_pairs={{0,24},{1,25},{2,26},{3,27},{4,28},{5,29},{6,30},{7,31},{8,16},{9,... | collective-permute-start | bytes 1572872 | tf_op jit(solution)/shard_map/ppermute | solution.py:323
  34.0 13.3 %copy-start = (bf16[2,5,4,128,128]{4,3,2,1,0:T(8,128)(2,1)S(1)}, bf16[2,5,4,128,128]{4,3,2,1,0:T(8,128)(2,1)}, u32[]{:S(2)}) copy-start(bf16[2,5,4,128,128]{4,3,2,1,0:T(8,128)(2,1)} %get-tuple-element.57.hh_ref) | copy-start | bytes 3932164
  34.0 13.3 %copy-start.1 = (bf16[2,5,4,128,128]{4,3,2,1,0:T(8,128)(2,1)S(1)}, bf16[2,5,4,128,128]{4,3,2,1,0:T(8,128)(2,1)}, u32[]{:S(2)}) copy-start(bf16[2,5,4,128,128]{4,3,2,1,0:T(8,128)(2,1)} %get-tuple-element.58.hl_ref) | copy-start | bytes 3932164
  34.0 15.4 %collective-permute-start = (f32[4,256,128]{2,1,0:T(8,128)S(1)}, f32[4,256,128]{2,1,0:T(8,128)S(1)}, u32[]{:S(2)}, u32[]{:S(2)}) collective-permute-start(f32[4,256,128]{2,1,0:T(8,128)S(1)} %bitcast.15), channel_id=1, source_target_pairs={{0,112},{1,113},{2,114},{3,115},{4,116},{5,117},{6,118},{7,119},{8... | collective-permute-start | bytes 1572872 | tf_op jit(solution)/shard_map/ppermute | solution.py:323
  36.4 2.5 %copy-start.2 = (bf16[2,5,512,512]{3,2,1,0:T(8,128)(2,1)S(1)}, bf16[2,5,512,512]{3,2,1,0:T(8,128)(2,1)}, u32[]{:S(2)}) copy-start(bf16[2,5,512,512]{3,2,1,0:T(8,128)(2,1)} %get-tuple-element.51.refs_4_.refs_6_) | copy-start | bytes 15728644
  38.9 2.5 %copy-start.4 = (bf16[2,5,512,512]{3,2,1,0:T(8,128)(2,1)S(1)}, bf16[2,5,512,512]{3,2,1,0:T(8,128)(2,1)}, u32[]{:S(2)}) copy-start(bf16[2,5,512,512]{3,2,1,0:T(8,128)(2,1)} %get-tuple-element.52.refs_5_.refs_7_) | copy-start | bytes 15728644
  47.3 5.4 %copy-start.3 = (bf16[2,5,512,512]{3,2,1,0:T(8,128)(2,1)S(1)}, bf16[2,5,512,512]{3,2,1,0:T(8,128)(2,1)}, u32[]{:S(2)}) copy-start(bf16[2,5,512,512]{3,2,1,0:T(8,128)(2,1)} %get-tuple-element.51.refs_4_.refs_6_) | copy-start | bytes 15728644
  48.3 13.8 %collective-permute-start.3 = (f32[4,256,128]{2,1,0:T(8,128)S(1)}, f32[4,256,128]{2,1,0:T(8,128)S(1)}, u32[]{:S(2)}, u32[]{:S(2)}) collective-permute-start(f32[4,256,128]{2,1,0:T(8,128)S(1)} %get-tuple-element.59.refs_0_.rest_0_), channel_id=1, source_target_pairs={{0,24},{1,25},{2,26},{3,27},{4,28},{5,29},{6,30},{7,31},{8,16},{9,... | collective-permute-start | bytes 1572872 | tf_op jit(solution)/shard_map/ppermute | solution.py:323
  50.3 14.3 %collective-permute-start.2 = (f32[4,256,128]{2,1,0:T(8,128)S(1)}, f32[4,256,128]{2,1,0:T(8,128)S(1)}, u32[]{:S(2)}, u32[]{:S(2)}) collective-permute-start(f32[4,256,128]{2,1,0:T(8,128)S(1)} %get-tuple-element.61.refs_1_.rest_0_), channel_id=1, source_target_pairs={{0,112},{1,113},{2,114},{3,115},{4,116},{5,117},{6,118},{7,119},{8... | collective-permute-start | bytes 1572872 | tf_op jit(solution)/shard_map/ppermute | solution.py:323
  63.1 12.9 %collective-permute-start.5 = (f32[4,256,128]{2,1,0:T(8,128)S(1)}, f32[4,256,128]{2,1,0:T(8,128)S(1)}, u32[]{:S(2)}, u32[]{:S(2)}) collective-permute-start(f32[4,256,128]{2,1,0:T(8,128)S(1)} %get-tuple-element.66.refs_0_.rest_0_), channel_id=1, source_target_pairs={{0,24},{1,25},{2,26},{3,27},{4,28},{5,29},{6,30},{7,31},{8,16},{9,... | collective-permute-start | bytes 1572872 | tf_op jit(solution)/shard_map/ppermute | solution.py:323
  65.6 13.2 %collective-permute-start.4 = (f32[4,256,128]{2,1,0:T(8,128)S(1)}, f32[4,256,128]{2,1,0:T(8,128)S(1)}, u32[]{:S(2)}, u32[]{:S(2)}) collective-permute-start(f32[4,256,128]{2,1,0:T(8,128)S(1)} %get-tuple-element.68.refs_1_.rest_0_), channel_id=1, source_target_pairs={{0,112},{1,113},{2,114},{3,115},{4,116},{5,117},{6,118},{7,119},{8... | collective-permute-start | bytes 1572872 | tf_op jit(solution)/shard_map/ppermute | solution.py:323
  76.9 12.2 %collective-permute-start.7 = (f32[4,256,128]{2,1,0:T(8,128)S(1)}, f32[4,256,128]{2,1,0:T(8,128)S(1)}, u32[]{:S(2)}, u32[]{:S(2)}) collective-permute-start(f32[4,256,128]{2,1,0:T(8,128)S(1)} %get-tuple-element.75.refs_0_), channel_id=1, source_target_pairs={{0,24},{1,25},{2,26},{3,27},{4,28},{5,29},{6,30},{7,31},{8,16},{9,... | collective-permute-start | bytes 1572872 | tf_op jit(solution)/shard_map/ppermute | solution.py:323
  79.8 12.3 %collective-permute-start.6 = (f32[4,256,128]{2,1,0:T(8,128)S(1)}, f32[4,256,128]{2,1,0:T(8,128)S(1)}, u32[]{:S(2)}, u32[]{:S(2)}) collective-permute-start(f32[4,256,128]{2,1,0:T(8,128)S(1)} %get-tuple-element.77.refs_1_), channel_id=1, source_target_pairs={{0,112},{1,113},{2,114},{3,115},{4,116},{5,117},{6,118},{7,119},{8... | collective-permute-start | bytes 1572872 | tf_op jit(solution)/shard_map/ppermute | solution.py:323

commit v7 on v6

--- a/solution.py
+++ b/solution.py
@@ -333,7 +333,7 @@
         rho = rho_new
         if not last:
             fresh = []
-            for l in range(layers):
+            for l in reversed(range(layers)):
                 if fresh:
                     pre[l], _ = lax.optimization_barrier((pre[l], fresh[0][1]))
                 fresh.append(
@@ -343,6 +343,7 @@
                         [halo[l], pre[l], hh, hl, d[l]],
                     )
                 )
+            fresh = fresh[::-1]
             r, d = zip(*fresh)
     (r_end,) = call(
         functools.partial(finish_kernel, group, None, 0), [layer], [halo[0], pre[0], hh, hl]

time: 133 us -> 135 us (1.015)
  waiting for transfers between devices: 11.2 us -> 15.9 us
  starting transfers between devices: 23.5 us -> 21.3 us
    ppermute x8, waiting for transfers between devices: 11.2 us -> 15.9 us  [per_device(): halo = [lax.ppermute(d[l], AXES, links[l]) for l in range(layers)]]
    ppermute x8, starting transfers between devices: 14.2 us -> 12 us  [per_device(): halo = [lax.ppermute(d[l], AXES, links[l]) for l in range(layers)]]
  transfers between devices with their start and end apart: 9 -> 9, of which waited for: 6 -> 6; matrix products, arithmetic and copies ran while one was open for 0% -> 0% of each run, Pallas kernels for 37% -> 36%
where the time goes in v7:
time: 135 us; the launch traced here: 134 us
  Pallas kernels  54.2 us (40%)
  blocking collectives  37 us (27%)
  starting transfers between devices  21.3 us (16%)
  waiting for transfers between devices  15.9 us (12%)
  local copies, waits for them, and re-layouts  5.15 us (4%)
    all_to_all x1, blocking collectives, per_device(): back = lax.all_to_all(send, 'mode', 0, 0, tiled=True)  37 us
    pallas_call x14, Pallas kernels, call(): pl.pallas_call(body, out_shape=outs, in_specs=[pl.BlockSpec(memory_space=...  35.7 us
    pallas_call x1, Pallas kernels, prepare(): pl.pallas_call(prepare_kernel, grid_spec=grid_spec, out_shape=[dense] * 2...  18.5 us
    ppermute x8, waiting for transfers between devices, per_device(): halo = [lax.ppermute(d[l], AXES, links[l]) for l in range(layers)]  15.9 us
    ppermute x8, starting transfers between devices, per_device(): halo = [lax.ppermute(d[l], AXES, links[l]) for l in range(layers)]  12 us
    all_to_all x1, starting transfers between devices, per_device(): got = lax.all_to_all(sent, 'mode', 0, 0, tiled=True)  9.3 us
    unnamed x14, local copies, waits for them, and re-layouts  4.99 us
  transfers between devices with their start and end apart: 9, of which 6 were waited for; matrix products, arithmetic and copies ran while one was open for 0% of the time, Pallas kernels for 36%

profile of v7, /device:TPU:1, one launch (start us, length us, event | category | flops | bytes accessed | tf_op | source)
XLA Modules:
  0.0 134.4 jit_solution(4440872413633283738)
XLA Ops:
  0.6 2.6 %shard_map.68 = f32[16,2,4,16,128]{4,3,2,1,0:T(8,128)} custom-call(f32[2,4,128,256]{3,2,1,0:T(8,128)} %field_ref.2), custom_call_target="tpu_custom_call" | custom-call | bytes 2097152 | tf_op jit(solution)/shard_map/pallas_call | solution.py:223
  3.2 9.3 %all-to-all-start = ((f32[16,2,4,16,128]{4,3,2,1,0:T(8,128)}), f32[16,2,4,16,128]{4,3,2,1,0:T(8,128)S(1)}, u32[]{:S(2)}, u32[]{:S(2)}) async-start(f32[16,2,4,16,128]{4,3,2,1,0:T(8,128)} %shard_map.68), calls=%async_computation | async-start | bytes 2097152 | tf_op jit(solution)/shard_map/all_to_all | solution.py:308
  12.5 18.5 %shard_map.69 = (bf16[2,5,512,512]{3,2,1,0:T(8,128)(2,1)}, bf16[2,5,512,512]{3,2,1,0:T(8,128)(2,1)}, bf16[2,5,4,128,128]{4,3,2,1,0:T(8,128)(2,1)}, bf16[2,5,4,12...) custom-call(s32[4]{0:T(128)} %masks_ref.1, ...), custom_call_target="tpu_custom_call" | custom-call | flops 100000000 | bytes 37748736 | tf_op jit(solution)/shard_map/pallas_call | solution.py:266
  31.0 0.0 all-to-all-done
  31.0 0.0 copy-start.5
  31.0 0.0 copy-start.6
  31.0 0.1 slice_bitcast_fusion
  31.2 2.9 %collective-permute-start = (f32[4,256,128]{2,1,0:T(8,128)S(1)}, f32[4,256,128]{2,1,0:T(8,128)S(1)}, u32[]{:S(2)}, u32[]{:S(2)}) collective-permute-start(f32[4,256,128]{2,1,0:T(8,128)S(1)} %bitcast.10), channel_id=1, source_target_pairs={{0,112},{1,113},{2,114},{3,115},{4,116},{5,117},{6,118},{7,119},{8... | collective-permute-start | bytes 1572872 | tf_op jit(solution)/shard_map/ppermute | solution.py:323
  34.1 0.0 copy-start
  34.1 0.0 copy-start.1
  34.1 1.5 %collective-permute-start.2 = (f32[4,256,128]{2,1,0:T(8,128)S(1)}, f32[4,256,128]{2,1,0:T(8,128)S(1)}, u32[]{:S(2)}, u32[]{:S(2)}) collective-permute-start(f32[4,256,128]{2,1,0:T(8,128)S(1)} %bitcast.15), channel_id=1, source_target_pairs={{0,24},{1,25},{2,26},{3,27},{4,28},{5,29},{6,30},{7,31},{8,16},{9,... | collective-permute-start | bytes 1572872 | tf_op jit(solution)/shard_map/ppermute | solution.py:323
  35.6 0.0 copy-done.5
  35.6 0.0 copy-done.6
  35.6 0.0 copy-start.2
  35.6 2.5 %copy-done.2 = bf16[2,5,512,512]{3,2,1,0:T(8,128)(2,1)S(1)} copy-done((bf16[2,5,512,512]{3,2,1,0:T(8,128)(2,1)S(1)}, bf16[2,5,512,512]{3,2,1,0:T(8,128)(2,1)}, u32[]{:S(2)}) %copy-start.2) | copy-done | bytes 5242904
  38.1 0.0 copy-start.4
  38.1 2.5 %copy-done.4 = bf16[2,5,512,512]{3,2,1,0:T(8,128)(2,1)S(1)} copy-done((bf16[2,5,512,512]{3,2,1,0:T(8,128)(2,1)S(1)}, bf16[2,5,512,512]{3,2,1,0:T(8,128)(2,1)}, u32[]{:S(2)}) %copy-start.4) | copy-done | bytes 5242904
  40.6 5.8 %shard_map.70 = (f32[4,256,128]{2,1,0:T(8,128)S(1)}, f32[4,256,128]{2,1,0:T(8,128)S(1)}) custom-call(f32[4,256,128]{2,1,0:T(8,128)S(1)} %bitcast.16, f32[4,256,128]{2,1,0:T(8,128)S(1)} %bitcast.11, f32[4,256,128]{2,1,0:T(8,128)S(1)} %bitcast.17, f32[4,256,128]{2,1,0:T(8,128)S(1)} %bitcast.12, bf16[2,5,512,512]{3,2,1,0:T(8,128)(2,1)S(1)} %copy-done.2, ...), custom_call_target="tpu_custom_call" | custom-call | bytes 16252928 | tf_op jit(solution)/shard_map/pallas_call | solution.py:223
  46.4 0.5 collective-permute-done.halo_ref
  46.9 0.0 copy-done
  46.9 0.0 copy-done.1
  46.9 0.0 copy-start.3
  46.9 1.0 shard_map.71
  47.8 2.9 %collective-permute-start.1 = (f32[4,256,128]{2,1,0:T(8,128)S(1)}, f32[4,256,128]{2,1,0:T(8,128)S(1)}, u32[]{:S(2)}, u32[]{:S(2)}) collective-permute-start(f32[4,256,128]{2,1,0:T(8,128)S(1)} %get-tuple-element.58.refs_1_.rest_0_), channel_id=1, source_target_pairs={{0,112},{1,113},{2,114},{3,115},{4,116},{5,117},{6,118},{7,119},{8... | collective-permute-start | bytes 1572872 | tf_op jit(solution)/shard_map/ppermute | solution.py:323
  50.7 0.0 collective-permute-done.2.halo_ref
  50.7 1.0 shard_map.72
  51.7 0.3 collective-permute-start.4
  52.0 0.0 copy-done.3
  52.0 5.8 %shard_map.73 = (f32[4,256,128]{2,1,0:T(8,128)S(1)}, f32[4,256,128]{2,1,0:T(8,128)S(1)}, f32[4,256,128]{2,1,0:T(8,128)S(1)}, f32[4,256,128]{2,1,0:T(8,128)S(1)}) custom-call(f32[4,256,128]{2,1,0:T(8,128)S(1)} %get-tuple-element.61.refs_0_.rest_0_, f32[4,256,128]{2,1,0:T(8,128)S(1)} %get-tuple-element.58.refs_1_.rest_0_, ...), custom_call_target="tpu_custom_call" | custom-call | bytes 18350080 | tf_op jit(solution)/shard_map/pallas_call | solution.py:223
  57.8 4.8 %collective-permute-done.1.halo_ref = f32[4,256,128]{2,1,0:T(8,128)S(1)} collective-permute-done((f32[4,256,128]{2,1,0:T(8,128)S(1)}, f32[4,256,128]{2,1,0:T(8,128)S(1)}, u32[]{:S(2)}, u32[]{:S(2)}) %collective-permute-start.1) | collective-permute-done | bytes 524320 | tf_op jit(solution)/shard_map/ppermute | solution.py:323
  62.6 1.0 shard_map.74
  63.6 2.9 %collective-permute-start.3 = (f32[4,256,128]{2,1,0:T(8,128)S(1)}, f32[4,256,128]{2,1,0:T(8,128)S(1)}, u32[]{:S(2)}, u32[]{:S(2)}) collective-permute-start(f32[4,256,128]{2,1,0:T(8,128)S(1)} %get-tuple-element.65.refs_1_.rest_0_), channel_id=1, source_target_pairs={{0,112},{1,113},{2,114},{3,115},{4,116},{5,117},{6,118},{7,119},{8... | collective-permute-start | bytes 1572872 | tf_op jit(solution)/shard_map/ppermute | solution.py:323
  66.5 0.0 collective-permute-done.4.halo_ref
  66.5 1.0 shard_map.75
  67.5 0.3 collective-permute-start.6
  67.8 5.8 %shard_map.76 = (f32[4,256,128]{2,1,0:T(8,128)S(1)}, f32[4,256,128]{2,1,0:T(8,128)S(1)}, f32[4,256,128]{2,1,0:T(8,128)S(1)}, f32[4,256,128]{2,1,0:T(8,128)S(1)}) custom-call(f32[4,256,128]{2,1,0:T(8,128)S(1)} %get-tuple-element.68.refs_0_.rest_0_, f32[4,256,128]{2,1,0:T(8,128)S(1)} %get-tuple-element.65.refs_1_.rest_0_, ...), custom_call_target="tpu_custom_call" | custom-call | bytes 18350080 | tf_op jit(solution)/shard_map/pallas_call | solution.py:223
  73.6 3.8 %collective-permute-done.3.halo_ref = f32[4,256,128]{2,1,0:T(8,128)S(1)} collective-permute-done((f32[4,256,128]{2,1,0:T(8,128)S(1)}, f32[4,256,128]{2,1,0:T(8,128)S(1)}, u32[]{:S(2)}, u32[]{:S(2)}) %collective-permute-start.3) | collective-permute-done | bytes 524320 | tf_op jit(solution)/shard_map/ppermute | solution.py:323
  77.4 1.0 shard_map.77
  78.4 2.0 %collective-permute-done.6.halo_ref = f32[4,256,128]{2,1,0:T(8,128)S(1)} collective-permute-done((f32[4,256,128]{2,1,0:T(8,128)S(1)}, f32[4,256,128]{2,1,0:T(8,128)S(1)}, u32[]{:S(2)}, u32[]{:S(2)}) %collective-permute-start.6) | collective-permute-done | bytes 524320 | tf_op jit(solution)/shard_map/ppermute | solution.py:323
  80.4 1.0 shard_map.78
  81.4 0.4 collective-permute-start.7
  81.7 1.0 collective-permute-start.5
  82.7 5.8 %shard_map.79 = (f32[4,256,128]{2,1,0:T(8,128)S(1)}, f32[4,256,128]{2,1,0:T(8,128)S(1)}, f32[4,256,128]{2,1,0:T(8,128)S(1)}, f32[4,256,128]{2,1,0:T(8,128)S(1)}) custom-call(f32[4,256,128]{2,1,0:T(8,128)S(1)} %get-tuple-element.77.refs_0_, f32[4,256,128]{2,1,0:T(8,128)S(1)} %get-tuple-element.74.refs_1_, f32[4,256,128]{2,1,0:T(8,128)S(1)} %get-tuple-element.78.refs_2_, ...), custom_call_target="tpu_custom_call" | custom-call | bytes 18350080 | tf_op jit(solution)/shard_map/pallas_call | solution.py:223
  88.5 4.6 %collective-permute-done.7.halo_ref = f32[4,256,128]{2,1,0:T(8,128)S(1)} collective-permute-done((f32[4,256,128]{2,1,0:T(8,128)S(1)}, f32[4,256,128]{2,1,0:T(8,128)S(1)}, u32[]{:S(2)}, u32[]{:S(2)}) %collective-permute-start.7) | collective-permute-done | bytes 524320 | tf_op jit(solution)/shard_map/ppermute | solution.py:323
  93.1 1.0 shard_map.80.r0_ref
  94.1 0.3 collective-permute-done.5.halo_ref
  94.4 1.3 shard_map.81
  95.7 37.0 %all_to_all.10.in_ref = f32[16,2,2,4,16,128]{5,4,3,2,1,0:T(8,128)S(1)} all-to-all(f32[16,2,2,4,16,128]{5,4,3,2,1,0:T(8,128)S(1)} %shard_map.81), channel_id=1, replica_groups=mesh['space'=8,'mode'=16] {'mode'}, dimensions={0} | all-to-all | bytes 4194304 | tf_op jit(solution)/shard_map/all_to_all | solution.py:360
  132.7 1.5 %shard_map.82 = (f32[2,4,128,256]{3,2,1,0:T(8,128)}, f32[2,4,128,256]{3,2,1,0:T(8,128)}) custom-call(f32[16,2,2,4,16,128]{5,4,3,2,1,0:T(8,128)S(1)} %all_to_all.10.in_ref), custom_call_target="tpu_custom_call" | custom-call | bytes 4194304 | tf_op jit(solution)/shard_map/pallas_call | solution.py:223
  (2 shorter events, 0.1 us)
Async XLA Ops:
  3.2 27.8 %all-to-all-start = ((f32[16,2,4,16,128]{4,3,2,1,0:T(8,128)}), f32[16,2,4,16,128]{4,3,2,1,0:T(8,128)S(1)}, u32[]{:S(2)}, u32[]{:S(2)}) async-start(f32[16,2,4,16,128]{4,3,2,1,0:T(8,128)} %shard_map.68), calls=%async_computation | async-start | bytes 2097152 | tf_op jit(solution)/shard_map/all_to_all | solution.py:308
  31.0 4.6 %copy-start.5 = (bf16[2,5,4,128,128]{4,3,2,1,0:T(8,128)(2,1)S(1)}, bf16[2,5,4,128,128]{4,3,2,1,0:T(8,128)(2,1)}, u32[]{:S(2)}) copy-start(bf16[2,5,4,128,128]{4,3,2,1,0:T(8,128)(2,1)} %get-tuple-element.53.refs_6_.refs_8_) | copy-start | bytes 3932164
  31.0 4.6 %copy-start.6 = (bf16[2,5,4,128,128]{4,3,2,1,0:T(8,128)(2,1)S(1)}, bf16[2,5,4,128,128]{4,3,2,1,0:T(8,128)(2,1)}, u32[]{:S(2)}) copy-start(bf16[2,5,4,128,128]{4,3,2,1,0:T(8,128)(2,1)} %get-tuple-element.54.refs_7_.refs_9_) | copy-start | bytes 3932164
  31.2 15.7 %collective-permute-start = (f32[4,256,128]{2,1,0:T(8,128)S(1)}, f32[4,256,128]{2,1,0:T(8,128)S(1)}, u32[]{:S(2)}, u32[]{:S(2)}) collective-permute-start(f32[4,256,128]{2,1,0:T(8,128)S(1)} %bitcast.10), channel_id=1, source_target_pairs={{0,112},{1,113},{2,114},{3,115},{4,116},{5,117},{6,118},{7,119},{8... | collective-permute-start | bytes 1572872 | tf_op jit(solution)/shard_map/ppermute | solution.py:323
  34.1 12.8 %copy-start = (bf16[2,5,4,128,128]{4,3,2,1,0:T(8,128)(2,1)S(1)}, bf16[2,5,4,128,128]{4,3,2,1,0:T(8,128)(2,1)}, u32[]{:S(2)}) copy-start(bf16[2,5,4,128,128]{4,3,2,1,0:T(8,128)(2,1)} %get-tuple-element.56.hh_ref) | copy-start | bytes 3932164
  34.1 12.8 %copy-start.1 = (bf16[2,5,4,128,128]{4,3,2,1,0:T(8,128)(2,1)S(1)}, bf16[2,5,4,128,128]{4,3,2,1,0:T(8,128)(2,1)}, u32[]{:S(2)}) copy-start(bf16[2,5,4,128,128]{4,3,2,1,0:T(8,128)(2,1)} %get-tuple-element.57.hl_ref) | copy-start | bytes 3932164
  34.1 16.6 %collective-permute-start.2 = (f32[4,256,128]{2,1,0:T(8,128)S(1)}, f32[4,256,128]{2,1,0:T(8,128)S(1)}, u32[]{:S(2)}, u32[]{:S(2)}) collective-permute-start(f32[4,256,128]{2,1,0:T(8,128)S(1)} %bitcast.15), channel_id=1, source_target_pairs={{0,24},{1,25},{2,26},{3,27},{4,28},{5,29},{6,30},{7,31},{8,16},{9,... | collective-permute-start | bytes 1572872 | tf_op jit(solution)/shard_map/ppermute | solution.py:323
  35.6 2.5 %copy-start.2 = (bf16[2,5,512,512]{3,2,1,0:T(8,128)(2,1)S(1)}, bf16[2,5,512,512]{3,2,1,0:T(8,128)(2,1)}, u32[]{:S(2)}) copy-start(bf16[2,5,512,512]{3,2,1,0:T(8,128)(2,1)} %get-tuple-element.51.refs_4_.refs_6_) | copy-start | bytes 15728644
  38.1 2.5 %copy-start.4 = (bf16[2,5,512,512]{3,2,1,0:T(8,128)(2,1)S(1)}, bf16[2,5,512,512]{3,2,1,0:T(8,128)(2,1)}, u32[]{:S(2)}) copy-start(bf16[2,5,512,512]{3,2,1,0:T(8,128)(2,1)} %get-tuple-element.52.refs_5_.refs_7_) | copy-start | bytes 15728644
  46.9 5.1 %copy-start.3 = (bf16[2,5,512,512]{3,2,1,0:T(8,128)(2,1)S(1)}, bf16[2,5,512,512]{3,2,1,0:T(8,128)(2,1)}, u32[]{:S(2)}) copy-start(bf16[2,5,512,512]{3,2,1,0:T(8,128)(2,1)} %get-tuple-element.51.refs_4_.refs_6_) | copy-start | bytes 15728644
  47.8 14.7 %collective-permute-start.1 = (f32[4,256,128]{2,1,0:T(8,128)S(1)}, f32[4,256,128]{2,1,0:T(8,128)S(1)}, u32[]{:S(2)}, u32[]{:S(2)}) collective-permute-start(f32[4,256,128]{2,1,0:T(8,128)S(1)} %get-tuple-element.58.refs_1_.rest_0_), channel_id=1, source_target_pairs={{0,112},{1,113},{2,114},{3,115},{4,116},{5,117},{6,118},{7,119},{8... | collective-permute-start | bytes 1572872 | tf_op jit(solution)/shard_map/ppermute | solution.py:323
  51.7 14.8 %collective-permute-start.4 = (f32[4,256,128]{2,1,0:T(8,128)S(1)}, f32[4,256,128]{2,1,0:T(8,128)S(1)}, u32[]{:S(2)}, u32[]{:S(2)}) collective-permute-start(f32[4,256,128]{2,1,0:T(8,128)S(1)} %get-tuple-element.61.refs_0_.rest_0_), channel_id=1, source_target_pairs={{0,24},{1,25},{2,26},{3,27},{4,28},{5,29},{6,30},{7,31},{8,16},{9,... | collective-permute-start | bytes 1572872 | tf_op jit(solution)/shard_map/ppermute | solution.py:323
  63.6 13.8 %collective-permute-start.3 = (f32[4,256,128]{2,1,0:T(8,128)S(1)}, f32[4,256,128]{2,1,0:T(8,128)S(1)}, u32[]{:S(2)}, u32[]{:S(2)}) collective-permute-start(f32[4,256,128]{2,1,0:T(8,128)S(1)} %get-tuple-element.65.refs_1_.rest_0_), channel_id=1, source_target_pairs={{0,112},{1,113},{2,114},{3,115},{4,116},{5,117},{6,118},{7,119},{8... | collective-permute-start | bytes 1572872 | tf_op jit(solution)/shard_map/ppermute | solution.py:323
  67.5 12.9 %collective-permute-start.6 = (f32[4,256,128]{2,1,0:T(8,128)S(1)}, f32[4,256,128]{2,1,0:T(8,128)S(1)}, u32[]{:S(2)}, u32[]{:S(2)}) collective-permute-start(f32[4,256,128]{2,1,0:T(8,128)S(1)} %get-tuple-element.68.refs_0_.rest_0_), channel_id=1, source_target_pairs={{0,24},{1,25},{2,26},{3,27},{4,28},{5,29},{6,30},{7,31},{8,16},{9,... | collective-permute-start | bytes 1572872 | tf_op jit(solution)/shard_map/ppermute | solution.py:323
  81.4 11.8 %collective-permute-start.7 = (f32[4,256,128]{2,1,0:T(8,128)S(1)}, f32[4,256,128]{2,1,0:T(8,128)S(1)}, u32[]{:S(2)}, u32[]{:S(2)}) collective-permute-start(f32[4,256,128]{2,1,0:T(8,128)S(1)} %get-tuple-element.77.refs_0_), channel_id=1, source_target_pairs={{0,24},{1,25},{2,26},{3,27},{4,28},{5,29},{6,30},{7,31},{8,16},{9,... | collective-permute-start | bytes 1572872 | tf_op jit(solution)/shard_map/ppermute | solution.py:323
  81.7 12.7 %collective-permute-start.5 = (f32[4,256,128]{2,1,0:T(8,128)S(1)}, f32[4,256,128]{2,1,0:T(8,128)S(1)}, u32[]{:S(2)}, u32[]{:S(2)}) collective-permute-start(f32[4,256,128]{2,1,0:T(8,128)S(1)} %get-tuple-element.74.refs_1_), channel_id=1, source_target_pairs={{0,112},{1,113},{2,114},{3,115},{4,116},{5,117},{6,118},{7,119},{8... | collective-permute-start | bytes 1572872 | tf_op jit(solution)/shard_map/ppermute | solution.py:323
